TPU v7x, 32 devices: a whole 2x2x4 slice. The times are simulated.
32 devices in a mesh: frame: 16 (over z, x, core), coil: 2 (over y).
Axes of the slice: x: 2, y: 2, z: 4, core: 2. Of those that a mesh axis runs over, the one named last changes fastest.
Arguments:
- kspace: bfloat16 [16, 64, 256, 512], P('frame', 'coil'), may hold values from -6 to 6
- sens: bfloat16 [64, 256, 512], P('coil'), may hold values from -0.5 to 0.5
- mask: int32 [16, 64, 256], P('frame', 'coil'), may hold values 0 or 1
- image: float32 [16, 256, 512], P('frame', 'coil'), may hold values from -6 to 6
- w_first: bfloat16 [3, 3, 3, 64, 2], replicated, may hold values from -0.875 to 0.875
- b_first: float32 [64], replicated, may hold values from -3 to 3
- w_mid: bfloat16 [3, 3, 3, 64, 64], replicated, may hold values from -0.15625 to 0.15625
- b_mid: float32 [64], replicated, may hold values from -3 to 3
- w_last: bfloat16 [3, 3, 3, 2, 64], replicated, may hold values from -0.15625 to 0.15625
Outputs:
- recon: float32 [16, 256, 512], P('frame', 'coil')
Inputs may be any that keep to these rules, and one draw needn't show every extreme that they name: mask is 1 on the acquired phase-encoding lines of a frame and coil and 0 on the others.
All inputs are finite; a program needn't handle non-finite values. No bound on the sum of `mask` on one device may be relied on, other than what follows from the above.
Results may differ from a plain program's by a relative error of at most 0.006.
Values may be sent and summed in bfloat16 or wider, within the bound.
No kernel may reach another device: no remote copies, remote signals or barrier semaphores. Data moves between devices by JAX's collectives and lax.ppermute only.
A program may use at most 192 MiB of HBM per device.

v0:
```python
import math

import jax
import jax.numpy as jnp
from jax import lax
from jax.sharding import PartitionSpec as P

step_size = 1.0


def with_halo(shard, sides, width):
    for axis, dim in sides:
        devices, length = (lax.axis_size(axis), shard.shape[dim])
        up = [(i, (i + 1) % devices) for i in range(devices - 1)]
        down = [(j, i) for i, j in up]
        last = lax.slice_in_dim(shard, length - width, length, axis=dim)
        leading = lax.slice_in_dim(shard, 0, width, axis=dim)
        before = lax.ppermute(last, axis, up)
        after = lax.ppermute(leading, axis, down)
        shard = jnp.concatenate([before, shard, after], axis=dim)
    return shard


def dft_parts(order):
    indices = jnp.arange(order, dtype=jnp.int32)
    phases = indices[:, None] * indices[None, :] % order
    angles = phases.astype(jnp.float32) * (2.0 * math.pi / order)
    factor = 1.0 / math.sqrt(order)
    return (
        (jnp.cos(angles) * factor).astype(jnp.bfloat16),
        (-jnp.sin(angles) * factor).astype(jnp.bfloat16),
    )


def column_tables(real_part, imag_part):
    ahead = jnp.concatenate(
        [jnp.concatenate([real_part, imag_part], 1), jnp.concatenate([-imag_part, real_part], 1)], 0
    )
    behind = jnp.concatenate(
        [jnp.concatenate([real_part, -imag_part], 1), jnp.concatenate([imag_part, real_part], 1)], 0
    )
    return (ahead, behind)


def swapped(values):
    half_width = values.shape[-1] // 2
    return jnp.concatenate([-values[..., half_width:], values[..., :half_width]], -1)


def complex_mul(first, second):
    half_width = first.shape[-1] // 2
    first_re, first_im = (first[..., :half_width], first[..., half_width:])
    second_re, second_im = (second[..., :half_width], second[..., half_width:])
    return jnp.concatenate(
        [first_re * second_re - first_im * second_im, first_re * second_im + first_im * second_re],
        -1,
    )


def conj_mul(first, second):
    half_width = first.shape[-1] // 2
    first_re, first_im = (first[..., :half_width], first[..., half_width:])
    second_re, second_im = (second[..., :half_width], second[..., half_width:])
    return jnp.concatenate(
        [first_re * second_re + first_im * second_im, first_re * second_im - first_im * second_re],
        -1,
    )


def data_step(image_now, kspace, sens, mask, row_real, row_imag, ahead, behind):
    f32 = jnp.float32
    sens_rows = sens.astype(f32)
    coil_image = complex_mul(
        sens_rows[None],
        lax.all_gather(image_now.astype(jnp.bfloat16), "coil", axis=1, tiled=True).astype(f32)[
            :, None
        ],
    ).astype(jnp.bfloat16)
    cols_spectrum = jnp.einsum(
        "fcrm,mn->fcrn", coil_image, ahead, preferred_element_type=f32
    ).astype(jnp.bfloat16)
    stacked = jnp.concatenate([cols_spectrum, swapped(cols_spectrum)], 2)
    row_ahead = jnp.concatenate([row_real, row_imag], 1)
    estimate = jnp.einsum("kr,fcrn->fckn", row_ahead, stacked, preferred_element_type=f32)
    misfit = (mask.astype(f32)[..., None] * (estimate - kspace.astype(f32))).astype(jnp.bfloat16)
    back_cols = jnp.einsum("fckm,mn->fckn", misfit, behind, preferred_element_type=f32).astype(
        jnp.bfloat16
    )
    stacked_back = jnp.concatenate([back_cols, swapped(back_cols)], 2)
    lower = -row_imag
    row_behind = jnp.concatenate([row_real, lower], 1)
    back_image = jnp.einsum("rk,fckn->fcrn", row_behind, stacked_back, preferred_element_type=f32)
    sens_rows = sens.astype(f32)
    term = jnp.sum(conj_mul(sens_rows[None], back_image), 1)
    summed = lax.psum_scatter(jnp.moveaxis(term, 1, 0), "coil", scatter_dimension=0, tiled=True)
    return image_now - step_size * jnp.moveaxis(summed, 0, 1)


def with_rims(hidden):
    wider = with_halo(hidden, (("frame", 0),), 1)
    return with_halo(wider, (("coil", 1),), 1)


def conv_layer(padded, weight):
    frames = padded.shape[0] - 2
    rows = padded.shape[1] - 2
    out_chan = weight.shape[3]
    in_chan = weight.shape[4]
    window = jnp.concatenate(
        [
            padded[tap_frame : tap_frame + frames, tap_row : tap_row + rows]
            for tap_frame in range(3)
            for tap_row in range(3)
        ],
        2,
    )
    matrix = jnp.transpose(weight, (2, 3, 0, 1, 4)).reshape(3 * out_chan, 9 * in_chan)
    taps_out = jnp.einsum("km,frmn->frkn", matrix, window, preferred_element_type=jnp.float32)
    left_taps = taps_out[:, :, :out_chan]
    centre = taps_out[:, :, out_chan : 2 * out_chan]
    right_taps = taps_out[:, :, 2 * out_chan :]
    zeros_col = jnp.zeros_like(left_taps[..., :1])
    return (
        centre
        + jnp.concatenate([zeros_col, left_taps[..., :-1]], -1)
        + jnp.concatenate([right_taps[..., 1:], zeros_col], -1)
    )


def denoise(image_now, w_first, b_first, w_mid, b_mid, w_last):
    frames, rows, double = image_now.shape
    hidden = image_now.reshape(frames, rows, 2, double // 2).astype(jnp.bfloat16)
    first = jax.nn.relu(
        conv_layer(with_rims(hidden), w_first) + b_first[None, None, :, None]
    ).astype(jnp.bfloat16)
    second = jax.nn.relu(conv_layer(with_rims(first), w_mid) + b_mid[None, None, :, None]).astype(
        jnp.bfloat16
    )
    update = conv_layer(with_rims(second), w_last)
    return image_now + update.reshape(frames, rows, double)


def shards(kspace, sens, mask, image, w_first, b_first, w_mid, b_mid, w_last):
    row_real, row_imag = dft_parts(sens.shape[1])
    col_real, col_imag = dft_parts(sens.shape[2] // 2)
    ahead, behind = column_tables(col_real, col_imag)
    image_now = image
    image_now = data_step(image_now, kspace, sens, mask, row_real, row_imag, ahead, behind)
    image_now = denoise(image_now, w_first, b_first, w_mid, b_mid, w_last)
    return image_now


def solution(mesh):
    in_specs = (
        P("frame", "coil", None, None),
        P("coil", None, None),
        P("frame", "coil", None),
        P("frame", "coil", None),
        P(),
        P(),
        P(),
        P(),
        P(),
    )
    out_specs = P("frame", "coil", None)
    return jax.shard_map(shards, mesh=mesh, in_specs=in_specs, out_specs=out_specs, check_vma=False)
```

profile of v0, /device:TPU:6, one launch (start us, length us, event | category | flops | bytes accessed | tf_op | source)
XLA Modules:
  0.0 511.7 jit_solution(16779190972869144724)
XLA Ops:
  6.5 1.1 multiply_convert_fusion
  8.7 11.5 %bitcast_convert_fusion = f32[1,32,256,512]{3,2,1,0:T(8,128)} fusion(bf16[32,256,512]{2,1,0:T(8,128)(2,1)} %param.10), kind=kLoop, calls=%fused_computation.39 | loop fusion | flops 4194304 | bytes 25165824 | tf_op jit(solution)/shard_map/broadcast_in_dim | solution.py:94
  20.2 6.4 %all_gather.3 = bf16[1,256,512]{2,1,0:T(8,128)(2,1)S(1)} all-gather(bf16[1,128,512]{2,1,0:T(8,128)(2,1)S(1)} %convert_element_type.90), channel_id=1, replica_groups=mesh['frame'=16,'coil'=2] {'coil'}, dimensions={1}, use_global_device_ids=true | all-gather | bytes 393216 | tf_op jit(solution)/shard_map/all_gather | solution.py:75
  26.7 7.3 %fusion.39 = (bf16[32,256,256]{2,1,0:T(8,128)(2,1)S(1)}, bf16[32,256,256]{2,1,0:T(8,128)(2,1)S(1)}) fusion(f32[1,32,256,512]{3,2,1,0:T(8,128)} %bitcast_convert_fusion, f32[256,256]{1,0:T(8,128)S(1)} %get-tuple-element.24, f32[256,256]{1,0:T(8,128)S(1)} %get-tuple-element.23), kind=kLoop, calls=%fused_computation.47 | loop fusion | flops 16777216 | bytes 25690112 | tf_op jit(solution)/shard_map/concatenate | solution.py:54
  34.0 5.0 convert_bitcast_fusion.1
  39.0 3.2 copy-done.12
  42.3 3.6 slice_negate_fusion.1
  45.8 11.9 %copy.16 = bf16[1,32,256,512]{2,3,1,0:T(8,128)(2,1)} copy(bf16[1,32,256,512]{3,2,1,0:T(8,128)(2,1)} %param.9) | data formatting | bytes 16777216 | tf_op args[0]
  57.8 23.1 %convert_bitcast_fusion = bf16[1,32,256,512]{3,2,1,0:T(8,128)(2,1)} fusion(bf16[1,32,256,512]{2,3,1,0:T(8,128)(2,1)} %copy.16, bf16[1,32,256,256]{3,2,1,0:T(8,128)(2,1)} %get-tuple-element.20, bf16[1,32,256,256]{3,2,1,0:T(8,128)(2,1)} %get-tuple-element.19, bf16[1,32,256,512]{3,2,1,0:T(8,128)(2,1)} %copy-done.12, f32[32,256]{1,0:T(8,128)S(1)} %convert_bitcast_fusion.2, ...), kind=kOutput, calls=%fused_computation.42 | convolution fusion | flops 8663859200 | bytes 33980416 | tf_op jit(solution)/shard_map/fckm,mn->fckn/dot_general | solution.py:86
  80.8 5.8 %slice_negate_fusion = (bf16[1,32,256,256]{3,2,1,0:T(8,128)(2,1)}, bf16[1,32,256,256]{3,2,1,0:T(8,128)(2,1)}) fusion(bf16[1,32,256,512]{3,2,1,0:T(8,128)(2,1)} %convert_bitcast_fusion), kind=kLoop, calls=%fused_computation.73 | loop fusion | flops 2097152 | bytes 16777216 | tf_op jit(solution)/shard_map/neg | solution.py:47
  86.6 11.6 %fusion.16 = f32[1,32,256,512]{3,2,1,0:T(8,128)} fusion(bf16[1,32,256,256]{3,2,1,0:T(8,128)(2,1)} %get-tuple-element.18, bf16[1,32,256,256]{3,2,1,0:T(8,128)(2,1)} %get-tuple-element.17, bf16[1,32,256,512]{3,2,1,0:T(8,128)(2,1)} %convert_bitcast_fusion, bf16[256,256]{1,0:T(8,128)(2,1)S(1)} %get-tuple-element.37, bf16[256,256]{1,0:T(8,128)(2,1)S(1)} %fusion.76), kind=kOutput, calls=%fused_computation.20 | convolution fusion | flops 4345823232 | bytes 33816576 | tf_op jit(solution)/shard_map/rk,fckn->fcrn/dot_general | solution.py:92
  98.2 18.8 %multiply_add_fusion = (f32[1,32,256,256]{3,2,1,0:T(8,128)}, f32[1,32,256,256]{3,2,1,0:T(8,128)}) fusion(f32[1,32,256,512]{3,2,1,0:T(8,128)} %fusion.16, f32[1,32,256,512]{3,2,1,0:T(8,128)} %bitcast_convert_fusion), kind=kLoop, calls=%fused_computation.41 | loop fusion | flops 12582912 | bytes 50331648 | tf_op jit(solution)/shard_map/add | solution.py:65
  117.0 7.4 %maximum_reduce_fusion = f32[256,512]{1,0:T(8,128)} fusion(f32[1,32,256,256]{3,2,1,0:T(8,128)} %get-tuple-element.6, f32[1,32,256,256]{3,2,1,0:T(8,128)} %get-tuple-element.5), kind=kLoop, calls=%fused_computation.16 | loop fusion | flops 8257536 | bytes 17301504 | tf_op jit(solution)/shard_map/reduce_sum | solution.py:94
  124.4 15.1 %reduce-scatter.2.cloned.1.call-done = f32[128,1,512]{2,0,1:T(8,128)} async-done(((f32[256,1,512]{2,0,1:T(8,128)}), f32[128,1,512]{2,0,1:T(8,128)}) %reduce-scatter.2.cloned.1.call-update) | async-done | bytes 262160 | tf_op jit(solution)/shard_map/reduce_scatter | solution.py:95
  140.5 1.9 collective-permute-start
  142.4 3.6 collective-permute-start.1
  147.0 1.6 collective-permute-done.1
  148.7 1.3 collective-permute-start.2
  150.0 4.5 collective-permute-start.3
  154.7 1.2 collective-permute-done.3
  156.4 1.9 concatenate.132
  158.4 10.2 %convolution_bitcast_fusion = f32[1,128,192,256]{3,2,1,0:T(8,128)} fusion(bf16[192,18,1]{0,1,2:T(8,128)(2,1)S(1)} %reshape.98, bf16[1,128,18,256]{3,2,1,0:T(8,128)(2,1)S(1)} %concatenate.132), kind=kOutput, calls=%fused_computation.22 | convolution fusion | flops 226492416 | bytes 26352384 | tf_op jit(solution)/shard_map/km,frmn->frkn/dot_general | solution.py:118
  168.6 9.6 %fusion.82 = (f32[1,128,64,255]{3,2,1,0:T(8,128)S(1)}, f32[1,128,64,255]{3,2,1,0:T(8,128)}) fusion(f32[1,128,192,256]{3,2,1,0:T(8,128)} %convolution_bitcast_fusion), kind=kLoop, calls=%fused_computation.141 | loop fusion | bytes 33423360 | tf_op jit(solution)/shard_map/slice | solution.py:125
  178.2 7.6 %fusion.27 = bf16[1,128,64,256]{3,2,1,0:T(8,128)(2,1)S(1)} fusion(f32[1,128,192,256]{3,2,1,0:T(8,128)} %convolution_bitcast_fusion, f32[1,128,64,255]{3,2,1,0:T(8,128)} %get-tuple-element.10, f32[1,128,64,255]{3,2,1,0:T(8,128)S(1)} %get-tuple-element.9, f32[64]{0:T(128)S(1)} %copy-done.20), kind=kLoop, calls=%fused_computation.32 | loop fusion | flops 10485760 | bytes 29294848 | tf_op jit(solution)/shard_map/convert_element_type | solution.py:135
  185.8 3.5 collective-permute-start.4
  189.3 2.2 collective-permute-start.5
  191.5 89.2 %collective-permute-done.4 = bf16[1,128,64,256]{3,2,1,0:T(8,128)(2,1)S(1)} collective-permute-done((bf16[1,128,64,256]{3,2,1,0:T(8,128)(2,1)S(1)}, bf16[1,128,64,256]{3,2,1,0:T(8,128)(2,1)S(1)}, u32[]{:S(2)}, u32[]{:S(2)}) %collective-permute-start.4) | collective-permute-done | bytes 4194336 | tf_op jit(solution)/shard_map/ppermute | solution.py:18
  280.7 1.9 copy-done.4
  282.7 1.3 copy-done.8
  284.0 1.3 collective-permute-start.6
  286.1 4.8 collective-permute-start.7
  290.9 4.1 maximum_dynamic-update-slice_fusion.7
  295.1 2.4 constant_dynamic-update-slice_fusion.5
  297.5 1.2 copy-done.1
  298.8 1.3 copy-done.9
  300.0 2.3 maximum_dynamic-update-slice_fusion.6
  302.3 2.2 maximum_dynamic-update-slice_fusion.5
  304.6 2.3 constant_dynamic-update-slice_fusion.4
  306.8 2.2 maximum_dynamic-update-slice_fusion.4
  309.0 2.3 fusion.44
  311.3 2.4 constant_dynamic-update-slice_fusion.3
  313.7 2.3 fusion.43
  316.0 25.4 %fusion.17 = f32[1,128,192,256]{3,2,1,0:T(8,128)} fusion(bf16[192,576,1]{1,0,2:T(8,128)(2,1)S(1)} %reshape.99, bf16[1,128,576,256]{3,2,1,0:T(8,128)(2,1)} %fusion.43), kind=kOutput, calls=%fused_computation.21 | convolution fusion | flops 7247757312 | bytes 63135744 | tf_op jit(solution)/shard_map/km,frmn->frkn/dot_general | solution.py:118
  341.4 9.7 %fusion.81 = (f32[1,128,64,255]{3,2,1,0:T(8,128)S(1)}, f32[1,128,64,255]{3,2,1,0:T(8,128)}) fusion(f32[1,128,192,256]{3,2,1,0:T(8,128)} %fusion.17), kind=kLoop, calls=%fused_computation.140 | loop fusion | bytes 33423360 | tf_op jit(solution)/shard_map/slice | solution.py:125
  351.1 7.6 %fusion.23 = bf16[1,128,64,256]{3,2,1,0:T(8,128)(2,1)S(1)} fusion(f32[1,128,192,256]{3,2,1,0:T(8,128)} %fusion.17, f32[1,128,64,255]{3,2,1,0:T(8,128)} %get-tuple-element.8, f32[1,128,64,255]{3,2,1,0:T(8,128)S(1)} %get-tuple-element.7, f32[64]{0:T(128)S(1)} %copy-done.21), kind=kLoop, calls=%fused_computation.27 | loop fusion | flops 10485760 | bytes 29294848 | tf_op jit(solution)/shard_map/convert_element_type | solution.py:136
  358.7 2.1 collective-permute-start.8
  360.8 3.6 collective-permute-start.9
  364.4 89.2 %collective-permute-done.8 = bf16[1,128,64,256]{3,2,1,0:T(8,128)(2,1)S(1)} collective-permute-done((bf16[1,128,64,256]{3,2,1,0:T(8,128)(2,1)S(1)}, bf16[1,128,64,256]{3,2,1,0:T(8,128)(2,1)S(1)}, u32[]{:S(2)}, u32[]{:S(2)}) %collective-permute-start.8) | collective-permute-done | bytes 4194336 | tf_op jit(solution)/shard_map/ppermute | solution.py:18
  453.7 1.9 copy-done.6
  455.6 1.3 copy-done.10
  456.9 1.3 collective-permute-start.10
  458.3 4.8 collective-permute-start.11
  463.4 4.1 maximum_dynamic-update-slice_fusion.3
  467.6 2.4 constant_dynamic-update-slice_fusion.8
  470.0 1.2 copy-done.3
  471.3 1.3 copy-done.11
  472.5 2.3 maximum_dynamic-update-slice_fusion.2
  474.8 2.2 maximum_dynamic-update-slice_fusion.1
  477.1 2.3 constant_dynamic-update-slice_fusion.7
  479.3 2.2 maximum_dynamic-update-slice_fusion
  481.5 2.3 fusion.42
  483.8 2.4 constant_dynamic-update-slice_fusion.6
  486.2 2.3 fusion.41
  488.5 14.3 %fusion.46 = f32[1,128,6,256]{3,2,1,0:T(8,128)S(1)} fusion(bf16[6,576,1]{1,0,2:T(8,128)(2,1)S(1)} %reshape.100, bf16[1,128,576,256]{3,2,1,0:T(8,128)(2,1)} %fusion.41), kind=kOutput, calls=%fused_computation.76 | convolution fusion | flops 226492416 | bytes 38542080 | tf_op jit(solution)/shard_map/km,frmn->frkn/dot_general | solution.py:118
  (69 shorter events, 6.8 us)
Async XLA Ops:
  6.5 132.9 %reduce-scatter.2.cloned.1.call-start = ((), (), s32[]{:S(2)}) async-start(), calls=%async_computation.1 | async-start | bytes 786432 | tf_op jit(solution)/shard_map/reduce_scatter | solution.py:95
  8.6 11.5 %copy-start.13 = (f32[1,128,512]{2,1,0:T(8,128)S(1)}, f32[1,128,512]{2,1,0:T(8,128)}, u32[]{:S(2)}) copy-start(f32[1,128,512]{2,1,0:T(8,128)} %param.12) | copy-start | bytes 786436
  39.0 3.2 copy-start.12
  45.8 11.9 %copy-start.17 = (s32[1,32,256]{2,1,0:T(8,128)S(1)}, s32[1,32,256]{2,1,0:T(8,128)}, u32[]{:S(2)}) copy-start(s32[1,32,256]{2,1,0:T(8,128)} %param.11) | copy-start | bytes 98308
  117.0 37.5 %copy-start.18 = (bf16[3,3,3,64,2]{3,4,2,1,0:T(2,128)(2,1)S(1)}, bf16[3,3,3,64,2]{3,4,2,1,0:T(2,128)(2,1)}, u32[]{:S(2)}) copy-start(bf16[3,3,3,64,2]{3,4,2,1,0:T(2,128)(2,1)} %param.13) | copy-start | bytes 20740
  140.5 6.3 %collective-permute-start = (bf16[1,128,2,256]{3,2,1,0:T(2,128)(2,1)S(1)}, bf16[1,128,2,256]{3,2,1,0:T(2,128)(2,1)S(1)}, u32[]{:S(2)}, u32[]{:S(2)}) collective-permute-start(bf16[1,128,2,256]{3,2,1,0:T(2,128)(2,1)S(1)} %convert_element_type.101), channel_id=1, source_target_pairs={{0,2},{2,4},{4,6},{6,8},{8,10},{10,12},{12,14},{14,16},{16,18},{18... | collective-permute-start | bytes 393224 | tf_op jit(solution)/shard_map/ppermute | solution.py:18
  142.4 6.1 %collective-permute-start.1 = (bf16[1,128,2,256]{3,2,1,0:T(2,128)(2,1)S(1)}, bf16[1,128,2,256]{3,2,1,0:T(2,128)(2,1)S(1)}, u32[]{:S(2)}, u32[]{:S(2)}) collective-permute-start(bf16[1,128,2,256]{3,2,1,0:T(2,128)(2,1)S(1)} %convert_element_type.101), channel_id=1, source_target_pairs={{2,0},{4,2},{6,4},{8,6},{10,8},{12,10},{14,12},{16,14},{18,16},{20... | collective-permute-start | bytes 393224 | tf_op jit(solution)/shard_map/ppermute | solution.py:19
  148.7 6.0 %collective-permute-start.2 = (bf16[3,1,2,256]{3,2,1,0:T(2,128)(2,1)S(1)}, bf16[3,1,2,256]{3,2,1,0:T(2,128)(2,1)S(1)}, u32[]{:S(2)}, u32[]{:S(2)}) collective-permute-start(bf16[3,1,2,256]{3,2,1,0:T(2,128)(2,1)S(1)} %get-tuple-element.35), channel_id=1, source_target_pairs={{0,1},{2,3},{4,5},{6,7},{8,9},{10,11},{12,13},{14,15},{16,17},{18,... | collective-permute-start | bytes 9224 | tf_op jit(solution)/shard_map/ppermute | solution.py:18
  150.0 5.9 %collective-permute-start.3 = (bf16[3,1,2,256]{3,2,1,0:T(2,128)(2,1)S(1)}, bf16[3,1,2,256]{3,2,1,0:T(2,128)(2,1)S(1)}, u32[]{:S(2)}, u32[]{:S(2)}) collective-permute-start(bf16[3,1,2,256]{3,2,1,0:T(2,128)(2,1)S(1)} %get-tuple-element.34), channel_id=1, source_target_pairs={{1,0},{3,2},{5,4},{7,6},{9,8},{11,10},{13,12},{15,14},{17,16},{19,... | collective-permute-start | bytes 9224 | tf_op jit(solution)/shard_map/ppermute | solution.py:19
  168.6 9.6 %copy-start.20 = (f32[64]{0:T(128)S(1)}, f32[64]{0:T(128)}, u32[]{:S(2)}) copy-start(f32[64]{0:T(128)} %param.14) | copy-start | bytes 772
  185.8 94.9 %copy-start = (bf16[1,128,64,256]{3,2,1,0:T(8,128)(2,1)}, bf16[1,128,64,256]{3,2,1,0:T(8,128)(2,1)S(1)}, u32[]{:S(2)}) copy-start(bf16[1,128,64,256]{3,2,1,0:T(8,128)(2,1)S(1)} %fusion.27) | copy-start | bytes 12582916
  185.8 99.5 %copy-start.16 = (bf16[3,3,3,64,64]{4,3,2,1,0:T(8,128)(2,1)S(1)}, bf16[3,3,3,64,64]{4,3,2,1,0:T(8,128)(2,1)}, u32[]{:S(2)}) copy-start(bf16[3,3,3,64,64]{4,3,2,1,0:T(8,128)(2,1)} %param.15) | copy-start | bytes 663556
  185.8 94.9 %collective-permute-start.4 = (bf16[1,128,64,256]{3,2,1,0:T(8,128)(2,1)S(1)}, bf16[1,128,64,256]{3,2,1,0:T(8,128)(2,1)S(1)}, u32[]{:S(2)}, u32[]{:S(2)}) collective-permute-start(bf16[1,128,64,256]{3,2,1,0:T(8,128)(2,1)S(1)} %fusion.27), channel_id=1, source_target_pairs={{0,2},{2,4},{4,6},{6,8},{8,10},{10,12},{12,14},{14,16},{16,18},{18... | collective-permute-start | bytes 12582920 | tf_op jit(solution)/shard_map/ppermute | solution.py:18
  189.3 91.4 %collective-permute-start.5 = (bf16[1,128,64,256]{3,2,1,0:T(8,128)(2,1)S(1)}, bf16[1,128,64,256]{3,2,1,0:T(8,128)(2,1)S(1)}, u32[]{:S(2)}, u32[]{:S(2)}) collective-permute-start(bf16[1,128,64,256]{3,2,1,0:T(8,128)(2,1)S(1)} %fusion.27), channel_id=1, source_target_pairs={{2,0},{4,2},{6,4},{8,6},{10,8},{12,10},{14,12},{16,14},{18,16},{20... | collective-permute-start | bytes 12582920 | tf_op jit(solution)/shard_map/ppermute | solution.py:19
  280.7 2.0 copy-start.4
  280.7 3.3 copy-start.8
  284.0 6.9 %collective-permute-start.6 = (bf16[3,1,64,256]{3,2,1,0:T(8,128)(2,1)S(1)}, bf16[3,1,64,256]{3,2,1,0:T(8,128)(2,1)S(1)}, u32[]{:S(2)}, u32[]{:S(2)}) collective-permute-start(bf16[3,1,64,256]{3,2,1,0:T(8,128)(2,1)S(1)} %get-tuple-element.16), channel_id=1, source_target_pairs={{0,1},{2,3},{4,5},{6,7},{8,9},{10,11},{12,13},{14,15},{16,17},{18,... | collective-permute-start | bytes 294920 | tf_op jit(solution)/shard_map/ppermute | solution.py:18
  286.1 9.0 %copy-start.5 = (bf16[1,128,64,256]{3,2,1,0:T(8,128)(2,1)S(1)}, bf16[1,128,64,256]{3,2,1,0:T(8,128)(2,1)}, u32[]{:S(2)}) copy-start(bf16[1,128,64,256]{3,2,1,0:T(8,128)(2,1)} %copy-done.4) | copy-start | bytes 12582916
  286.1 11.4 %collective-permute-start.7 = (bf16[3,1,64,256]{3,2,1,0:T(8,128)(2,1)S(1)}, bf16[3,1,64,256]{3,2,1,0:T(8,128)(2,1)S(1)}, u32[]{:S(2)}, u32[]{:S(2)}) collective-permute-start(bf16[3,1,64,256]{3,2,1,0:T(8,128)(2,1)S(1)} %get-tuple-element.15), channel_id=1, source_target_pairs={{1,0},{3,2},{5,4},{7,6},{9,8},{11,10},{13,12},{15,14},{17,16},{19,... | collective-permute-start | bytes 294920 | tf_op jit(solution)/shard_map/ppermute | solution.py:19
  295.1 3.7 copy-start.1
  295.1 5.0 copy-start.9
  341.4 9.7 %copy-start.21 = (f32[64]{0:T(128)S(1)}, f32[64]{0:T(128)}, u32[]{:S(2)}) copy-start(f32[64]{0:T(128)} %param.16) | copy-start | bytes 772
  358.7 94.9 %copy-start.2 = (bf16[1,128,64,256]{3,2,1,0:T(8,128)(2,1)}, bf16[1,128,64,256]{3,2,1,0:T(8,128)(2,1)S(1)}, u32[]{:S(2)}) copy-start(bf16[1,128,64,256]{3,2,1,0:T(8,128)(2,1)S(1)} %fusion.23) | copy-start | bytes 12582916
  358.7 99.5 %copy-start.19 = (bf16[3,3,3,2,64]{4,3,2,1,0:T(2,128)(2,1)S(1)}, bf16[3,3,3,2,64]{4,3,2,1,0:T(2,128)(2,1)}, u32[]{:S(2)}) copy-start(bf16[3,3,3,2,64]{4,3,2,1,0:T(2,128)(2,1)} %param.17) | copy-start | bytes 20740
  358.7 94.9 %collective-permute-start.8 = (bf16[1,128,64,256]{3,2,1,0:T(8,128)(2,1)S(1)}, bf16[1,128,64,256]{3,2,1,0:T(8,128)(2,1)S(1)}, u32[]{:S(2)}, u32[]{:S(2)}) collective-permute-start(bf16[1,128,64,256]{3,2,1,0:T(8,128)(2,1)S(1)} %fusion.23), channel_id=1, source_target_pairs={{0,2},{2,4},{4,6},{6,8},{8,10},{10,12},{12,14},{14,16},{16,18},{18... | collective-permute-start | bytes 12582920 | tf_op jit(solution)/shard_map/ppermute | solution.py:18
  360.8 92.8 %collective-permute-start.9 = (bf16[1,128,64,256]{3,2,1,0:T(8,128)(2,1)S(1)}, bf16[1,128,64,256]{3,2,1,0:T(8,128)(2,1)S(1)}, u32[]{:S(2)}, u32[]{:S(2)}) collective-permute-start(bf16[1,128,64,256]{3,2,1,0:T(8,128)(2,1)S(1)} %fusion.23), channel_id=1, source_target_pairs={{2,0},{4,2},{6,4},{8,6},{10,8},{12,10},{14,12},{16,14},{18,16},{20... | collective-permute-start | bytes 12582920 | tf_op jit(solution)/shard_map/ppermute | solution.py:19
  453.6 2.0 copy-start.6
  453.6 3.3 copy-start.10
  456.9 6.5 %collective-permute-start.10 = (bf16[3,1,64,256]{3,2,1,0:T(8,128)(2,1)S(1)}, bf16[3,1,64,256]{3,2,1,0:T(8,128)(2,1)S(1)}, u32[]{:S(2)}, u32[]{:S(2)}) collective-permute-start(bf16[3,1,64,256]{3,2,1,0:T(8,128)(2,1)S(1)} %get-tuple-element.14), channel_id=1, source_target_pairs={{0,1},{2,3},{4,5},{6,7},{8,9},{10,11},{12,13},{14,15},{16,17},{18,... | collective-permute-start | bytes 294920 | tf_op jit(solution)/shard_map/ppermute | solution.py:18
  458.3 9.2 %copy-start.7 = (bf16[1,128,64,256]{3,2,1,0:T(8,128)(2,1)S(1)}, bf16[1,128,64,256]{3,2,1,0:T(8,128)(2,1)}, u32[]{:S(2)}) copy-start(bf16[1,128,64,256]{3,2,1,0:T(8,128)(2,1)} %copy-done.6) | copy-start | bytes 12582916
  458.3 11.7 %collective-permute-start.11 = (bf16[3,1,64,256]{3,2,1,0:T(8,128)(2,1)S(1)}, bf16[3,1,64,256]{3,2,1,0:T(8,128)(2,1)S(1)}, u32[]{:S(2)}, u32[]{:S(2)}) collective-permute-start(bf16[3,1,64,256]{3,2,1,0:T(8,128)(2,1)S(1)} %get-tuple-element.13), channel_id=1, source_target_pairs={{1,0},{3,2},{5,4},{7,6},{9,8},{11,10},{13,12},{15,14},{17,16},{19,... | collective-permute-start | bytes 294920 | tf_op jit(solution)/shard_map/ppermute | solution.py:19
  467.6 3.7 copy-start.3
  467.6 5.0 copy-start.11
  488.5 15.3 %copy-start.14 = (f32[1,128,512]{2,1,0:T(8,128)S(1)}, f32[1,128,512]{2,1,0:T(8,128)}, u32[]{:S(2)}) copy-start(f32[1,128,512]{2,1,0:T(8,128)} %param.12) | copy-start | bytes 786436
  488.5 15.3 %copy-start.15 = (f32[128,1,512]{2,0,1:T(8,128)S(1)}, f32[128,1,512]{2,0,1:T(8,128)}, u32[]{:S(2)}) copy-start(f32[128,1,512]{2,0,1:T(8,128)} %reduce-scatter.2.cloned.1.call-done) | copy-start | bytes 786436
Sparse Core Ops, SparseCore 0:
  124.6 14.8 reduce-scatter.1
where the time goes:
time: 515 us; the launch traced here: 512 us
  waiting for transfers between devices  197 us (38%)
  other arithmetic  105 us (20%)
  matrix products  89.5 us (17%)
  local copies, waits for them, and re-layouts  64.1 us (12%)
  starting transfers between devices  35 us (7%)
  between operations  14.1 us (3%)
  blocking collectives  6.43 us (1%)
    ppermute x6, waiting for transfers between devices, with_halo(): before = lax.ppermute(last, axis, up)  179 us
    dot_general x3, matrix products, conv_layer(): jnp.einsum('km,frmn->frkn', matrix, window, preferred_element_type=jnp.fl...  49.9 us
    unnamed x53, local copies, waits for them, and re-layouts  41.2 us
    unnamed x10, other arithmetic  26.2 us
    ppermute x6, starting transfers between devices, with_halo(): after = lax.ppermute(leading, axis, down)  23.6 us
    dot_general x1, matrix products, data_step(): jnp.einsum('fckm,mn->fckn', misfit, behind, preferred_element_type=f32)  23.1 us
    slice x3, local copies, waits for them, and re-layouts, conv_layer(): left_taps[..., :-1]  19.6 us
    add x1, other arithmetic, conj_mul(): first_re * second_re + first_im * second_im  18.8 us
  transfers between devices with their start and end apart: 13, of which 7 were waited for; matrix products, arithmetic and copies ran while one was open for 3% of the time, Pallas kernels for 0%

commit v1 on v0

v1 whole, which is shorter than its diff:
```python
import functools
import math

import jax
import jax.numpy as jnp
import numpy as np
from jax import lax
from jax.experimental import pallas as pl
from jax.experimental.pallas import tpu as pltpu
from jax.sharding import PartitionSpec as P

F32 = jnp.float32
BF16 = jnp.bfloat16

step_size = 1.0
RIM = 8
SLOT = 32


def dft_parts(order):
    indices = jnp.arange(order, dtype=jnp.int32)
    phases = indices[:, None] * indices[None, :] % order
    angles = phases.astype(F32) * (2.0 * math.pi / order)
    factor = 1.0 / math.sqrt(order)
    return (
        (jnp.cos(angles) * factor).astype(BF16),
        (-jnp.sin(angles) * factor).astype(BF16),
    )


def side_by_side(real_part, imag_part):
    return jnp.concatenate(
        [
            jnp.concatenate([real_part, imag_part], 1),
            jnp.concatenate([-imag_part, real_part], 1),
        ],
        0,
    )


def data_kernel(
    coils_at_once,
    chunk,
    where_ref,
    image_ref,
    others_ref,
    kspace_ref,
    sens_ref,
    mask_ref,
    col_ahead_ref,
    col_behind_ref,
    row_ahead_ref,
    row_behind_ref,
    own_ref,
    send_ref,
    full_ref,
    acc_ref,
    coil_ref,
    spec_ref,
    esti_ref,
):
    groups = others_ref.shape[0] + 1
    own_rows = image_ref.shape[0]
    n_rows, double = full_ref.shape
    half = double // 2
    me = where_ref[0]
    step = pl.program_id(0)

    @pl.when(step == 0)
    def _():
        acc_ref[...] = jnp.zeros_like(acc_ref)
        mine = pl.multiple_of(me * own_rows, RIM)
        acc_ref[pl.ds(pl.multiple_of(mine + RIM, RIM), own_rows), :] = image_ref[...]
        full_ref[pl.ds(mine, own_rows), :] = image_ref[...].astype(BF16).astype(F32)
        for hop in range(1, groups):
            theirs = pl.multiple_of(lax.rem(me + groups - hop, groups) * own_rows, RIM)
            full_ref[pl.ds(theirs, own_rows), :] = others_ref[hop - 1].astype(F32)

    for coil in range(coils_at_once):
        for start in range(0, n_rows, chunk):
            rows = slice(start, start + chunk)
            sens_re = sens_ref[coil, rows, :half].astype(F32)
            sens_im = sens_ref[coil, rows, half:].astype(F32)
            x_re, x_im = full_ref[rows, :half], full_ref[rows, half:]
            out = slice(coil * n_rows + start, coil * n_rows + start + chunk)
            coil_ref[out, :half] = (sens_re * x_re - sens_im * x_im).astype(BF16)
            coil_ref[out, half:] = (sens_re * x_im + sens_im * x_re).astype(BF16)
    spec_ref[...] = jnp.dot(
        coil_ref[...], col_ahead_ref[...], preferred_element_type=F32
    ).astype(BF16)
    for coil in range(coils_at_once):
        block = slice(coil * n_rows, (coil + 1) * n_rows)
        stacked = jnp.concatenate([spec_ref[block, :half], spec_ref[block, half:]], 0)
        esti_ref[coil] = jnp.dot(row_ahead_ref[...], stacked, preferred_element_type=F32)
    for coil in range(coils_at_once):
        sampled = jnp.broadcast_to(mask_ref[coil].astype(F32), (128, n_rows)).T
        for start in range(0, n_rows, chunk):
            rows = slice(start, start + chunk)
            out = slice(coil * n_rows + start, coil * n_rows + start + chunk)
            line = jnp.concatenate([sampled[rows]] * (half // 128), 1)
            coil_ref[out, :half] = (
                line * (esti_ref[coil, rows, :] - kspace_ref[coil, rows, :half].astype(F32))
            ).astype(BF16)
            lower = slice(n_rows + start, n_rows + start + chunk)
            coil_ref[out, half:] = (
                line * (esti_ref[coil, lower, :] - kspace_ref[coil, rows, half:].astype(F32))
            ).astype(BF16)
    spec_ref[...] = jnp.dot(
        coil_ref[...], col_behind_ref[...], preferred_element_type=F32
    ).astype(BF16)
    for coil in range(coils_at_once):
        block = slice(coil * n_rows, (coil + 1) * n_rows)
        stacked = jnp.concatenate([spec_ref[block, :half], spec_ref[block, half:]], 0)
        esti_ref[coil] = jnp.dot(row_behind_ref[...], stacked, preferred_element_type=F32)
    for start in range(0, n_rows, chunk):
        rows = slice(start, start + chunk)
        place = slice(RIM + start, RIM + start + chunk)
        lower = slice(n_rows + start, n_rows + start + chunk)
        total_re, total_im = acc_ref[place, :half], acc_ref[place, half:]
        for coil in range(coils_at_once):
            sens_re = sens_ref[coil, rows, :half].astype(F32) * step_size
            sens_im = sens_ref[coil, rows, half:].astype(F32) * step_size
            back_re, back_im = esti_ref[coil, rows, :], esti_ref[coil, lower, :]
            total_re = total_re - (sens_re * back_re + sens_im * back_im)
            total_im = total_im - (sens_re * back_im - sens_im * back_re)
        acc_ref[place, :half] = total_re
        acc_ref[place, half:] = total_im

    @pl.when(step == pl.num_programs(0) - 1)
    def _():
        window = own_rows + 2 * RIM
        own_ref[...] = acc_ref[pl.ds(pl.multiple_of(me * own_rows, RIM), window), :]
        for hop in range(1, groups):
            theirs = pl.multiple_of(lax.rem(me + hop, groups) * own_rows, RIM)
            send_ref[hop - 1] = acc_ref[pl.ds(theirs, window), :]


def data_step(image, kspace, sens, mask, here, groups):
    own_rows, double = image.shape
    coils, n_rows, _ = sens.shape
    half = double // 2
    coils_at_once = 2
    shift = lambda hop: [(i, (i + hop) % groups) for i in range(groups)]
    low = image.astype(BF16)
    others = jnp.stack([lax.ppermute(low, "coil", shift(hop)) for hop in range(1, groups)])
    row_re, row_im = dft_parts(n_rows)
    col_re, col_im = dft_parts(half)
    tables = (
        side_by_side(col_re, col_im),
        side_by_side(col_re, -col_im),
        side_by_side(row_re, row_im).T,
        side_by_side(row_re, -row_im).T,
    )
    window = own_rows + 2 * RIM
    whole = lambda a: pl.BlockSpec(a.shape, lambda i: (0,) * a.ndim)
    per_coil = lambda a: pl.BlockSpec(
        (coils_at_once,) + a.shape[1:], lambda i: (i,) + (0,) * (a.ndim - 1)
    )
    mask = mask.reshape(coils, 1, n_rows)
    own, send = pl.pallas_call(
        functools.partial(data_kernel, coils_at_once, 32),
        grid=(coils // coils_at_once,),
        in_specs=[
            pl.BlockSpec(memory_space=pltpu.SMEM),
            whole(image),
            whole(others),
            per_coil(kspace),
            per_coil(sens),
            per_coil(mask),
        ]
        + [whole(table) for table in tables],
        out_specs=[
            pl.BlockSpec((window, double), lambda i: (0, 0)),
            pl.BlockSpec((groups - 1, window, double), lambda i: (0, 0, 0)),
        ],
        out_shape=[
            jax.ShapeDtypeStruct((window, double), F32),
            jax.ShapeDtypeStruct((groups - 1, window, double), F32),
        ],
        scratch_shapes=[
            pltpu.VMEM((n_rows, double), F32),
            pltpu.VMEM((n_rows + 2 * RIM, double), F32),
            pltpu.VMEM((coils_at_once * n_rows, double), BF16),
            pltpu.VMEM((coils_at_once * n_rows, double), BF16),
            pltpu.VMEM((coils_at_once, 2 * n_rows, half), F32),
        ],
        cost_estimate=pl.CostEstimate(
            flops=32 * coils * n_rows * n_rows * half,
            bytes_accessed=4 * coils * n_rows * double,
            transcendentals=0,
        ),
        name="data_step",
    )(here, image, others, kspace, sens, mask, *tables)
    for hop in range(1, groups):
        own = own + lax.ppermute(send[hop - 1], "coil", shift(hop))
    return own


def first_selector(channels_in):
    taps = 27 * channels_in
    select = np.zeros((4, 3, taps + 3, 6 * SLOT), np.float32)
    for row in range(4):
        for frame in range(3):
            for a in range(3):
                for b in range(3):
                    for e in range(3):
                        for c in range(channels_in):
                            tap = ((a * 3 + b) * 3 + e) * channels_in + c
                            at = ((frame + a) * channels_in + c) * 3 + e
                            select[row, frame, tap, (row + b) * SLOT + at] = 1.0
            for part in range(3):
                at = (part // 2) * SLOT + SLOT - 2 + part % 2
                select[row, frame, taps + part, at] = 1.0
    return select.reshape(12, taps + 3, 6 * SLOT)


def three_parts(values):
    high = lax.reduce_precision(values, 8, 7)
    rest = values - high
    middle = lax.reduce_precision(rest, 8, 7)
    return jnp.stack([high, middle, rest - middle], -1).astype(BF16)


def shifted(values, amount):
    width = values.shape[-1]
    lane = lax.broadcasted_iota(jnp.int32, values.shape, 1)
    if amount > 0:
        return jnp.where(lane == 0, 0.0, pltpu.roll(values, 1, 1))
    return jnp.where(lane == width - 1, 0.0, pltpu.roll(values, width - 1, 1))


def denoise_kernel(
    where_ref,
    x_ref,
    f0_ref,
    f1_ref,
    f2_ref,
    f3_ref,
    f4_ref,
    w1_ref,
    select_ref,
    wm_ref,
    bm_ref,
    wl_ref,
    before_ref,
    base_ref,
    after_ref,
    slab_ref,
    wide_ref,
    h1_ref,
    h2_ref,
):
    window, double = x_ref.shape
    half = double // 2
    rows = window - 2 * RIM
    out_chan = w1_ref.shape[0]
    per_row = 3 * out_chan
    first_group, last_group = where_ref[0], where_ref[1]

    for frame, ref in enumerate((f0_ref, f1_ref, f2_ref, f3_ref, f4_ref)):
        for c in range(2):
            plane = ref[:, c * half : (c + 1) * half].astype(F32)
            for e, moved in enumerate((shifted(plane, 1), plane, shifted(plane, -1))):
                for j in range(half // 128):
                    slab_ref[j, pl.ds((frame * 2 + c) * 3 + e, window, stride=SLOT), :] = (
                        moved[:, j * 128 : (j + 1) * 128]
                    )
    ones = jnp.ones((window, 128), F32)
    for spare in (SLOT - 2, SLOT - 1):
        for j in range(half // 128):
            slab_ref[j, pl.ds(spare, window, stride=SLOT), :] = ones
    for row in range(4):
        for frame in range(3):
            band = jnp.dot(
                w1_ref[...], select_ref[row * 3 + frame], preferred_element_type=F32
            )
            if frame != 1:
                band = band * where_ref[2 + frame // 2].astype(F32)
            at = (row * 3 + frame) * out_chan
            wide_ref[at : at + out_chan, :] = band.astype(BF16)

    def first(q, carry):
        source = pl.multiple_of((4 * q + RIM - 3) * SLOT, SLOT)
        taps = jnp.concatenate(
            [slab_ref[j, pl.ds(source, 6 * SLOT), :] for j in range(half // 128)], 1
        ).astype(BF16)
        made = jnp.dot(wide_ref[...], taps, preferred_element_type=F32)
        target = pl.multiple_of(4 * q * per_row, per_row)
        h1_ref[pl.ds(target, 4 * per_row), :] = jnp.maximum(made, 0.0).astype(BF16)
        return carry

    lax.fori_loop(0, (rows + 4) // 4, first, 0)
    edge = jnp.zeros((2 * per_row, half), BF16)

    @pl.when(first_group == 1)
    def _():
        h1_ref[: 2 * per_row, :] = edge

    @pl.when(last_group == 1)
    def _():
        h1_ref[(rows + 2) * per_row :, :] = edge

    both = 2 * out_chan
    bias = jnp.broadcast_to(bm_ref[...], (both, half))

    def mid(p, carry):
        source = pl.multiple_of(2 * p * per_row, 2 * per_row)
        taps = h1_ref[pl.ds(source, 4 * per_row), :]
        made = jnp.dot(wm_ref[...], taps, preferred_element_type=F32)
        total = (
            made[both : 2 * both]
            + shifted(made[:both], 1)
            + shifted(made[2 * both :], -1)
            + bias
        )
        target = pl.multiple_of(p * both, both)
        h2_ref[pl.ds(target, both), :] = jnp.maximum(total, 0.0).astype(BF16)
        return carry

    lax.fori_loop(0, (rows + 2) // 2, mid, 0)
    edge2 = jnp.zeros((out_chan, half), BF16)

    @pl.when(first_group == 1)
    def _():
        h2_ref[:out_chan, :] = edge2

    @pl.when(last_group == 1)
    def _():
        h2_ref[(rows + 1) * out_chan :, :] = edge2

    def last(q, carry):
        source = pl.multiple_of(8 * q * out_chan, 8 * out_chan)
        taps = h2_ref[pl.ds(source, 10 * out_chan), :]
        made = jnp.dot(wl_ref[...], taps, preferred_element_type=F32)
        total = made[48:96] + shifted(made[:48], 1) + shifted(made[96:], -1)
        at = pl.ds(pl.multiple_of(8 * q, 8), 8)
        for c in range(2):
            lanes = slice(c * half, (c + 1) * half)
            piece = lambda a: total[(a * 2 + c) * 8 : (a * 2 + c) * 8 + 8]
            after_ref[at, lanes] = piece(0)
            base_ref[at, lanes] = (
                x_ref[pl.ds(pl.multiple_of(8 * q + RIM, 8), 8), lanes] + piece(1)
            )
            before_ref[at, lanes] = piece(2)
        return carry

    lax.fori_loop(0, rows // 8, last, 0)


def denoise(x, w_first, b_first, w_mid, b_mid, w_last, frame, frames, group, groups):
    window, double = x.shape
    rows, half = window - 2 * RIM, double // 2
    out_chan = w_mid.shape[3]
    hidden = x.astype(BF16)
    near = {0: hidden}
    for by in (1, 2):
        near[-by] = lax.ppermute(hidden, "frame", [(i, i + by) for i in range(frames - by)])
        near[by] = lax.ppermute(hidden, "frame", [(i + by, i) for i in range(frames - by)])
    where = jnp.stack(
        [group == 0, group == groups - 1, frame > 0, frame < frames - 1]
    ).astype(jnp.int32)
    w1 = jnp.concatenate(
        [
            jnp.transpose(w_first, (3, 0, 1, 2, 4)).reshape(out_chan, -1),
            three_parts(b_first),
        ],
        1,
    )
    select = jnp.asarray(first_selector(w_first.shape[4]), BF16)
    mid = jnp.transpose(w_mid, (2, 3, 1, 0, 4)).reshape(3, out_chan, -1)
    spare = 3 * out_chan
    wm = jnp.stack(
        [
            jnp.pad(mid, ((0, 0), (0, 0), (0, spare))),
            jnp.pad(mid, ((0, 0), (0, 0), (spare, 0))),
        ],
        1,
    ).reshape(6 * out_chan, -1)
    bm = jnp.concatenate([b_mid, b_mid])[:, None]
    last = jnp.transpose(w_last, (2, 0, 3, 1, 4)).reshape(18, -1)
    wl = jnp.stack(
        [jnp.pad(last, ((0, 0), (r * out_chan, (7 - r) * out_chan))) for r in range(8)], 1
    ).reshape(144, -1)
    vmem = pl.BlockSpec(memory_space=pltpu.VMEM)
    out = jax.ShapeDtypeStruct((rows, double), F32)
    before, base, after = pl.pallas_call(
        denoise_kernel,
        in_specs=[pl.BlockSpec(memory_space=pltpu.SMEM)] + [vmem] * 11,
        out_specs=[vmem] * 3,
        out_shape=[out] * 3,
        scratch_shapes=[
            pltpu.VMEM((half // 128, window * SLOT, 128), F32),
            pltpu.VMEM((12 * out_chan, 6 * SLOT), BF16),
            pltpu.VMEM(((rows + 4) * 3 * out_chan, half), BF16),
            pltpu.VMEM(((rows + 2) * out_chan, half), BF16),
        ],
        cost_estimate=pl.CostEstimate(
            flops=2 * (rows + 2) * half * 192 * 1152,
            bytes_accessed=4 * window * double * 5,
            transcendentals=0,
        ),
        name="denoise",
    )(where, x, *[near[by] for by in (-2, -1, 0, 1, 2)], w1, select, wm, bm, wl)
    upward = [(i, i + 1) for i in range(frames - 1)]
    downward = [(i + 1, i) for i in range(frames - 1)]
    return (
        base + lax.ppermute(after, "frame", upward) + lax.ppermute(before, "frame", downward)
    )


def shards(kspace, sens, mask, image, w_first, b_first, w_mid, b_mid, w_last):
    frame, group = lax.axis_index("frame"), lax.axis_index("coil")
    frames, groups = lax.axis_size("frame"), lax.axis_size("coil")
    here = group.astype(jnp.int32)[None]
    x = data_step(image[0], kspace[0], sens, mask[0], here, groups)
    return denoise(x, w_first, b_first, w_mid, b_mid, w_last, frame, frames, group, groups)[None]


def solution(mesh):
    in_specs = (
        P("frame", "coil", None, None),
        P("coil", None, None),
        P("frame", "coil", None),
        P("frame", "coil", None),
        P(),
        P(),
        P(),
        P(),
        P(),
    )
    out_specs = P("frame", "coil", None)
    return jax.shard_map(shards, mesh=mesh, in_specs=in_specs, out_specs=out_specs, check_vma=False)
```

time: 515 us -> 129 us (0.25)
  the two profiles are of different devices: /device:TPU:6 before, /device:TPU:1 now
where the time goes in v1:
time: 129 us; the launch traced here: 128 us
  Pallas kernels  75.1 us (58%)
  starting transfers between devices  20.1 us (16%)
  waiting for transfers between devices  14.6 us (11%)
  other arithmetic  9.26 us (7%)
  local copies, waits for them, and re-layouts  9.07 us (7%)
    pallas_call x1, Pallas kernels, denoise(): pl.pallas_call(denoise_kernel, in_specs=[pl.BlockSpec(memory_space=pltpu....  46.5 us
    pallas_call x1, Pallas kernels, data_step(): pl.pallas_call(functools.partial(data_kernel, coils_at_once, 32), grid=(c...  28.7 us
    ppermute x2, starting transfers between devices, denoise(): lax.ppermute(hidden, 'frame', [(i, i + by) for i in range(frames - by)])  8.1 us
    ppermute x1, waiting for transfers between devices, data_step(): own = own + lax.ppermute(send[hop - 1], 'coil', shift(hop))  7.8 us
    ppermute x1, starting transfers between devices, denoise(): lax.ppermute(after, 'frame', upward)  3.98 us
    ppermute x2, starting transfers between devices, denoise(): lax.ppermute(hidden, 'frame', [(i + by, i) for i in range(frames - by)])  3.21 us
    ppermute x1, starting transfers between devices, denoise(): lax.ppermute(before, 'frame', downward)  2.64 us
  transfers between devices with their start and end apart: 8, of which 4 were waited for; matrix products, arithmetic and copies ran while one was open for 10% of the time, Pallas kernels for 0%

profile of v1, /device:TPU:1, one launch (start us, length us, event | category | flops | bytes accessed | tf_op | source)
XLA Modules:
  0.0 128.2 jit_solution(12946106694044334257)
XLA Ops:
  0.0 1.0 bitcast_convert_fusion
  1.0 2.1 %collective-permute-start = (bf16[128,512]{1,0:T(8,128)(2,1)S(1)}, bf16[128,512]{1,0:T(8,128)(2,1)S(1)}, u32[]{:S(2)}, u32[]{:S(2)}) collective-permute-start(bf16[128,512]{1,0:T(8,128)(2,1)S(1)} %bitcast_convert_fusion), channel_id=1, source_target_pairs={{0,1},{1,0},{2,3},{3,2},{4,5},{5,4},{6,7},{7,6},{8,9},{9,8},{10,11... | collective-permute-start | bytes 393224 | tf_op jit(solution)/shard_map/ppermute | solution.py:145
  3.1 1.1 multiply_convert_fusion
  4.2 1.0 fusion.8
  5.2 1.4 %reshape_squeeze.3.mask_ref = s32[32,1,256]{2,1,0:T(1,128)} reshape(s32[1,32,256]{2,1,0:T(8,128)} %param.12) | data formatting | bytes 65536 | tf_op jit(solution)/shard_map/reshape;squeeze | solution.py:159
  6.6 1.2 fusion.13
  7.8 0.0 copy-start
  7.8 1.0 copy.26.col_ahead_ref
  8.8 1.0 copy.27.col_behind_ref
  9.8 0.0 copy-done
  9.8 0.0 copy-start.3
  9.8 0.2 copy.32
  10.0 0.2 pad_bitcast_fusion.1
  10.2 0.3 copy-done.3
  10.5 0.1 reshape.18
  10.6 0.1 bitcast_dynamic-update-slice_fusion.6
  10.7 0.1 bitcast_dynamic-update-slice_fusion.4
  10.8 0.1 bitcast_dynamic-update-slice_fusion.2
  10.9 0.1 bitcast_dynamic-update-slice_fusion
  11.0 0.3 pad_maximum_fusion
  11.2 0.0 collective-permute-done
  11.3 0.0 copy-start.9
  11.3 0.6 copy-done.9
  11.9 0.0 copy-start.10
  11.9 0.0 copy-start.4
  11.9 0.0 copy-start.2
  11.9 28.7 %data_step.1 = (f32[144,512]{1,0:T(8,128)}, f32[1,144,512]{2,1,0:T(8,128)}) custom-call(s32[1]{0:T(128)} %bitcast.4.where_ref, f32[128,512]{1,0:T(8,128)} %bitcast.57, bf16[1,128,512]{2,1,0:T(8,128)(2,1)} %bitcast.63, bf16[32,256,512]{2,1,0:T(8,128)(2,1)} %bitcast.61, bf16[32,256,512]{2,1,0:T(8,128)(2,1)} %sens_ref.1, ...), custom_call_target="tpu_custom_call" | custom-call | flops 17179869184 | bytes 16777216 | tf_op jit(solution)/shard_map/data_step/pallas_call | solution.py:160
  40.6 0.0 collective-permute-start.1
  40.6 0.0 copy-done.10
  40.6 0.1 maximum_bitcast_fusion
  40.7 0.0 copy-done.4
  40.7 7.8 %collective-permute-done.1 = f32[144,512]{1,0:T(8,128)S(1)} collective-permute-done((f32[144,512]{1,0:T(8,128)}, f32[144,512]{1,0:T(8,128)S(1)}, u32[]{:S(2)}, u32[]{:S(2)}) %collective-permute-start.1) | collective-permute-done | bytes 294944 | tf_op jit(solution)/shard_map/ppermute | solution.py:195
  48.5 1.7 %fusion.15 = (bf16[144,512]{1,0:T(8,128)(2,1)S(1)}, f32[144,512]{1,0:T(8,128)}) fusion(f32[144,512]{1,0:T(8,128)} %get-tuple-element.10, f32[144,512]{1,0:T(8,128)S(1)} %collective-permute-done.1), kind=kLoop, calls=%fused_computation.45 | loop fusion | flops 147456 | bytes 1032192 | tf_op jit(solution)/shard_map/convert_element_type | solution.py:354
  50.2 3.0 %collective-permute-start.2 = (bf16[144,512]{1,0:T(8,128)(2,1)S(1)}, bf16[144,512]{1,0:T(8,128)(2,1)S(1)}, u32[]{:S(2)}, u32[]{:S(2)}) collective-permute-start(bf16[144,512]{1,0:T(8,128)(2,1)S(1)} %get-tuple-element.15.f2_ref), channel_id=1, source_target_pairs={{0,4},{2,6},{4,8},{6,10},{8,12},{10,14},{12,16},{14,18},{16,20},{1... | collective-permute-start | bytes 442376 | tf_op jit(solution)/shard_map/ppermute | solution.py:357
  53.2 5.1 %collective-permute-start.3 = (bf16[144,512]{1,0:T(8,128)(2,1)S(1)}, bf16[144,512]{1,0:T(8,128)(2,1)S(1)}, u32[]{:S(2)}, u32[]{:S(2)}) collective-permute-start(bf16[144,512]{1,0:T(8,128)(2,1)S(1)} %get-tuple-element.15.f2_ref), channel_id=1, source_target_pairs={{0,2},{2,4},{4,6},{6,8},{8,10},{10,12},{12,14},{14,16},{16,18},{18... | collective-permute-start | bytes 442376 | tf_op jit(solution)/shard_map/ppermute | solution.py:357
  58.3 1.9 %collective-permute-start.4 = (bf16[144,512]{1,0:T(8,128)(2,1)S(1)}, bf16[144,512]{1,0:T(8,128)(2,1)S(1)}, u32[]{:S(2)}, u32[]{:S(2)}) collective-permute-start(bf16[144,512]{1,0:T(8,128)(2,1)S(1)} %get-tuple-element.15.f2_ref), channel_id=1, source_target_pairs={{2,0},{4,2},{6,4},{8,6},{10,8},{12,10},{14,12},{16,14},{18,16},{20... | collective-permute-start | bytes 442376 | tf_op jit(solution)/shard_map/ppermute | solution.py:358
  60.3 1.3 %collective-permute-start.5 = (bf16[144,512]{1,0:T(8,128)(2,1)S(1)}, bf16[144,512]{1,0:T(8,128)(2,1)S(1)}, u32[]{:S(2)}, u32[]{:S(2)}) collective-permute-start(bf16[144,512]{1,0:T(8,128)(2,1)S(1)} %get-tuple-element.15.f2_ref), channel_id=1, source_target_pairs={{4,0},{6,2},{8,4},{10,6},{12,8},{14,10},{16,12},{18,14},{20,16},{2... | collective-permute-start | bytes 442376 | tf_op jit(solution)/shard_map/ppermute | solution.py:358
  61.6 0.6 add_convert_fusion.where_ref
  62.1 0.1 copy.31
  62.2 0.1 copy.30
  62.3 0.1 copy.29
  62.5 0.0 copy-done.2
  62.5 0.1 copy.28
  62.6 1.3 copy.33
  63.9 0.7 copy.36.bm_ref
  64.6 0.7 copy.38
  65.3 0.0 copy-done.1
  65.3 0.7 pad_maximum_fusion.5.w1_ref
  66.0 0.0 collective-permute-done.2.f0_ref
  66.0 0.0 collective-permute-done.3.f1_ref
  66.0 0.0 copy-start.6
  66.0 0.0 collective-permute-done.4.f3_ref
  66.0 0.0 copy-start.7
  66.0 1.9 %collective-permute-done.5.f4_ref = bf16[144,512]{1,0:T(8,128)(2,1)S(1)} collective-permute-done((bf16[144,512]{1,0:T(8,128)(2,1)S(1)}, bf16[144,512]{1,0:T(8,128)(2,1)S(1)}, u32[]{:S(2)}, u32[]{:S(2)}) %collective-permute-start.5) | collective-permute-done | bytes 147488 | tf_op jit(solution)/shard_map/ppermute | solution.py:358
  67.9 0.0 copy-done.5
  67.9 0.0 copy-done.6
  67.9 0.0 copy-done.7
  67.9 0.6 copy-done.8
  68.5 46.5 %denoise.1 = (f32[128,512]{1,0:T(8,128)}, f32[128,512]{1,0:T(8,128)}, f32[128,512]{1,0:T(8,128)}) custom-call(s32[4]{0:T(128)} %add_convert_fusion.where_ref, f32[144,512]{1,0:T(8,128)} %get-tuple-element.16.x_ref, bf16[144,512]{1,0:T(8,128)(2,1)} %copy-done.5, bf16[144,512]{1,0:T(8,128)(2,1)} %copy-done.6, bf16[144,512]{1,0:T(8,128)(2,1)} %copy-done.1, ...), custom_call_target="tpu_custom_call" | custom-call | flops 14722007040 | bytes 1474560 | tf_op jit(solution)/shard_map/denoise/pallas_call | solution.py:386
  115.0 2.6 %collective-permute-start.7 = (f32[128,512]{1,0:T(8,128)}, f32[128,512]{1,0:T(8,128)S(1)}, u32[]{:S(2)}, u32[]{:S(2)}) collective-permute-start(f32[128,512]{1,0:T(8,128)} %get-tuple-element.14), channel_id=1, source_target_pairs={{2,0},{4,2},{6,4},{8,6},{10,8},{12,10},{14,12},{16,14},{18,16},{20... | collective-permute-start | bytes 786440 | tf_op jit(solution)/shard_map/ppermute | solution.py:407
  117.6 4.0 %collective-permute-start.6 = (f32[128,512]{1,0:T(8,128)}, f32[128,512]{1,0:T(8,128)S(1)}, u32[]{:S(2)}, u32[]{:S(2)}) collective-permute-start(f32[128,512]{1,0:T(8,128)} %get-tuple-element.13), channel_id=1, source_target_pairs={{0,2},{2,4},{4,6},{6,8},{8,10},{10,12},{12,14},{14,16},{16,18},{18... | collective-permute-start | bytes 786440 | tf_op jit(solution)/shard_map/ppermute | solution.py:407
  121.6 2.3 %collective-permute-done.7 = f32[128,512]{1,0:T(8,128)S(1)} collective-permute-done((f32[128,512]{1,0:T(8,128)}, f32[128,512]{1,0:T(8,128)S(1)}, u32[]{:S(2)}, u32[]{:S(2)}) %collective-permute-start.7) | collective-permute-done | bytes 262176 | tf_op jit(solution)/shard_map/ppermute | solution.py:407
  124.0 2.6 %collective-permute-done.6 = f32[128,512]{1,0:T(8,128)S(1)} collective-permute-done((f32[128,512]{1,0:T(8,128)}, f32[128,512]{1,0:T(8,128)S(1)}, u32[]{:S(2)}, u32[]{:S(2)}) %collective-permute-start.6) | collective-permute-done | bytes 262176 | tf_op jit(solution)/shard_map/ppermute | solution.py:407
  126.5 1.7 %add_bitcast_fusion = f32[1,128,512]{2,1,0:T(8,128)} fusion(f32[128,512]{1,0:T(8,128)S(1)} %collective-permute-done.7, f32[128,512]{1,0:T(8,128)} %get-tuple-element.12, f32[128,512]{1,0:T(8,128)S(1)} %collective-permute-done.6), kind=kLoop, calls=%fused_computation.15 | loop fusion | flops 131072 | bytes 1048576 | tf_op jit(solution)/shard_map/broadcast_in_dim | solution.py:416
  (10 shorter events, 0.1 us)
Async XLA Ops:
  1.0 10.3 %collective-permute-start = (bf16[128,512]{1,0:T(8,128)(2,1)S(1)}, bf16[128,512]{1,0:T(8,128)(2,1)S(1)}, u32[]{:S(2)}, u32[]{:S(2)}) collective-permute-start(bf16[128,512]{1,0:T(8,128)(2,1)S(1)} %bitcast_convert_fusion), channel_id=1, source_target_pairs={{0,1},{1,0},{2,3},{3,2},{4,5},{5,4},{6,7},{7,6},{8,9},{9,8},{10,11... | collective-permute-start | bytes 393224 | tf_op jit(solution)/shard_map/ppermute | solution.py:145
  7.8 2.0 %copy-start = (bf16[3,3,3,64,64]{4,3,2,1,0:T(8,128)(2,1)S(1)}, bf16[3,3,3,64,64]{4,3,2,1,0:T(8,128)(2,1)}, u32[]{:S(2)}) copy-start(bf16[3,3,3,64,64]{4,3,2,1,0:T(8,128)(2,1)} %param.16) | copy-start | bytes 663556
  9.8 0.7 copy-start.3
  11.3 0.7 copy-start.9
  11.9 28.7 %copy-start.10 = (f32[64]{0:T(128)S(1)}, f32[64]{0:T(128)}, u32[]{:S(2)}) copy-start(f32[64]{0:T(128)} %param.17) | copy-start | bytes 772
  11.9 28.8 %copy-start.4 = (f32[64]{0:T(128)S(1)}, f32[64]{0:T(128)}, u32[]{:S(2)}) copy-start(f32[64]{0:T(128)} %param.15) | copy-start | bytes 772
  11.9 50.5 %copy-start.2 = (bf16[3,3,3,64,2]{3,4,2,1,0:T(2,128)(2,1)S(1)}, bf16[3,3,3,64,2]{3,4,2,1,0:T(2,128)(2,1)}, u32[]{:S(2)}) copy-start(bf16[3,3,3,64,2]{3,4,2,1,0:T(2,128)(2,1)} %param.14) | copy-start | bytes 20740
  40.6 7.9 %collective-permute-start.1 = (f32[144,512]{1,0:T(8,128)}, f32[144,512]{1,0:T(8,128)S(1)}, u32[]{:S(2)}, u32[]{:S(2)}) collective-permute-start(f32[144,512]{1,0:T(8,128)} %bitcast.62), channel_id=1, source_target_pairs={{0,1},{1,0},{2,3},{3,2},{4,5},{5,4},{6,7},{7,6},{8,9},{9,8},{10,11... | collective-permute-start | bytes 884744 | tf_op jit(solution)/shard_map/ppermute | solution.py:195
  50.2 15.1 %copy-start.1 = (bf16[144,512]{1,0:T(8,128)(2,1)}, bf16[144,512]{1,0:T(8,128)(2,1)S(1)}, u32[]{:S(2)}) copy-start(bf16[144,512]{1,0:T(8,128)(2,1)S(1)} %get-tuple-element.15.f2_ref) | copy-start | bytes 442372
  50.2 15.8 %collective-permute-start.2 = (bf16[144,512]{1,0:T(8,128)(2,1)S(1)}, bf16[144,512]{1,0:T(8,128)(2,1)S(1)}, u32[]{:S(2)}, u32[]{:S(2)}) collective-permute-start(bf16[144,512]{1,0:T(8,128)(2,1)S(1)} %get-tuple-element.15.f2_ref), channel_id=1, source_target_pairs={{0,4},{2,6},{4,8},{6,10},{8,12},{10,14},{12,16},{14,18},{16,20},{1... | collective-permute-start | bytes 442376 | tf_op jit(solution)/shard_map/ppermute | solution.py:357
  53.2 12.8 %collective-permute-start.3 = (bf16[144,512]{1,0:T(8,128)(2,1)S(1)}, bf16[144,512]{1,0:T(8,128)(2,1)S(1)}, u32[]{:S(2)}, u32[]{:S(2)}) collective-permute-start(bf16[144,512]{1,0:T(8,128)(2,1)S(1)} %get-tuple-element.15.f2_ref), channel_id=1, source_target_pairs={{0,2},{2,4},{4,6},{6,8},{8,10},{10,12},{12,14},{14,16},{16,18},{18... | collective-permute-start | bytes 442376 | tf_op jit(solution)/shard_map/ppermute | solution.py:357
  58.3 7.7 %collective-permute-start.4 = (bf16[144,512]{1,0:T(8,128)(2,1)S(1)}, bf16[144,512]{1,0:T(8,128)(2,1)S(1)}, u32[]{:S(2)}, u32[]{:S(2)}) collective-permute-start(bf16[144,512]{1,0:T(8,128)(2,1)S(1)} %get-tuple-element.15.f2_ref), channel_id=1, source_target_pairs={{2,0},{4,2},{6,4},{8,6},{10,8},{12,10},{14,12},{16,14},{18,16},{20... | collective-permute-start | bytes 442376 | tf_op jit(solution)/shard_map/ppermute | solution.py:358
  60.3 7.6 %collective-permute-start.5 = (bf16[144,512]{1,0:T(8,128)(2,1)S(1)}, bf16[144,512]{1,0:T(8,128)(2,1)S(1)}, u32[]{:S(2)}, u32[]{:S(2)}) collective-permute-start(bf16[144,512]{1,0:T(8,128)(2,1)S(1)} %get-tuple-element.15.f2_ref), channel_id=1, source_target_pairs={{4,0},{6,2},{8,4},{10,6},{12,8},{14,10},{16,12},{18,14},{20,16},{2... | collective-permute-start | bytes 442376 | tf_op jit(solution)/shard_map/ppermute | solution.py:358
  66.0 1.9 %copy-start.5 = (bf16[144,512]{1,0:T(8,128)(2,1)}, bf16[144,512]{1,0:T(8,128)(2,1)S(1)}, u32[]{:S(2)}) copy-start(bf16[144,512]{1,0:T(8,128)(2,1)S(1)} %collective-permute-done.2.f0_ref) | copy-start | bytes 442372
  66.0 1.9 %copy-start.6 = (bf16[144,512]{1,0:T(8,128)(2,1)}, bf16[144,512]{1,0:T(8,128)(2,1)S(1)}, u32[]{:S(2)}) copy-start(bf16[144,512]{1,0:T(8,128)(2,1)S(1)} %collective-permute-done.3.f1_ref) | copy-start | bytes 442372
  66.0 1.9 %copy-start.7 = (bf16[144,512]{1,0:T(8,128)(2,1)}, bf16[144,512]{1,0:T(8,128)(2,1)S(1)}, u32[]{:S(2)}) copy-start(bf16[144,512]{1,0:T(8,128)(2,1)S(1)} %collective-permute-done.4.f3_ref) | copy-start | bytes 442372
  67.9 0.7 copy-start.8
  115.0 9.0 %collective-permute-start.7 = (f32[128,512]{1,0:T(8,128)}, f32[128,512]{1,0:T(8,128)S(1)}, u32[]{:S(2)}, u32[]{:S(2)}) collective-permute-start(f32[128,512]{1,0:T(8,128)} %get-tuple-element.14), channel_id=1, source_target_pairs={{2,0},{4,2},{6,4},{8,6},{10,8},{12,10},{14,12},{16,14},{18,16},{20... | collective-permute-start | bytes 786440 | tf_op jit(solution)/shard_map/ppermute | solution.py:407
  117.6 8.9 %collective-permute-start.6 = (f32[128,512]{1,0:T(8,128)}, f32[128,512]{1,0:T(8,128)S(1)}, u32[]{:S(2)}, u32[]{:S(2)}) collective-permute-start(f32[128,512]{1,0:T(8,128)} %get-tuple-element.13), channel_id=1, source_target_pairs={{0,2},{2,4},{4,6},{6,8},{8,10},{10,12},{12,14},{14,16},{16,18},{18... | collective-permute-start | bytes 786440 | tf_op jit(solution)/shard_map/ppermute | solution.py:407

commit v2 on v1

v2 whole, which is shorter than its diff:
```python
import functools
import math

import jax
import jax.numpy as jnp
import numpy as np
from jax import lax
from jax.experimental import pallas as pl
from jax.experimental.pallas import tpu as pltpu
from jax.sharding import PartitionSpec as P

F32 = jnp.float32
BF16 = jnp.bfloat16

step_size = 1.0
RIM = 8
SLOT = 32


def dft_parts(order):
    indices = np.arange(order)
    angles = (indices[:, None] * indices[None, :] % order).astype(np.float32)
    angles = angles * np.float32(2.0 * math.pi / order)
    factor = np.float32(1.0 / math.sqrt(order))
    return jnp.asarray(np.stack([np.cos(angles) * factor, -np.sin(angles) * factor]), BF16)


def put_table(ref, top_left, top_right, low_left, low_right):
    half = top_left.shape[0]
    ref[:half, :half] = top_left
    ref[:half, half:] = top_right
    ref[half:, :half] = low_left
    ref[half:, half:] = low_right


def data_kernel(
    coils_at_once,
    chunk,
    where_ref,
    image_ref,
    others_ref,
    kspace_ref,
    sens_ref,
    mask_ref,
    cols_ref,
    lines_ref,
    own_ref,
    send_ref,
    full_ref,
    acc_ref,
    coil_ref,
    spec_ref,
    esti_ref,
    miss_ref,
    back_ref,
    bimg_ref,
    col_ahead_ref,
    col_behind_ref,
    row_ahead_ref,
    row_behind_ref,
):
    groups = others_ref.shape[0] + 1
    own_rows = image_ref.shape[0]
    n_rows, double = full_ref.shape
    half = double // 2
    me = where_ref[0]
    step = pl.program_id(0)

    @pl.when(step == 0)
    def _():
        for ref, ahead_ref, behind_ref in (
            (cols_ref, col_ahead_ref, col_behind_ref),
            (lines_ref, row_behind_ref, row_ahead_ref),
        ):
            real, imag = ref[0], ref[1]
            put_table(ahead_ref, real, imag, -imag, real)
            put_table(behind_ref, real, -imag, imag, real)
        acc_ref[...] = jnp.zeros_like(acc_ref)
        mine = pl.multiple_of(me * own_rows, RIM)
        acc_ref[pl.ds(pl.multiple_of(mine + RIM, RIM), own_rows), :] = image_ref[...]
        full_ref[pl.ds(mine, own_rows), :] = image_ref[...].astype(BF16).astype(F32)
        for hop in range(1, groups):
            theirs = pl.multiple_of(lax.rem(me + groups - hop, groups) * own_rows, RIM)
            full_ref[pl.ds(theirs, own_rows), :] = others_ref[hop - 1].astype(F32)

    for coil in range(coils_at_once):
        for start in range(0, n_rows, chunk):
            rows = slice(start, start + chunk)
            sens_re = sens_ref[coil, rows, :half].astype(F32)
            sens_im = sens_ref[coil, rows, half:].astype(F32)
            x_re, x_im = full_ref[rows, :half], full_ref[rows, half:]
            out = slice(coil * n_rows + start, coil * n_rows + start + chunk)
            coil_ref[out, :half] = (sens_re * x_re - sens_im * x_im).astype(BF16)
            coil_ref[out, half:] = (sens_re * x_im + sens_im * x_re).astype(BF16)
    spec_ref[...] = jnp.dot(
        coil_ref[...], col_ahead_ref[...], preferred_element_type=F32
    ).astype(BF16)
    for coil in range(coils_at_once):
        block = slice(coil * n_rows, (coil + 1) * n_rows)
        stacked = jnp.concatenate([spec_ref[block, :half], spec_ref[block, half:]], 0)
        esti_ref[coil] = jnp.dot(row_ahead_ref[...], stacked, preferred_element_type=F32)
    for coil in range(coils_at_once):
        line = mask_ref[pl.ds(step * coils_at_once + coil, 1), :].astype(F32)
        sampled = jnp.broadcast_to(line, (128, n_rows)).T
        for start in range(0, n_rows, chunk):
            rows = slice(start, start + chunk)
            out = slice(coil * n_rows + start, coil * n_rows + start + chunk)
            line = jnp.concatenate([sampled[rows]] * (half // 128), 1)
            miss_ref[out, :half] = (
                line * (esti_ref[coil, rows, :] - kspace_ref[coil, rows, :half].astype(F32))
            ).astype(BF16)
            lower = slice(n_rows + start, n_rows + start + chunk)
            miss_ref[out, half:] = (
                line * (esti_ref[coil, lower, :] - kspace_ref[coil, rows, half:].astype(F32))
            ).astype(BF16)
    back_ref[...] = jnp.dot(
        miss_ref[...], col_behind_ref[...], preferred_element_type=F32
    ).astype(BF16)
    for coil in range(coils_at_once):
        block = slice(coil * n_rows, (coil + 1) * n_rows)
        stacked = jnp.concatenate([back_ref[block, :half], back_ref[block, half:]], 0)
        bimg_ref[coil] = jnp.dot(row_behind_ref[...], stacked, preferred_element_type=F32)
    for start in range(0, n_rows, chunk):
        rows = slice(start, start + chunk)
        place = slice(RIM + start, RIM + start + chunk)
        lower = slice(n_rows + start, n_rows + start + chunk)
        total_re, total_im = acc_ref[place, :half], acc_ref[place, half:]
        for coil in range(coils_at_once):
            sens_re = sens_ref[coil, rows, :half].astype(F32) * step_size
            sens_im = sens_ref[coil, rows, half:].astype(F32) * step_size
            back_re, back_im = bimg_ref[coil, rows, :], bimg_ref[coil, lower, :]
            total_re = total_re - (sens_re * back_re + sens_im * back_im)
            total_im = total_im - (sens_re * back_im - sens_im * back_re)
        acc_ref[place, :half] = total_re
        acc_ref[place, half:] = total_im

    @pl.when(step == pl.num_programs(0) - 1)
    def _():
        window = own_rows + 2 * RIM
        own_ref[...] = acc_ref[pl.ds(pl.multiple_of(me * own_rows, RIM), window), :]
        for hop in range(1, groups):
            theirs = pl.multiple_of(lax.rem(me + hop, groups) * own_rows, RIM)
            send_ref[hop - 1] = acc_ref[pl.ds(theirs, window), :].astype(BF16)


def data_step(image, kspace, sens, mask, here, groups):
    own_rows, double = image.shape
    coils, n_rows, _ = sens.shape
    half = double // 2
    coils_at_once = unrolled(coils, 4)
    shift = lambda hop: [(i, (i + hop) % groups) for i in range(groups)]
    low = image.astype(BF16)
    others = jnp.stack([lax.ppermute(low, "coil", shift(hop)) for hop in range(1, groups)])
    cols, lines = dft_parts(half), dft_parts(n_rows)
    window = own_rows + 2 * RIM
    whole = lambda a: pl.BlockSpec(a.shape, lambda i: (0,) * a.ndim)
    per_coil = lambda a: pl.BlockSpec(
        (coils_at_once,) + a.shape[1:], lambda i: (i,) + (0,) * (a.ndim - 1)
    )
    own, send = pl.pallas_call(
        functools.partial(data_kernel, coils_at_once, 32),
        grid=(coils // coils_at_once,),
        in_specs=[
            pl.BlockSpec(memory_space=pltpu.SMEM),
            whole(image),
            whole(others),
            per_coil(kspace),
            per_coil(sens),
            whole(mask),
            whole(cols),
            whole(lines),
        ],
        out_specs=[
            pl.BlockSpec((window, double), lambda i: (0, 0)),
            pl.BlockSpec((groups - 1, window, double), lambda i: (0, 0, 0)),
        ],
        out_shape=[
            jax.ShapeDtypeStruct((window, double), F32),
            jax.ShapeDtypeStruct((groups - 1, window, double), BF16),
        ],
        scratch_shapes=[
            pltpu.VMEM((n_rows, double), F32),
            pltpu.VMEM((n_rows + 2 * RIM, double), F32),
            pltpu.VMEM((coils_at_once * n_rows, double), BF16),
            pltpu.VMEM((coils_at_once * n_rows, double), BF16),
            pltpu.VMEM((coils_at_once, 2 * n_rows, half), F32),
            pltpu.VMEM((coils_at_once * n_rows, double), BF16),
            pltpu.VMEM((coils_at_once * n_rows, double), BF16),
            pltpu.VMEM((coils_at_once, 2 * n_rows, half), F32),
        ]
        + [pltpu.VMEM((double, double), BF16)] * 2
        + [pltpu.VMEM((2 * n_rows, 2 * n_rows), BF16)] * 2,
        compiler_params=pltpu.CompilerParams(vmem_limit_bytes=57 << 20),
        cost_estimate=pl.CostEstimate(
            flops=32 * coils * n_rows * n_rows * half,
            bytes_accessed=4 * coils * n_rows * double,
            transcendentals=0,
        ),
        name="data_step",
    )(here, image, others, kspace, sens, mask, cols, lines)
    for hop in range(1, groups):
        own = own + lax.ppermute(send[hop - 1], "coil", shift(hop)).astype(F32)
    return own


def first_selector(channels_in):
    taps = 27 * channels_in
    select = np.zeros((4, 3, 64, 6 * SLOT), np.float32)
    for row in range(4):
        for frame in range(3):
            for a in range(3):
                for b in range(3):
                    for e in range(3):
                        for c in range(channels_in):
                            tap = ((a * 3 + b) * 3 + e) * channels_in + c
                            at = ((frame + a) * channels_in + c) * 3 + e
                            select[row, frame, tap, (row + b) * SLOT + at] = 1.0
            for part in range(3):
                at = (part // 2) * SLOT + SLOT - 2 + part % 2
                select[row, frame, taps + part, at] = 1.0
    return select.reshape(12, 64, 6 * SLOT)


def interleaver():
    order = np.zeros((8 * SLOT, 8 * SLOT), np.float32)
    for row in range(8):
        for plane in range(SLOT):
            order[row * SLOT + plane, plane * 8 + row] = 1.0
    return order


def last_selector():
    select = np.zeros((3, 3, 3, 2, 8, 54), np.float32)
    for b in range(3):
        for e in range(3):
            for a in range(3):
                for c in range(2):
                    select[b, e, a, c, :, ((a * 3 + b) * 3 + e) * 2 + c] = 1.0
    return select.reshape(432, 54)


def unrolled(count, at_most):
    return max(d for d in range(1, at_most + 1) if count % d == 0)


def shifted(values, amount):
    width = values.shape[-1]
    lane = lax.broadcasted_iota(jnp.int32, values.shape, 1)
    if amount > 0:
        return jnp.where(lane == 0, 0.0, pltpu.roll(values, 1, 1))
    return jnp.where(lane == width - 1, 0.0, pltpu.roll(values, width - 1, 1))


def denoise_kernel(
    groups,
    frames,
    group_ref,
    frame_ref,
    x_ref,
    f0_ref,
    f1_ref,
    f2_ref,
    f3_ref,
    f4_ref,
    w1_ref,
    b1_ref,
    select_ref,
    order_ref,
    wmid_ref,
    bm_ref,
    wlast_ref,
    place_ref,
    before_ref,
    base_ref,
    after_ref,
    plane_ref,
    slab_ref,
    wide_ref,
    wm_ref,
    wl_ref,
    h1_ref,
    h2_ref,
):
    window, double = x_ref.shape
    half = double // 2
    rows = window - 2 * RIM
    out_chan = wmid_ref.shape[1]
    per_row = 3 * out_chan
    group, frame_now = group_ref[0], frame_ref[0]

    bias1 = b1_ref[...]
    high = bias1.astype(BF16).astype(F32)
    middle = (bias1 - high).astype(BF16).astype(F32)
    parts = [w1_ref[...].astype(F32), high, middle, bias1 - high - middle]
    spare = 64 - sum(part.shape[0] for part in parts)
    w1 = jnp.concatenate(parts + [jnp.zeros((spare, out_chan), F32)], 0).T.astype(BF16)
    inside = (frame_now > 0, None, frame_now < frames - 1)
    for row in range(4):
        for frame in range(3):
            band = jnp.dot(w1, select_ref[row * 3 + frame], preferred_element_type=F32)
            if inside[frame] is not None:
                band = band * jnp.where(inside[frame], 1.0, 0.0)
            at = (row * 3 + frame) * out_chan
            wide_ref[at : at + out_chan, :] = band.astype(BF16)
    nothing = jnp.zeros((out_chan, out_chan), BF16)
    for e in range(3):
        for row in range(2):
            blocks = [
                wmid_ref[(a * 3 + r - row) * 3 + e] if 0 <= r - row <= 2 else nothing
                for r in range(4)
                for a in range(3)
            ]
            at = (e * 2 + row) * out_chan
            wm_ref[at : at + out_chan, :] = jnp.concatenate(blocks, 1)
    picked = jnp.dot(place_ref[...], wlast_ref[...], preferred_element_type=F32)
    eight = lax.broadcasted_iota(jnp.int32, (144, out_chan), 0) & 7
    wl_ref[...] = jnp.concatenate(
        [
            sum(
                jnp.where(eight == r - b, picked[b * 144 : (b + 1) * 144], 0.0)
                for b in range(3)
            )
            for r in range(10)
        ],
        1,
    ).astype(BF16)
    for frame, ref in enumerate((f0_ref, f1_ref, f2_ref, f3_ref, f4_ref)):
        for c in range(2):
            plane = ref[:, c * half : (c + 1) * half].astype(F32)
            for e, moved in enumerate((shifted(plane, 1), plane, shifted(plane, -1))):
                plane_ref[(frame * 2 + c) * 3 + e] = moved
    ones = jnp.ones((16, half), F32)

    def interleave(block, carry):
        rows8 = pl.ds(pl.multiple_of(block * 8, 8), 8)
        planes = [plane_ref[k, rows8, :] for k in range(30)] + [ones]
        taps = jnp.concatenate(planes, 0).astype(BF16)
        made = jnp.dot(order_ref[...], taps, preferred_element_type=F32)
        slab_ref[pl.ds(pl.multiple_of(block * 8 * SLOT, 8 * SLOT), 8 * SLOT), :] = made.astype(BF16)
        return carry

    lax.fori_loop(0, window // 8, interleave, 0, unroll=unrolled(window // 8, 6))

    def first(q, carry):
        source = pl.multiple_of((4 * q + RIM - 3) * SLOT, SLOT)
        taps = slab_ref[pl.ds(source, 6 * SLOT), :]
        made = jnp.dot(wide_ref[...], taps, preferred_element_type=F32)
        target = pl.multiple_of(4 * q * per_row, per_row)
        h1_ref[pl.ds(target, 4 * per_row), :] = jnp.maximum(made, 0.0).astype(BF16)
        return carry

    lax.fori_loop(0, (rows + 4) // 4, first, 0, unroll=unrolled((rows + 4) // 4, 11))
    edge = jnp.zeros((2 * per_row, half), BF16)

    @pl.when(group == 0)
    def _():
        h1_ref[: 2 * per_row, :] = edge

    @pl.when(group == groups - 1)
    def _():
        h1_ref[(rows + 2) * per_row :, :] = edge

    both = 2 * out_chan
    bias = jnp.broadcast_to(bm_ref[...], (128, out_chan)).T
    bias = jnp.concatenate([bias] * 2, 0)
    bias = jnp.concatenate([bias] * (half // 128), 1)

    def mid(p, carry):
        source = pl.multiple_of(2 * p * per_row, 2 * per_row)
        taps = h1_ref[pl.ds(source, 4 * per_row), :]
        made = jnp.dot(wm_ref[...], taps, preferred_element_type=F32)
        total = (
            made[both : 2 * both]
            + shifted(made[:both], 1)
            + shifted(made[2 * both :], -1)
            + bias
        )
        target = pl.multiple_of(p * both, both)
        h2_ref[pl.ds(target, both), :] = jnp.maximum(total, 0.0).astype(BF16)
        return carry

    lax.fori_loop(0, (rows + 2) // 2, mid, 0, unroll=unrolled((rows + 2) // 2, 13))
    edge2 = jnp.zeros((out_chan, half), BF16)

    @pl.when(group == 0)
    def _():
        h2_ref[:out_chan, :] = edge2

    @pl.when(group == groups - 1)
    def _():
        h2_ref[(rows + 1) * out_chan :, :] = edge2

    def last(q, carry):
        source = pl.multiple_of(8 * q * out_chan, 8 * out_chan)
        taps = h2_ref[pl.ds(source, 10 * out_chan), :]
        made = jnp.dot(wl_ref[...], taps, preferred_element_type=F32)
        total = made[48:96] + shifted(made[:48], 1) + shifted(made[96:], -1)
        at = pl.ds(pl.multiple_of(8 * q, 8), 8)
        for c in range(2):
            lanes = slice(c * half, (c + 1) * half)
            piece = lambda a: total[(a * 2 + c) * 8 : (a * 2 + c) * 8 + 8]
            after_ref[at, lanes] = piece(0).astype(BF16)
            base_ref[at, lanes] = (
                x_ref[pl.ds(pl.multiple_of(8 * q + RIM, 8), 8), lanes] + piece(1)
            )
            before_ref[at, lanes] = piece(2).astype(BF16)
        return carry

    lax.fori_loop(0, rows // 8, last, 0, unroll=unrolled(rows // 8, 8))


def denoise(x, w_first, b_first, w_mid, b_mid, w_last, frame, frames, group, groups):
    window, double = x.shape
    rows, half = window - 2 * RIM, double // 2
    out_chan = w_mid.shape[3]
    hidden = x.astype(BF16)
    near = {0: hidden}
    for by in (1, 2):
        near[-by] = lax.ppermute(hidden, "frame", [(i, i + by) for i in range(frames - by)])
        near[by] = lax.ppermute(hidden, "frame", [(i + by, i) for i in range(frames - by)])
    weights = (
        jnp.transpose(w_first, (0, 1, 2, 4, 3)).reshape(-1, out_chan),
        b_first[None],
        jnp.asarray(first_selector(w_first.shape[4]), BF16),
        jnp.asarray(interleaver(), BF16),
        w_mid.reshape(-1, out_chan, out_chan),
        b_mid[None],
        w_last.reshape(-1, out_chan),
        jnp.asarray(last_selector(), BF16),
    )
    vmem = pl.BlockSpec(memory_space=pltpu.VMEM)
    smem = pl.BlockSpec(memory_space=pltpu.SMEM)
    out = lambda dtype: jax.ShapeDtypeStruct((rows, double), dtype)
    before, base, after = pl.pallas_call(
        functools.partial(denoise_kernel, groups, frames),
        in_specs=[smem] * 2 + [vmem] * 14,
        out_specs=[vmem] * 3,
        out_shape=[out(BF16), out(F32), out(BF16)],
        compiler_params=pltpu.CompilerParams(vmem_limit_bytes=44 << 20),
        scratch_shapes=[
            pltpu.VMEM((30, window, half), F32),
            pltpu.VMEM((window * SLOT, half), BF16),
            pltpu.VMEM((12 * out_chan, 6 * SLOT), BF16),
            pltpu.VMEM((6 * out_chan, 12 * out_chan), BF16),
            pltpu.VMEM((144, 10 * out_chan), BF16),
            pltpu.VMEM(((rows + 4) * 3 * out_chan, half), BF16),
            pltpu.VMEM(((rows + 2) * out_chan, half), BF16),
        ],
        cost_estimate=pl.CostEstimate(
            flops=2 * (rows + 2) * half * 192 * 1152,
            bytes_accessed=4 * window * double * 5,
            transcendentals=0,
        ),
        name="denoise",
    )(
        group.astype(jnp.int32)[None],
        frame.astype(jnp.int32)[None],
        x,
        *[near[by] for by in (-2, -1, 0, 1, 2)],
        *weights,
    )
    upward = [(i, i + 1) for i in range(frames - 1)]
    downward = [(i + 1, i) for i in range(frames - 1)]
    above = lax.ppermute(after, "frame", upward).astype(F32)
    below = lax.ppermute(before, "frame", downward).astype(F32)
    return base + above + below


def shards(kspace, sens, mask, image, w_first, b_first, w_mid, b_mid, w_last):
    frame, group = lax.axis_index("frame"), lax.axis_index("coil")
    frames, groups = lax.axis_size("frame"), lax.axis_size("coil")
    here = group.astype(jnp.int32)[None]
    x = data_step(image[0], kspace[0], sens, mask[0], here, groups)
    return denoise(x, w_first, b_first, w_mid, b_mid, w_last, frame, frames, group, groups)[None]


def solution(mesh):
    in_specs = (
        P("frame", "coil", None, None),
        P("coil", None, None),
        P("frame", "coil", None),
        P("frame", "coil", None),
        P(),
        P(),
        P(),
        P(),
        P(),
    )
    out_specs = P("frame", "coil", None)
    return jax.shard_map(shards, mesh=mesh, in_specs=in_specs, out_specs=out_specs, check_vma=False)
```

time: 129 us -> 85.8 us (0.67)
  the two profiles are of different devices: /device:TPU:1 before, /device:TPU:23 now
where the time goes in v2:
time: 85.8 us; the launch traced here: 85.5 us
  Pallas kernels  44 us (51%)
  starting transfers between devices  20.5 us (24%)
  waiting for transfers between devices  17.4 us (20%)
  other arithmetic  2.71 us (3%)
    pallas_call x1, Pallas kernels, data_step(): pl.pallas_call(functools.partial(data_kernel, coils_at_once, 32), grid=(c...  24.7 us
    pallas_call x1, Pallas kernels, denoise(): pl.pallas_call(functools.partial(denoise_kernel, groups, frames), in_spec...  19.3 us
    ppermute x2, starting transfers between devices, denoise(): lax.ppermute(hidden, 'frame', [(i + by, i) for i in range(frames - by)])  7.03 us
    ppermute x2, starting transfers between devices, denoise(): lax.ppermute(hidden, 'frame', [(i, i + by) for i in range(frames - by)])  6.2 us
    ppermute x1, waiting for transfers between devices, denoise(): below = lax.ppermute(before, 'frame', downward).astype(F32)  5.25 us
    ppermute x1, starting transfers between devices, denoise(): above = lax.ppermute(after, 'frame', upward).astype(F32)  4.8 us
    ppermute x1, waiting for transfers between devices, data_step(): lax.ppermute(low, 'coil', shift(hop))  4.16 us
    ppermute x2, waiting for transfers between devices, denoise(): lax.ppermute(hidden, 'frame', [(i, i + by) for i in range(frames - by)])  4.02 us
  transfers between devices with their start and end apart: 8, of which 4 were waited for; matrix products, arithmetic and copies ran while one was open for 0% of the time, Pallas kernels for 0%

profile of v2, /device:TPU:23, one launch (start us, length us, event | category | flops | bytes accessed | tf_op | source)
XLA Modules:
  0.0 85.5 jit_solution(15222347790545752905)
XLA Ops:
  0.0 1.0 %bitcast_convert_fusion = bf16[128,512]{1,0:T(8,128)(2,1)S(1)} fusion(f32[1,128,512]{2,1,0:T(8,128)} %param.17), kind=kLoop, calls=%fused_computation.2 | loop fusion | flops 65536 | bytes 393216 | tf_op jit(solution)/shard_map/convert_element_type | solution.py:152
  1.0 0.3 collective-permute-start
  1.3 4.2 %collective-permute-done = bf16[128,512]{1,0:T(8,128)(2,1)S(1)} collective-permute-done((bf16[128,512]{1,0:T(8,128)(2,1)S(1)}, bf16[128,512]{1,0:T(8,128)(2,1)S(1)}, u32[]{:S(2)}, u32[]{:S(2)}) %collective-permute-start) | collective-permute-done | bytes 131104 | tf_op jit(solution)/shard_map/ppermute | solution.py:153
  5.4 0.0 copy-start.8
  5.4 0.6 copy-done.8
  6.1 0.0 copy-start.6
  6.1 0.0 copy-start.7
  6.1 0.0 copy-start
  6.1 0.0 copy-start.1
  6.1 0.0 copy-start.2
  6.1 0.0 copy-start.3
  6.1 0.0 copy-start.4
  6.1 0.0 copy-start.5
  6.1 24.7 %data_step.1 = (f32[144,512]{1,0:T(8,128)}, bf16[1,144,512]{2,1,0:T(8,128)(2,1)}) custom-call(s32[1]{0:T(128)} %bitcast.where_ref.group_ref, f32[128,512]{1,0:T(8,128)} %bitcast.17, bf16[1,128,512]{2,1,0:T(8,128)(2,1)} %bitcast.21, bf16[32,256,512]{2,1,0:T(8,128)(2,1)} %bitcast.19, bf16[32,256,512]{2,1,0:T(8,128)(2,1)} %sens_ref.1, s32[32,256]{1,0:T(8,128)} %bitcast.22, ...), custom_call_target="tpu_custom_call" | custom-call | flops 17179869184 | bytes 16777216 | tf_op jit(solution)/shard_map/data_step/pallas_call | solution.py:160
  30.8 0.2 collective-permute-start.1
  31.0 4.0 %collective-permute-done.1 = bf16[144,512]{1,0:T(8,128)(2,1)S(1)} collective-permute-done((bf16[144,512]{1,0:T(8,128)(2,1)}, bf16[144,512]{1,0:T(8,128)(2,1)S(1)}, u32[]{:S(2)}, u32[]{:S(2)}) %collective-permute-start.1) | collective-permute-done | bytes 147488 | tf_op jit(solution)/shard_map/ppermute | solution.py:202
  35.0 1.0 %fusion = (bf16[144,512]{1,0:T(8,128)(2,1)S(1)}, f32[144,512]{1,0:T(8,128)S(1)}) fusion(f32[144,512]{1,0:T(8,128)} %get-tuple-element.10, bf16[144,512]{1,0:T(8,128)(2,1)S(1)} %collective-permute-done.1), kind=kLoop, calls=%fused_computation.3 | loop fusion | flops 221184 | bytes 884736 | tf_op jit(solution)/shard_map/convert_element_type | solution.py:416
  36.0 2.2 %collective-permute-start.5 = (bf16[144,512]{1,0:T(8,128)(2,1)S(1)}, bf16[144,512]{1,0:T(8,128)(2,1)S(1)}, u32[]{:S(2)}, u32[]{:S(2)}) collective-permute-start(bf16[144,512]{1,0:T(8,128)(2,1)S(1)} %get-tuple-element.15.f2_ref), channel_id=1, source_target_pairs={{4,0},{6,2},{8,4},{10,6},{12,8},{14,10},{16,12},{18,14},{20,16},{2... | collective-permute-start | bytes 442376 | tf_op jit(solution)/shard_map/ppermute | solution.py:420
  38.2 4.9 %collective-permute-start.4 = (bf16[144,512]{1,0:T(8,128)(2,1)S(1)}, bf16[144,512]{1,0:T(8,128)(2,1)S(1)}, u32[]{:S(2)}, u32[]{:S(2)}) collective-permute-start(bf16[144,512]{1,0:T(8,128)(2,1)S(1)} %get-tuple-element.15.f2_ref), channel_id=1, source_target_pairs={{2,0},{4,2},{6,4},{8,6},{10,8},{12,10},{14,12},{16,14},{18,16},{20... | collective-permute-start | bytes 442376 | tf_op jit(solution)/shard_map/ppermute | solution.py:420
  43.1 3.9 %collective-permute-start.3 = (bf16[144,512]{1,0:T(8,128)(2,1)S(1)}, bf16[144,512]{1,0:T(8,128)(2,1)S(1)}, u32[]{:S(2)}, u32[]{:S(2)}) collective-permute-start(bf16[144,512]{1,0:T(8,128)(2,1)S(1)} %get-tuple-element.15.f2_ref), channel_id=1, source_target_pairs={{0,2},{2,4},{4,6},{6,8},{8,10},{10,12},{12,14},{14,16},{16,18},{18... | collective-permute-start | bytes 442376 | tf_op jit(solution)/shard_map/ppermute | solution.py:419
  47.0 2.3 %collective-permute-start.2 = (bf16[144,512]{1,0:T(8,128)(2,1)S(1)}, bf16[144,512]{1,0:T(8,128)(2,1)S(1)}, u32[]{:S(2)}, u32[]{:S(2)}) collective-permute-start(bf16[144,512]{1,0:T(8,128)(2,1)S(1)} %get-tuple-element.15.f2_ref), channel_id=1, source_target_pairs={{0,4},{2,6},{4,8},{6,10},{8,12},{10,14},{12,16},{14,18},{16,20},{1... | collective-permute-start | bytes 442376 | tf_op jit(solution)/shard_map/ppermute | solution.py:419
  49.3 0.0 copy-done.6
  49.3 0.0 copy-done.7
  49.4 0.0 collective-permute-done.5.f4_ref
  49.4 0.0 collective-permute-done.4.f3_ref
  49.4 0.0 collective-permute-done.3.f1_ref
  49.4 4.0 %collective-permute-done.2.f0_ref = bf16[144,512]{1,0:T(8,128)(2,1)S(1)} collective-permute-done((bf16[144,512]{1,0:T(8,128)(2,1)S(1)}, bf16[144,512]{1,0:T(8,128)(2,1)S(1)}, u32[]{:S(2)}, u32[]{:S(2)}) %collective-permute-start.2) | collective-permute-done | bytes 147488 | tf_op jit(solution)/shard_map/ppermute | solution.py:419
  53.4 0.0 copy-done
  53.4 0.0 copy-done.1
  53.4 0.0 copy-done.2
  53.4 0.0 copy-done.3
  53.4 0.0 copy-done.4
  53.4 0.0 copy-done.5
  53.4 19.3 %denoise.1 = (bf16[128,512]{1,0:T(8,128)(2,1)S(1)}, f32[128,512]{1,0:T(8,128)S(1)}, bf16[128,512]{1,0:T(8,128)(2,1)S(1)}) custom-call(s32[1]{0:T(128)} %bitcast.where_ref.group_ref, s32[1]{0:T(128)} %bitcast.1.frame_ref, f32[144,512]{1,0:T(8,128)S(1)} %get-tuple-element.16.x_ref, bf16[144,512]{1,0:T(8,128)(2,1)S(1)} %collective-permute-done.2.f0_ref, ...), custom_call_target="tpu_custom_call" | custom-call | flops 14722007040 | bytes 1474560 | tf_op jit(solution)/shard_map/denoise/pallas_call | solution.py:434
  72.7 4.8 %collective-permute-start.6 = (bf16[128,512]{1,0:T(8,128)(2,1)S(1)}, bf16[128,512]{1,0:T(8,128)(2,1)S(1)}, u32[]{:S(2)}, u32[]{:S(2)}) collective-permute-start(bf16[128,512]{1,0:T(8,128)(2,1)S(1)} %get-tuple-element.13), channel_id=1, source_target_pairs={{0,2},{2,4},{4,6},{6,8},{8,10},{10,12},{12,14},{14,16},{16,18},{18... | collective-permute-start | bytes 393224 | tf_op jit(solution)/shard_map/ppermute | solution.py:464
  77.5 1.9 %collective-permute-start.7 = (bf16[128,512]{1,0:T(8,128)(2,1)S(1)}, bf16[128,512]{1,0:T(8,128)(2,1)S(1)}, u32[]{:S(2)}, u32[]{:S(2)}) collective-permute-start(bf16[128,512]{1,0:T(8,128)(2,1)S(1)} %get-tuple-element.14), channel_id=1, source_target_pairs={{2,0},{4,2},{6,4},{8,6},{10,8},{12,10},{14,12},{16,14},{18,16},{20... | collective-permute-start | bytes 393224 | tf_op jit(solution)/shard_map/ppermute | solution.py:465
  79.5 0.0 collective-permute-done.6
  79.5 5.2 %collective-permute-done.7 = bf16[128,512]{1,0:T(8,128)(2,1)S(1)} collective-permute-done((bf16[128,512]{1,0:T(8,128)(2,1)S(1)}, bf16[128,512]{1,0:T(8,128)(2,1)S(1)}, u32[]{:S(2)}, u32[]{:S(2)}) %collective-permute-start.7) | collective-permute-done | bytes 131104 | tf_op jit(solution)/shard_map/ppermute | solution.py:465
  84.7 0.7 add_bitcast_fusion
  (2 shorter events, 0.1 us)
Async XLA Ops:
  1.0 4.4 %collective-permute-start = (bf16[128,512]{1,0:T(8,128)(2,1)S(1)}, bf16[128,512]{1,0:T(8,128)(2,1)S(1)}, u32[]{:S(2)}, u32[]{:S(2)}) collective-permute-start(bf16[128,512]{1,0:T(8,128)(2,1)S(1)} %bitcast_convert_fusion), channel_id=1, source_target_pairs={{0,1},{1,0},{2,3},{3,2},{4,5},{5,4},{6,7},{7,6},{8,9},{9,8},{10,11... | collective-permute-start | bytes 393224 | tf_op jit(solution)/shard_map/ppermute | solution.py:153
  5.4 0.6 copy-start.8
  6.1 43.2 %copy-start.6 = (bf16[3,3,3,64,2]{3,4,2,1,0:T(2,128)(2,1)S(1)}, bf16[3,3,3,64,2]{3,4,2,1,0:T(2,128)(2,1)}, u32[]{:S(2)}) copy-start(bf16[3,3,3,64,2]{3,4,2,1,0:T(2,128)(2,1)} %param.18) | copy-start | bytes 20740
  6.1 43.2 %copy-start.7 = (bf16[3,3,3,2,64]{4,3,2,1,0:T(2,128)(2,1)S(1)}, bf16[3,3,3,2,64]{4,3,2,1,0:T(2,128)(2,1)}, u32[]{:S(2)}) copy-start(bf16[3,3,3,2,64]{4,3,2,1,0:T(2,128)(2,1)} %param.22) | copy-start | bytes 20740
  6.1 47.3 %copy-start = (bf16[3,3,3,64,64]{4,3,2,1,0:T(8,128)(2,1)S(1)}, bf16[3,3,3,64,64]{4,3,2,1,0:T(8,128)(2,1)}, u32[]{:S(2)}) copy-start(bf16[3,3,3,64,64]{4,3,2,1,0:T(8,128)(2,1)} %param.20) | copy-start | bytes 663556
  6.1 47.3 %copy-start.1 = (f32[64]{0:T(128)S(1)}, f32[64]{0:T(128)}, u32[]{:S(2)}) copy-start(f32[64]{0:T(128)} %param.19) | copy-start | bytes 772
  6.1 47.3 %copy-start.2 = (f32[64]{0:T(128)S(1)}, f32[64]{0:T(128)}, u32[]{:S(2)}) copy-start(f32[64]{0:T(128)} %param.21) | copy-start | bytes 772
  6.1 47.3 %copy-start.3 = (bf16[12,64,192]{2,1,0:T(8,128)(2,1)S(1)}, bf16[12,64,192]{2,1,0:T(8,128)(2,1)}, u32[]{:S(2)}) copy-start(bf16[12,64,192]{2,1,0:T(8,128)(2,1)} %constant.17.clone.select_ref) | copy-start | bytes 884740
  6.1 47.3 %copy-start.4 = (bf16[256,256]{1,0:T(8,128)(2,1)S(1)}, bf16[256,256]{1,0:T(8,128)(2,1)}, u32[]{:S(2)}) copy-start(bf16[256,256]{1,0:T(8,128)(2,1)} %constant.18.clone.order_ref) | copy-start | bytes 393220
  6.1 47.3 %copy-start.5 = (bf16[432,54]{1,0:T(8,128)(2,1)S(1)}, bf16[432,54]{1,0:T(8,128)(2,1)}, u32[]{:S(2)}) copy-start(bf16[432,54]{1,0:T(8,128)(2,1)} %constant.19.clone.place_ref) | copy-start | bytes 139972
  30.8 4.2 %collective-permute-start.1 = (bf16[144,512]{1,0:T(8,128)(2,1)}, bf16[144,512]{1,0:T(8,128)(2,1)S(1)}, u32[]{:S(2)}, u32[]{:S(2)}) collective-permute-start(bf16[144,512]{1,0:T(8,128)(2,1)} %bitcast.20), channel_id=1, source_target_pairs={{0,1},{1,0},{2,3},{3,2},{4,5},{5,4},{6,7},{7,6},{8,9},{9,8},{10,11... | collective-permute-start | bytes 442376 | tf_op jit(solution)/shard_map/ppermute | solution.py:202
  36.0 13.3 %collective-permute-start.5 = (bf16[144,512]{1,0:T(8,128)(2,1)S(1)}, bf16[144,512]{1,0:T(8,128)(2,1)S(1)}, u32[]{:S(2)}, u32[]{:S(2)}) collective-permute-start(bf16[144,512]{1,0:T(8,128)(2,1)S(1)} %get-tuple-element.15.f2_ref), channel_id=1, source_target_pairs={{4,0},{6,2},{8,4},{10,6},{12,8},{14,10},{16,12},{18,14},{20,16},{2... | collective-permute-start | bytes 442376 | tf_op jit(solution)/shard_map/ppermute | solution.py:420
  38.2 11.2 %collective-permute-start.4 = (bf16[144,512]{1,0:T(8,128)(2,1)S(1)}, bf16[144,512]{1,0:T(8,128)(2,1)S(1)}, u32[]{:S(2)}, u32[]{:S(2)}) collective-permute-start(bf16[144,512]{1,0:T(8,128)(2,1)S(1)} %get-tuple-element.15.f2_ref), channel_id=1, source_target_pairs={{2,0},{4,2},{6,4},{8,6},{10,8},{12,10},{14,12},{16,14},{18,16},{20... | collective-permute-start | bytes 442376 | tf_op jit(solution)/shard_map/ppermute | solution.py:420
  43.1 6.3 %collective-permute-start.3 = (bf16[144,512]{1,0:T(8,128)(2,1)S(1)}, bf16[144,512]{1,0:T(8,128)(2,1)S(1)}, u32[]{:S(2)}, u32[]{:S(2)}) collective-permute-start(bf16[144,512]{1,0:T(8,128)(2,1)S(1)} %get-tuple-element.15.f2_ref), channel_id=1, source_target_pairs={{0,2},{2,4},{4,6},{6,8},{8,10},{10,12},{12,14},{14,16},{16,18},{18... | collective-permute-start | bytes 442376 | tf_op jit(solution)/shard_map/ppermute | solution.py:419
  47.0 6.4 %collective-permute-start.2 = (bf16[144,512]{1,0:T(8,128)(2,1)S(1)}, bf16[144,512]{1,0:T(8,128)(2,1)S(1)}, u32[]{:S(2)}, u32[]{:S(2)}) collective-permute-start(bf16[144,512]{1,0:T(8,128)(2,1)S(1)} %get-tuple-element.15.f2_ref), channel_id=1, source_target_pairs={{0,4},{2,6},{4,8},{6,10},{8,12},{10,14},{12,16},{14,18},{16,20},{1... | collective-permute-start | bytes 442376 | tf_op jit(solution)/shard_map/ppermute | solution.py:419
  72.7 6.7 %collective-permute-start.6 = (bf16[128,512]{1,0:T(8,128)(2,1)S(1)}, bf16[128,512]{1,0:T(8,128)(2,1)S(1)}, u32[]{:S(2)}, u32[]{:S(2)}) collective-permute-start(bf16[128,512]{1,0:T(8,128)(2,1)S(1)} %get-tuple-element.13), channel_id=1, source_target_pairs={{0,2},{2,4},{4,6},{6,8},{8,10},{10,12},{12,14},{14,16},{16,18},{18... | collective-permute-start | bytes 393224 | tf_op jit(solution)/shard_map/ppermute | solution.py:464
  77.5 7.2 %collective-permute-start.7 = (bf16[128,512]{1,0:T(8,128)(2,1)S(1)}, bf16[128,512]{1,0:T(8,128)(2,1)S(1)}, u32[]{:S(2)}, u32[]{:S(2)}) collective-permute-start(bf16[128,512]{1,0:T(8,128)(2,1)S(1)} %get-tuple-element.14), channel_id=1, source_target_pairs={{2,0},{4,2},{6,4},{8,6},{10,8},{12,10},{14,12},{16,14},{18,16},{20... | collective-permute-start | bytes 393224 | tf_op jit(solution)/shard_map/ppermute | solution.py:465

commit v3 on v2

--- a/solution.py
+++ b/solution.py
@@ -22,7 +22,7 @@
     angles = (indices[:, None] * indices[None, :] % order).astype(np.float32)
     angles = angles * np.float32(2.0 * math.pi / order)
     factor = np.float32(1.0 / math.sqrt(order))
-    return jnp.asarray(np.stack([np.cos(angles) * factor, -np.sin(angles) * factor]), BF16)
+    return np.stack([np.cos(angles) * factor, -np.sin(angles) * factor])
 
 
 def put_table(ref, top_left, top_right, low_left, low_right):
@@ -31,6 +31,21 @@
     ref[:half, half:] = top_right
     ref[half:, :half] = low_left
     ref[half:, half:] = low_right
+
+
+def halved(parts):
+    short = parts.shape[1] // 2
+    tables = []
+    for real, imag in ((parts[0], parts[1]), (parts[0], -parts[1])):
+        for odd in range(2):
+            if len(tables) < 2:
+                re, im = real[:short, odd::2], imag[:short, odd::2]
+            else:
+                re, im = real[odd::2, :short], imag[odd::2, :short]
+            tables.append(
+                np.concatenate([np.concatenate([re, -im], 1), np.concatenate([im, re], 1)], 0)
+            )
+    return np.stack(tables)
 
 
 def data_kernel(
@@ -43,104 +58,144 @@
     sens_ref,
     mask_ref,
     cols_ref,
-    lines_ref,
+    rows_ref,
     own_ref,
     send_ref,
     full_ref,
     acc_ref,
+    natural_ref,
+    smooth_ref,
     coil_ref,
     spec_ref,
     esti_ref,
     miss_ref,
-    back_ref,
+    fold_ref,
     bimg_ref,
     col_ahead_ref,
     col_behind_ref,
-    row_ahead_ref,
-    row_behind_ref,
 ):
     groups = others_ref.shape[0] + 1
     own_rows = image_ref.shape[0]
     n_rows, double = full_ref.shape
-    half = double // 2
+    half, short = double // 2, n_rows // 2
+    lanes = double // 128
     me = where_ref[0]
     step = pl.program_id(0)
 
     @pl.when(step == 0)
     def _():
-        for ref, ahead_ref, behind_ref in (
-            (cols_ref, col_ahead_ref, col_behind_ref),
-            (lines_ref, row_behind_ref, row_ahead_ref),
-        ):
-            real, imag = ref[0], ref[1]
-            put_table(ahead_ref, real, imag, -imag, real)
-            put_table(behind_ref, real, -imag, imag, real)
+        real, imag = cols_ref[0], cols_ref[1]
+        put_table(col_ahead_ref, real, imag, -imag, real)
+        put_table(col_behind_ref, real, -imag, imag, real)
         acc_ref[...] = jnp.zeros_like(acc_ref)
-        mine = pl.multiple_of(me * own_rows, RIM)
-        acc_ref[pl.ds(pl.multiple_of(mine + RIM, RIM), own_rows), :] = image_ref[...]
-        full_ref[pl.ds(mine, own_rows), :] = image_ref[...].astype(BF16).astype(F32)
-        for hop in range(1, groups):
-            theirs = pl.multiple_of(lax.rem(me + groups - hop, groups) * own_rows, RIM)
-            full_ref[pl.ds(theirs, own_rows), :] = others_ref[hop - 1].astype(F32)
+        natural_ref[...] = jnp.zeros_like(natural_ref)
+        for j in range(lanes):
+            part = slice(j * 128, (j + 1) * 128)
+            mine = pl.multiple_of(me * own_rows + RIM, RIM)
+            natural_ref[j, pl.ds(mine, own_rows), :] = image_ref[:, part].astype(BF16).astype(F32)
+            for hop in range(1, groups):
+                theirs = lax.rem(me + groups - hop, groups) * own_rows + RIM
+                natural_ref[j, pl.ds(pl.multiple_of(theirs, RIM), own_rows), :] = others_ref[
+                    hop - 1, :, part
+                ].astype(F32)
+            for odd in range(2):
+                full_ref[odd * short : (odd + 1) * short, part] = natural_ref[
+                    j, pl.ds(RIM + odd, short, stride=2), :
+                ]
 
     for coil in range(coils_at_once):
-        for start in range(0, n_rows, chunk):
-            rows = slice(start, start + chunk)
-            sens_re = sens_ref[coil, rows, :half].astype(F32)
-            sens_im = sens_ref[coil, rows, half:].astype(F32)
+        for j in range(lanes):
+            smooth_ref[coil, j] = sens_ref[coil, :, j * 128 : (j + 1) * 128].astype(F32)
+
+    def maps(coil, odd, start):
+        at = pl.ds(2 * start + odd, chunk, stride=2)
+        pieces = [smooth_ref[coil, j, at, :] for j in range(lanes)]
+        return (
+            jnp.concatenate(pieces[: lanes // 2], 1),
+            jnp.concatenate(pieces[lanes // 2 :], 1),
+        )
+
+    for odd in range(2):
+        for start in range(0, short, chunk):
+            place = odd * short + start
+            rows = slice(place, place + chunk)
             x_re, x_im = full_ref[rows, :half], full_ref[rows, half:]
-            out = slice(coil * n_rows + start, coil * n_rows + start + chunk)
-            coil_ref[out, :half] = (sens_re * x_re - sens_im * x_im).astype(BF16)
-            coil_ref[out, half:] = (sens_re * x_im + sens_im * x_re).astype(BF16)
+            for coil in range(coils_at_once):
+                sens_re, sens_im = maps(coil, odd, start)
+                out = slice(coil * n_rows + place, coil * n_rows + place + chunk)
+                coil_ref[out, :half] = (sens_re * x_re - sens_im * x_im).astype(BF16)
+                coil_ref[out, half:] = (sens_re * x_im + sens_im * x_re).astype(BF16)
     spec_ref[...] = jnp.dot(
         coil_ref[...], col_ahead_ref[...], preferred_element_type=F32
     ).astype(BF16)
     for coil in range(coils_at_once):
-        block = slice(coil * n_rows, (coil + 1) * n_rows)
-        stacked = jnp.concatenate([spec_ref[block, :half], spec_ref[block, half:]], 0)
-        esti_ref[coil] = jnp.dot(row_ahead_ref[...], stacked, preferred_element_type=F32)
+        for odd in range(2):
+            at = coil * n_rows + odd * short
+            stacked = jnp.concatenate(
+                [spec_ref[at : at + short, :half], spec_ref[at : at + short, half:]], 0
+            )
+            esti_ref[coil, odd] = jnp.dot(rows_ref[odd], stacked, preferred_element_type=F32)
     for coil in range(coils_at_once):
         line = mask_ref[pl.ds(step * coils_at_once + coil, 1), :].astype(F32)
         sampled = jnp.broadcast_to(line, (128, n_rows)).T
-        for start in range(0, n_rows, chunk):
-            rows = slice(start, start + chunk)
-            out = slice(coil * n_rows + start, coil * n_rows + start + chunk)
-            line = jnp.concatenate([sampled[rows]] * (half // 128), 1)
-            miss_ref[out, :half] = (
-                line * (esti_ref[coil, rows, :] - kspace_ref[coil, rows, :half].astype(F32))
-            ).astype(BF16)
-            lower = slice(n_rows + start, n_rows + start + chunk)
-            miss_ref[out, half:] = (
-                line * (esti_ref[coil, lower, :] - kspace_ref[coil, rows, half:].astype(F32))
-            ).astype(BF16)
-    back_ref[...] = jnp.dot(
-        miss_ref[...], col_behind_ref[...], preferred_element_type=F32
-    ).astype(BF16)
+        for start in range(0, short, chunk):
+            for c in range(2):
+                rows = slice(c * short + start, c * short + start + chunk)
+                even, uneven = esti_ref[coil, 0, rows, :], esti_ref[coil, 1, rows, :]
+                for upper, estimate in enumerate((even + uneven, even - uneven)):
+                    at = slice(upper * short + start, upper * short + start + chunk)
+                    taken = jnp.concatenate([sampled[at]] * (half // 128), 1)
+                    part = slice(c * half, (c + 1) * half)
+                    out = slice(
+                        coil * n_rows + upper * short + start,
+                        coil * n_rows + upper * short + start + chunk,
+                    )
+                    miss_ref[out, part] = (
+                        taken * (estimate - kspace_ref[coil, at, part].astype(F32))
+                    ).astype(BF16)
     for coil in range(coils_at_once):
-        block = slice(coil * n_rows, (coil + 1) * n_rows)
-        stacked = jnp.concatenate([back_ref[block, :half], back_ref[block, half:]], 0)
-        bimg_ref[coil] = jnp.dot(row_behind_ref[...], stacked, preferred_element_type=F32)
-    for start in range(0, n_rows, chunk):
-        rows = slice(start, start + chunk)
-        place = slice(RIM + start, RIM + start + chunk)
-        lower = slice(n_rows + start, n_rows + start + chunk)
-        total_re, total_im = acc_ref[place, :half], acc_ref[place, half:]
-        for coil in range(coils_at_once):
-            sens_re = sens_ref[coil, rows, :half].astype(F32) * step_size
-            sens_im = sens_ref[coil, rows, half:].astype(F32) * step_size
-            back_re, back_im = bimg_ref[coil, rows, :], bimg_ref[coil, lower, :]
-            total_re = total_re - (sens_re * back_re + sens_im * back_im)
-            total_im = total_im - (sens_re * back_im - sens_im * back_re)
-        acc_ref[place, :half] = total_re
-        acc_ref[place, half:] = total_im
+        at = coil * n_rows
+        lines = jnp.dot(
+            miss_ref[at : at + n_rows, :], col_behind_ref[...], preferred_element_type=F32
+        )
+        for odd, folded in enumerate(
+            (lines[:short] + lines[short:], lines[:short] - lines[short:])
+        ):
+            fold_ref[coil, odd, :short, :] = folded[:, :half].astype(BF16)
+            fold_ref[coil, odd, short:, :] = folded[:, half:].astype(BF16)
+    for coil in range(coils_at_once):
+        for odd in range(2):
+            bimg_ref[coil, odd] = jnp.dot(
+                rows_ref[2 + odd], fold_ref[coil, odd], preferred_element_type=F32
+            )
+    for odd in range(2):
+        for start in range(0, short, chunk):
+            place = slice(odd * short + start, odd * short + start + chunk)
+            rows, lower = slice(start, start + chunk), slice(short + start, short + start + chunk)
+            total_re, total_im = acc_ref[place, :half], acc_ref[place, half:]
+            for coil in range(coils_at_once):
+                sens_re, sens_im = maps(coil, odd, start)
+                back_re, back_im = bimg_ref[coil, odd, rows, :], bimg_ref[coil, odd, lower, :]
+                total_re = total_re + (sens_re * back_re + sens_im * back_im)
+                total_im = total_im + (sens_re * back_im - sens_im * back_re)
+            acc_ref[place, :half] = total_re
+            acc_ref[place, half:] = total_im
 
     @pl.when(step == pl.num_programs(0) - 1)
     def _():
         window = own_rows + 2 * RIM
-        own_ref[...] = acc_ref[pl.ds(pl.multiple_of(me * own_rows, RIM), window), :]
-        for hop in range(1, groups):
-            theirs = pl.multiple_of(lax.rem(me + hop, groups) * own_rows, RIM)
-            send_ref[hop - 1] = acc_ref[pl.ds(theirs, window), :].astype(BF16)
+        for j in range(lanes):
+            part = slice(j * 128, (j + 1) * 128)
+            for odd in range(2):
+                natural_ref[j, pl.ds(RIM + odd, short, stride=2), :] = (
+                    acc_ref[odd * short : (odd + 1) * short, part] * -step_size
+                )
+            mine = pl.ds(pl.multiple_of(me * own_rows + RIM, RIM), own_rows)
+            natural_ref[j, mine, :] += image_ref[:, part]
+            own_ref[:, part] = natural_ref[j, pl.ds(pl.multiple_of(me * own_rows, RIM), window), :]
+            for hop in range(1, groups):
+                theirs = pl.multiple_of(lax.rem(me + hop, groups) * own_rows, RIM)
+                send_ref[hop - 1, :, part] = natural_ref[j, pl.ds(theirs, window), :].astype(BF16)
 
 
 def data_step(image, kspace, sens, mask, here, groups):
@@ -151,9 +206,10 @@
     shift = lambda hop: [(i, (i + hop) % groups) for i in range(groups)]
     low = image.astype(BF16)
     others = jnp.stack([lax.ppermute(low, "coil", shift(hop)) for hop in range(1, groups)])
-    cols, lines = dft_parts(half), dft_parts(n_rows)
+    cols = jnp.asarray(dft_parts(half), BF16)
+    lines = jnp.asarray(halved(dft_parts(n_rows)), BF16)
     window = own_rows + 2 * RIM
-    whole = lambda a: pl.BlockSpec(a.shape, lambda i: (0,) * a.ndim)
+    vmem = pl.BlockSpec(memory_space=pltpu.VMEM)
     per_coil = lambda a: pl.BlockSpec(
         (coils_at_once,) + a.shape[1:], lambda i: (i,) + (0,) * (a.ndim - 1)
     )
@@ -162,13 +218,13 @@
         grid=(coils // coils_at_once,),
         in_specs=[
             pl.BlockSpec(memory_space=pltpu.SMEM),
-            whole(image),
-            whole(others),
+            vmem,
+            vmem,
             per_coil(kspace),
             per_coil(sens),
-            whole(mask),
-            whole(cols),
-            whole(lines),
+            vmem,
+            vmem,
+            vmem,
         ],
         out_specs=[
             pl.BlockSpec((window, double), lambda i: (0, 0)),
@@ -180,16 +236,17 @@
         ],
         scratch_shapes=[
             pltpu.VMEM((n_rows, double), F32),
-            pltpu.VMEM((n_rows + 2 * RIM, double), F32),
+            pltpu.VMEM((n_rows, double), F32),
+            pltpu.VMEM((double // 128, n_rows + 2 * RIM, 128), F32),
+            pltpu.VMEM((coils_at_once, double // 128, n_rows, 128), F32),
             pltpu.VMEM((coils_at_once * n_rows, double), BF16),
             pltpu.VMEM((coils_at_once * n_rows, double), BF16),
-            pltpu.VMEM((coils_at_once, 2 * n_rows, half), F32),
+            pltpu.VMEM((coils_at_once, 2, n_rows, half), F32),
             pltpu.VMEM((coils_at_once * n_rows, double), BF16),
-            pltpu.VMEM((coils_at_once * n_rows, double), BF16),
-            pltpu.VMEM((coils_at_once, 2 * n_rows, half), F32),
+            pltpu.VMEM((coils_at_once, 2, n_rows, half), BF16),
+            pltpu.VMEM((coils_at_once, 2, n_rows, half), F32),
         ]
-        + [pltpu.VMEM((double, double), BF16)] * 2
-        + [pltpu.VMEM((2 * n_rows, 2 * n_rows), BF16)] * 2,
+        + [pltpu.VMEM((double, double), BF16)] * 2,
         compiler_params=pltpu.CompilerParams(vmem_limit_bytes=57 << 20),
         cost_estimate=pl.CostEstimate(
             flops=32 * coils * n_rows * n_rows * half,
@@ -257,11 +314,12 @@
     group_ref,
     frame_ref,
     x_ref,
-    f0_ref,
-    f1_ref,
-    f2_ref,
-    f3_ref,
-    f4_ref,
+    hidden_ref,
+    partner_ref,
+    first_pair_ref,
+    other_pair_ref,
+    first_handed_ref,
+    other_handed_ref,
     w1_ref,
     b1_ref,
     select_ref,
@@ -270,9 +328,9 @@
     bm_ref,
     wlast_ref,
     place_ref,
-    before_ref,
+    inner_ref,
     base_ref,
-    after_ref,
+    outer_ref,
     plane_ref,
     slab_ref,
     wide_ref,
@@ -324,11 +382,24 @@
         ],
         1,
     ).astype(BF16)
-    for frame, ref in enumerate((f0_ref, f1_ref, f2_ref, f3_ref, f4_ref)):
+    odd_frame = frame_now & 1
+    odd_pair = (frame_now >> 1) & 1
+    handed_on = jnp.where(
+        odd_frame == odd_pair,
+        other_handed_ref[...].astype(F32),
+        first_handed_ref[...].astype(F32),
+    )
+    for slot, frame_values in (
+        (4 - 4 * odd_pair, first_pair_ref[...].astype(F32)),
+        (3 - 2 * odd_frame, partner_ref[...].astype(F32)),
+        (2, hidden_ref[...].astype(F32)),
+        (1 + 2 * odd_frame, handed_on),
+        (4 * odd_pair, other_pair_ref[...].astype(F32)),
+    ):
         for c in range(2):
-            plane = ref[:, c * half : (c + 1) * half].astype(F32)
+            plane = frame_values[:, c * half : (c + 1) * half]
             for e, moved in enumerate((shifted(plane, 1), plane, shifted(plane, -1))):
-                plane_ref[(frame * 2 + c) * 3 + e] = moved
+                plane_ref[(slot * 2 + c) * 3 + e] = moved
     ones = jnp.ones((16, half), F32)
 
     def interleave(block, carry):
@@ -399,14 +470,20 @@
         for c in range(2):
             lanes = slice(c * half, (c + 1) * half)
             piece = lambda a: total[(a * 2 + c) * 8 : (a * 2 + c) * 8 + 8]
-            after_ref[at, lanes] = piece(0).astype(BF16)
+            to_after, to_before = piece(0), piece(2)
+            inner_ref[at, lanes] = jnp.where(odd_frame == 0, to_after, to_before).astype(BF16)
+            outer_ref[at, lanes] = jnp.where(odd_frame == 0, to_before, to_after).astype(BF16)
             base_ref[at, lanes] = (
                 x_ref[pl.ds(pl.multiple_of(8 * q + RIM, 8), 8), lanes] + piece(1)
             )
-            before_ref[at, lanes] = piece(2).astype(BF16)
         return carry
 
     lax.fori_loop(0, rows // 8, last, 0, unroll=unrolled(rows // 8, 8))
+
+
+def swaps(count, size, odd):
+    ups = [(i, i + size) for i in range(count - size) if (i // size) % 2 == odd]
+    return ups + [(j, i) for i, j in ups]
 
 
 def denoise(x, w_first, b_first, w_mid, b_mid, w_last, frame, frames, group, groups):
@@ -414,10 +491,13 @@
     rows, half = window - 2 * RIM, double // 2
     out_chan = w_mid.shape[3]
     hidden = x.astype(BF16)
-    near = {0: hidden}
-    for by in (1, 2):
-        near[-by] = lax.ppermute(hidden, "frame", [(i, i + by) for i in range(frames - by)])
-        near[by] = lax.ppermute(hidden, "frame", [(i + by, i) for i in range(frames - by)])
+    within = swaps(frames, 1, 0)
+    partner = lax.ppermute(hidden, "frame", within)
+    first_pair = lax.ppermute(hidden, "frame", swaps(frames, 2, 0))
+    other_pair = lax.ppermute(hidden, "frame", swaps(frames, 2, 1))
+    first_handed = lax.ppermute(first_pair, "frame", within)
+    other_handed = lax.ppermute(other_pair, "frame", within)
+    near = (hidden, partner, first_pair, other_pair, first_handed, other_handed)
     weights = (
         jnp.transpose(w_first, (0, 1, 2, 4, 3)).reshape(-1, out_chan),
         b_first[None],
@@ -431,9 +511,9 @@
     vmem = pl.BlockSpec(memory_space=pltpu.VMEM)
     smem = pl.BlockSpec(memory_space=pltpu.SMEM)
     out = lambda dtype: jax.ShapeDtypeStruct((rows, double), dtype)
-    before, base, after = pl.pallas_call(
+    inner, base, outer = pl.pallas_call(
         functools.partial(denoise_kernel, groups, frames),
-        in_specs=[smem] * 2 + [vmem] * 14,
+        in_specs=[smem] * 2 + [vmem] * 15,
         out_specs=[vmem] * 3,
         out_shape=[out(BF16), out(F32), out(BF16)],
         compiler_params=pltpu.CompilerParams(vmem_limit_bytes=44 << 20),
@@ -456,14 +536,13 @@
         group.astype(jnp.int32)[None],
         frame.astype(jnp.int32)[None],
         x,
-        *[near[by] for by in (-2, -1, 0, 1, 2)],
+        *near,
         *weights,
     )
-    upward = [(i, i + 1) for i in range(frames - 1)]
-    downward = [(i + 1, i) for i in range(frames - 1)]
-    above = lax.ppermute(after, "frame", upward).astype(F32)
-    below = lax.ppermute(before, "frame", downward).astype(F32)
-    return base + above + below
+    across = swaps(frames, 1, 1)
+    outer = lax.ppermute(outer, "frame", across).astype(F32)
+    inner = lax.ppermute(inner, "frame", within).astype(F32)
+    return base + inner + outer
 
 
 def shards(kspace, sens, mask, image, w_first, b_first, w_mid, b_mid, w_last):

time: 85.8 us -> 74.1 us (0.86)
  the two profiles are of different devices: /device:TPU:23 before, /device:TPU:29 now
where the time goes in v3:
time: 74.1 us; the launch traced here: 73.9 us
  Pallas kernels  40.4 us (55%)
  waiting for transfers between devices  15.6 us (21%)
  starting transfers between devices  14.3 us (19%)
  other arithmetic  2.71 us (4%)
    pallas_call x1, Pallas kernels, data_step(): pl.pallas_call(functools.partial(data_kernel, coils_at_once, 32), grid=(c...  21.1 us
    pallas_call x1, Pallas kernels, denoise(): pl.pallas_call(functools.partial(denoise_kernel, groups, frames), in_spec...  19.3 us
    ppermute x1, waiting for transfers between devices, denoise(): outer = lax.ppermute(outer, 'frame', across).astype(F32)  5.75 us
    ppermute x1, waiting for transfers between devices, data_step(): lax.ppermute(low, 'coil', shift(hop))  4.16 us
    ppermute x1, waiting for transfers between devices, data_step(): own = own + lax.ppermute(send[hop - 1], 'coil', shift(hop)).astype(F32)  4 us
    ppermute x1, starting transfers between devices, denoise(): other_handed = lax.ppermute(other_pair, 'frame', within)  3.82 us
    ppermute x1, starting transfers between devices, denoise(): other_pair = lax.ppermute(hidden, 'frame', swaps(frames, 2, 1))  3.01 us
    ppermute x1, starting transfers between devices, denoise(): partner = lax.ppermute(hidden, 'frame', within)  3.01 us
  transfers between devices with their start and end apart: 9, of which 5 were waited for; matrix products, arithmetic and copies ran while one was open for 0% of the time, Pallas kernels for 0%

profile of v3, /device:TPU:29, one launch (start us, length us, event | category | flops | bytes accessed | tf_op | source)
XLA Modules:
  0.0 73.9 jit_solution(17212459667159603093)
XLA Ops:
  0.0 1.0 %bitcast_convert_fusion = bf16[128,512]{1,0:T(8,128)(2,1)S(1)} fusion(f32[1,128,512]{2,1,0:T(8,128)} %param.17), kind=kLoop, calls=%fused_computation.2 | loop fusion | flops 65536 | bytes 393216 | tf_op jit(solution)/shard_map/convert_element_type | solution.py:207
  1.0 0.3 collective-permute-start
  1.3 4.2 %collective-permute-done = bf16[128,512]{1,0:T(8,128)(2,1)S(1)} collective-permute-done((bf16[128,512]{1,0:T(8,128)(2,1)S(1)}, bf16[128,512]{1,0:T(8,128)(2,1)S(1)}, u32[]{:S(2)}, u32[]{:S(2)}) %collective-permute-start) | collective-permute-done | bytes 131104 | tf_op jit(solution)/shard_map/ppermute | solution.py:208
  5.4 0.0 copy-start.8
  5.4 0.6 copy-done.8
  6.1 0.0 copy-start.6
  6.1 0.0 copy-start.7
  6.1 0.0 copy-start
  6.1 0.0 copy-start.1
  6.1 0.0 copy-start.2
  6.1 0.0 copy-start.3
  6.1 0.0 copy-start.4
  6.1 0.0 copy-start.5
  6.1 21.1 %data_step.1 = (f32[144,512]{1,0:T(8,128)}, bf16[1,144,512]{2,1,0:T(8,128)(2,1)}) custom-call(s32[1]{0:T(128)} %bitcast.where_ref.group_ref, f32[128,512]{1,0:T(8,128)} %bitcast.17, bf16[1,128,512]{2,1,0:T(8,128)(2,1)} %bitcast.21, bf16[32,256,512]{2,1,0:T(8,128)(2,1)} %bitcast.19, bf16[32,256,512]{2,1,0:T(8,128)(2,1)} %sens_ref.1, s32[32,256]{1,0:T(8,128)} %bitcast.22, ...), custom_call_target="tpu_custom_call" | custom-call | flops 17179869184 | bytes 16777216 | tf_op jit(solution)/shard_map/data_step/pallas_call | solution.py:216
  27.2 0.2 collective-permute-start.1
  27.5 4.0 %collective-permute-done.1 = bf16[144,512]{1,0:T(8,128)(2,1)S(1)} collective-permute-done((bf16[144,512]{1,0:T(8,128)(2,1)}, bf16[144,512]{1,0:T(8,128)(2,1)S(1)}, u32[]{:S(2)}, u32[]{:S(2)}) %collective-permute-start.1) | collective-permute-done | bytes 147488 | tf_op jit(solution)/shard_map/ppermute | solution.py:259
  31.4 1.0 %fusion = (bf16[144,512]{1,0:T(8,128)(2,1)S(1)}, f32[144,512]{1,0:T(8,128)S(1)}) fusion(f32[144,512]{1,0:T(8,128)} %get-tuple-element.10, bf16[144,512]{1,0:T(8,128)(2,1)S(1)} %collective-permute-done.1), kind=kLoop, calls=%fused_computation.3 | loop fusion | flops 221184 | bytes 884736 | tf_op jit(solution)/shard_map/convert_element_type | solution.py:493
  32.5 3.0 %collective-permute-start.4 = (bf16[144,512]{1,0:T(8,128)(2,1)S(1)}, bf16[144,512]{1,0:T(8,128)(2,1)S(1)}, u32[]{:S(2)}, u32[]{:S(2)}) collective-permute-start(bf16[144,512]{1,0:T(8,128)(2,1)S(1)} %get-tuple-element.15.hidden_ref), channel_id=1, source_target_pairs={{4,8},{6,10},{12,16},{14,18},{20,24},{22,26},{8,4},{10,6},{16,12},... | collective-permute-start | bytes 442376 | tf_op jit(solution)/shard_map/ppermute | solution.py:497
  35.5 0.1 collective-permute-start.3
  35.6 3.0 %collective-permute-start.2 = (bf16[144,512]{1,0:T(8,128)(2,1)S(1)}, bf16[144,512]{1,0:T(8,128)(2,1)S(1)}, u32[]{:S(2)}, u32[]{:S(2)}) collective-permute-start(bf16[144,512]{1,0:T(8,128)(2,1)S(1)} %get-tuple-element.15.hidden_ref), channel_id=1, source_target_pairs={{0,2},{4,6},{8,10},{12,14},{16,18},{20,22},{24,26},{28,30},{2,0},{... | collective-permute-start | bytes 442376 | tf_op jit(solution)/shard_map/ppermute | solution.py:495
  38.6 0.8 %collective-permute-done.4.other_pair_ref = bf16[144,512]{1,0:T(8,128)(2,1)S(1)} collective-permute-done((bf16[144,512]{1,0:T(8,128)(2,1)S(1)}, bf16[144,512]{1,0:T(8,128)(2,1)S(1)}, u32[]{:S(2)}, u32[]{:S(2)}) %collective-permute-start.4) | collective-permute-done | bytes 147488 | tf_op jit(solution)/shard_map/ppermute | solution.py:497
  39.3 3.8 %collective-permute-start.6 = (bf16[144,512]{1,0:T(8,128)(2,1)S(1)}, bf16[144,512]{1,0:T(8,128)(2,1)S(1)}, u32[]{:S(2)}, u32[]{:S(2)}) collective-permute-start(bf16[144,512]{1,0:T(8,128)(2,1)S(1)} %collective-permute-done.4.other_pair_ref), channel_id=1, source_target_pairs={{0,2},{4,6},{8,10},{12,14},{16,18},{20,22},{24,26},{28,30},{2,0},{... | collective-permute-start | bytes 442376 | tf_op jit(solution)/shard_map/ppermute | solution.py:499
  43.2 0.0 collective-permute-done.3.first_pair_ref
  43.2 1.5 %collective-permute-start.5 = (bf16[144,512]{1,0:T(8,128)(2,1)S(1)}, bf16[144,512]{1,0:T(8,128)(2,1)S(1)}, u32[]{:S(2)}, u32[]{:S(2)}) collective-permute-start(bf16[144,512]{1,0:T(8,128)(2,1)S(1)} %collective-permute-done.3.first_pair_ref), channel_id=1, source_target_pairs={{0,2},{4,6},{8,10},{12,14},{16,18},{20,22},{24,26},{28,30},{2,0},{... | collective-permute-start | bytes 442376 | tf_op jit(solution)/shard_map/ppermute | solution.py:498
  44.7 0.0 copy-done.6
  44.7 0.0 copy-done.7
  44.7 0.0 collective-permute-done.2.partner_ref
  44.8 0.0 collective-permute-done.6.other_handed_ref
  44.8 0.9 %collective-permute-done.5.first_handed_ref = bf16[144,512]{1,0:T(8,128)(2,1)S(1)} collective-permute-done((bf16[144,512]{1,0:T(8,128)(2,1)S(1)}, bf16[144,512]{1,0:T(8,128)(2,1)S(1)}, u32[]{:S(2)}, u32[]{:S(2)}) %collective-permute-start.5) | collective-permute-done | bytes 147488 | tf_op jit(solution)/shard_map/ppermute | solution.py:498
  45.7 0.0 copy-done
  45.7 0.0 copy-done.1
  45.7 0.0 copy-done.2
  45.7 0.0 copy-done.3
  45.7 0.0 copy-done.4
  45.7 0.0 copy-done.5
  45.7 19.3 %denoise.1 = (bf16[128,512]{1,0:T(8,128)(2,1)S(1)}, f32[128,512]{1,0:T(8,128)S(1)}, bf16[128,512]{1,0:T(8,128)(2,1)S(1)}) custom-call(s32[1]{0:T(128)} %bitcast.where_ref.group_ref, s32[1]{0:T(128)} %bitcast.1.frame_ref, f32[144,512]{1,0:T(8,128)S(1)} %get-tuple-element.16.x_ref, bf16[144,512]{1,0:T(8,128)(2,1)S(1)} %get-tuple-element.15.hidden_ref, ...), custom_call_target="tpu_custom_call" | custom-call | flops 14722007040 | bytes 1474560 | tf_op jit(solution)/shard_map/denoise/pallas_call | solution.py:514
  65.1 0.4 collective-permute-start.7
  65.5 1.9 %collective-permute-start.8 = (bf16[128,512]{1,0:T(8,128)(2,1)S(1)}, bf16[128,512]{1,0:T(8,128)(2,1)S(1)}, u32[]{:S(2)}, u32[]{:S(2)}) collective-permute-start(bf16[128,512]{1,0:T(8,128)(2,1)S(1)} %get-tuple-element.14), channel_id=1, source_target_pairs={{2,4},{6,8},{10,12},{14,16},{18,20},{22,24},{26,28},{4,2},{8,6},{1... | collective-permute-start | bytes 393224 | tf_op jit(solution)/shard_map/ppermute | solution.py:543
  67.4 0.0 collective-permute-done.7
  67.4 5.8 %collective-permute-done.8 = bf16[128,512]{1,0:T(8,128)(2,1)S(1)} collective-permute-done((bf16[128,512]{1,0:T(8,128)(2,1)S(1)}, bf16[128,512]{1,0:T(8,128)(2,1)S(1)}, u32[]{:S(2)}, u32[]{:S(2)}) %collective-permute-start.8) | collective-permute-done | bytes 131104 | tf_op jit(solution)/shard_map/ppermute | solution.py:543
  73.2 0.7 %add_bitcast_fusion = f32[1,128,512]{2,1,0:T(8,128)} fusion(bf16[128,512]{1,0:T(8,128)(2,1)S(1)} %collective-permute-done.8, f32[128,512]{1,0:T(8,128)S(1)} %get-tuple-element.12, bf16[128,512]{1,0:T(8,128)(2,1)S(1)} %collective-permute-done.7), kind=kLoop, calls=%fused_computation.1 | loop fusion | flops 262144 | bytes 786432 | tf_op jit(solution)/shard_map/broadcast_in_dim | solution.py:553
  (2 shorter events, 0.1 us)
Async XLA Ops:
  1.0 4.4 %collective-permute-start = (bf16[128,512]{1,0:T(8,128)(2,1)S(1)}, bf16[128,512]{1,0:T(8,128)(2,1)S(1)}, u32[]{:S(2)}, u32[]{:S(2)}) collective-permute-start(bf16[128,512]{1,0:T(8,128)(2,1)S(1)} %bitcast_convert_fusion), channel_id=1, source_target_pairs={{0,1},{1,0},{2,3},{3,2},{4,5},{5,4},{6,7},{7,6},{8,9},{9,8},{10,11... | collective-permute-start | bytes 393224 | tf_op jit(solution)/shard_map/ppermute | solution.py:208
  5.4 0.6 copy-start.8
  6.1 38.6 %copy-start.6 = (bf16[3,3,3,64,2]{3,4,2,1,0:T(2,128)(2,1)S(1)}, bf16[3,3,3,64,2]{3,4,2,1,0:T(2,128)(2,1)}, u32[]{:S(2)}) copy-start(bf16[3,3,3,64,2]{3,4,2,1,0:T(2,128)(2,1)} %param.18) | copy-start | bytes 20740
  6.1 38.6 %copy-start.7 = (bf16[3,3,3,2,64]{4,3,2,1,0:T(2,128)(2,1)S(1)}, bf16[3,3,3,2,64]{4,3,2,1,0:T(2,128)(2,1)}, u32[]{:S(2)}) copy-start(bf16[3,3,3,2,64]{4,3,2,1,0:T(2,128)(2,1)} %param.22) | copy-start | bytes 20740
  6.1 39.6 %copy-start = (bf16[3,3,3,64,64]{4,3,2,1,0:T(8,128)(2,1)S(1)}, bf16[3,3,3,64,64]{4,3,2,1,0:T(8,128)(2,1)}, u32[]{:S(2)}) copy-start(bf16[3,3,3,64,64]{4,3,2,1,0:T(8,128)(2,1)} %param.20) | copy-start | bytes 663556
  6.1 39.6 %copy-start.1 = (f32[64]{0:T(128)S(1)}, f32[64]{0:T(128)}, u32[]{:S(2)}) copy-start(f32[64]{0:T(128)} %param.19) | copy-start | bytes 772
  6.1 39.6 %copy-start.2 = (f32[64]{0:T(128)S(1)}, f32[64]{0:T(128)}, u32[]{:S(2)}) copy-start(f32[64]{0:T(128)} %param.21) | copy-start | bytes 772
  6.1 39.6 %copy-start.3 = (bf16[12,64,192]{2,1,0:T(8,128)(2,1)S(1)}, bf16[12,64,192]{2,1,0:T(8,128)(2,1)}, u32[]{:S(2)}) copy-start(bf16[12,64,192]{2,1,0:T(8,128)(2,1)} %constant.20.clone.select_ref) | copy-start | bytes 884740
  6.1 39.6 %copy-start.4 = (bf16[256,256]{1,0:T(8,128)(2,1)S(1)}, bf16[256,256]{1,0:T(8,128)(2,1)}, u32[]{:S(2)}) copy-start(bf16[256,256]{1,0:T(8,128)(2,1)} %constant.21.clone.order_ref) | copy-start | bytes 393220
  6.1 39.6 %copy-start.5 = (bf16[432,54]{1,0:T(8,128)(2,1)S(1)}, bf16[432,54]{1,0:T(8,128)(2,1)}, u32[]{:S(2)}) copy-start(bf16[432,54]{1,0:T(8,128)(2,1)} %constant.22.clone.place_ref) | copy-start | bytes 139972
  27.2 4.2 %collective-permute-start.1 = (bf16[144,512]{1,0:T(8,128)(2,1)}, bf16[144,512]{1,0:T(8,128)(2,1)S(1)}, u32[]{:S(2)}, u32[]{:S(2)}) collective-permute-start(bf16[144,512]{1,0:T(8,128)(2,1)} %bitcast.20), channel_id=1, source_target_pairs={{0,1},{1,0},{2,3},{3,2},{4,5},{5,4},{6,7},{7,6},{8,9},{9,8},{10,11... | collective-permute-start | bytes 442376 | tf_op jit(solution)/shard_map/ppermute | solution.py:259
  32.5 6.9 %collective-permute-start.4 = (bf16[144,512]{1,0:T(8,128)(2,1)S(1)}, bf16[144,512]{1,0:T(8,128)(2,1)S(1)}, u32[]{:S(2)}, u32[]{:S(2)}) collective-permute-start(bf16[144,512]{1,0:T(8,128)(2,1)S(1)} %get-tuple-element.15.hidden_ref), channel_id=1, source_target_pairs={{4,8},{6,10},{12,16},{14,18},{20,24},{22,26},{8,4},{10,6},{16,12},... | collective-permute-start | bytes 442376 | tf_op jit(solution)/shard_map/ppermute | solution.py:497
  35.5 7.7 %collective-permute-start.3 = (bf16[144,512]{1,0:T(8,128)(2,1)S(1)}, bf16[144,512]{1,0:T(8,128)(2,1)S(1)}, u32[]{:S(2)}, u32[]{:S(2)}) collective-permute-start(bf16[144,512]{1,0:T(8,128)(2,1)S(1)} %get-tuple-element.15.hidden_ref), channel_id=1, source_target_pairs={{0,4},{2,6},{8,12},{10,14},{16,20},{18,22},{24,28},{26,30},{4,0},{... | collective-permute-start | bytes 442376 | tf_op jit(solution)/shard_map/ppermute | solution.py:496
  35.6 9.2 %collective-permute-start.2 = (bf16[144,512]{1,0:T(8,128)(2,1)S(1)}, bf16[144,512]{1,0:T(8,128)(2,1)S(1)}, u32[]{:S(2)}, u32[]{:S(2)}) collective-permute-start(bf16[144,512]{1,0:T(8,128)(2,1)S(1)} %get-tuple-element.15.hidden_ref), channel_id=1, source_target_pairs={{0,2},{4,6},{8,10},{12,14},{16,18},{20,22},{24,26},{28,30},{2,0},{... | collective-permute-start | bytes 442376 | tf_op jit(solution)/shard_map/ppermute | solution.py:495
  39.3 5.4 %collective-permute-start.6 = (bf16[144,512]{1,0:T(8,128)(2,1)S(1)}, bf16[144,512]{1,0:T(8,128)(2,1)S(1)}, u32[]{:S(2)}, u32[]{:S(2)}) collective-permute-start(bf16[144,512]{1,0:T(8,128)(2,1)S(1)} %collective-permute-done.4.other_pair_ref), channel_id=1, source_target_pairs={{0,2},{4,6},{8,10},{12,14},{16,18},{20,22},{24,26},{28,30},{2,0},{... | collective-permute-start | bytes 442376 | tf_op jit(solution)/shard_map/ppermute | solution.py:499
  43.2 2.5 %collective-permute-start.5 = (bf16[144,512]{1,0:T(8,128)(2,1)S(1)}, bf16[144,512]{1,0:T(8,128)(2,1)S(1)}, u32[]{:S(2)}, u32[]{:S(2)}) collective-permute-start(bf16[144,512]{1,0:T(8,128)(2,1)S(1)} %collective-permute-done.3.first_pair_ref), channel_id=1, source_target_pairs={{0,2},{4,6},{8,10},{12,14},{16,18},{20,22},{24,26},{28,30},{2,0},{... | collective-permute-start | bytes 442376 | tf_op jit(solution)/shard_map/ppermute | solution.py:498
  65.1 2.4 %collective-permute-start.7 = (bf16[128,512]{1,0:T(8,128)(2,1)S(1)}, bf16[128,512]{1,0:T(8,128)(2,1)S(1)}, u32[]{:S(2)}, u32[]{:S(2)}) collective-permute-start(bf16[128,512]{1,0:T(8,128)(2,1)S(1)} %get-tuple-element.13), channel_id=1, source_target_pairs={{0,2},{4,6},{8,10},{12,14},{16,18},{20,22},{24,26},{28,30},{2,0},{... | collective-permute-start | bytes 393224 | tf_op jit(solution)/shard_map/ppermute | solution.py:544
  65.5 7.7 %collective-permute-start.8 = (bf16[128,512]{1,0:T(8,128)(2,1)S(1)}, bf16[128,512]{1,0:T(8,128)(2,1)S(1)}, u32[]{:S(2)}, u32[]{:S(2)}) collective-permute-start(bf16[128,512]{1,0:T(8,128)(2,1)S(1)} %get-tuple-element.14), channel_id=1, source_target_pairs={{2,4},{6,8},{10,12},{14,16},{18,20},{22,24},{26,28},{4,2},{8,6},{1... | collective-permute-start | bytes 393224 | tf_op jit(solution)/shard_map/ppermute | solution.py:543

commit v4 on v3

--- a/solution.py
+++ b/solution.py
@@ -410,34 +410,22 @@
         slab_ref[pl.ds(pl.multiple_of(block * 8 * SLOT, 8 * SLOT), 8 * SLOT), :] = made.astype(BF16)
         return carry
 
-    lax.fori_loop(0, window // 8, interleave, 0, unroll=unrolled(window // 8, 6))
-
-    def first(q, carry):
-        source = pl.multiple_of((4 * q + RIM - 3) * SLOT, SLOT)
-        taps = slab_ref[pl.ds(source, 6 * SLOT), :]
-        made = jnp.dot(wide_ref[...], taps, preferred_element_type=F32)
-        target = pl.multiple_of(4 * q * per_row, per_row)
-        h1_ref[pl.ds(target, 4 * per_row), :] = jnp.maximum(made, 0.0).astype(BF16)
-        return carry
-
-    lax.fori_loop(0, (rows + 4) // 4, first, 0, unroll=unrolled((rows + 4) // 4, 11))
-    edge = jnp.zeros((2 * per_row, half), BF16)
-
-    @pl.when(group == 0)
-    def _():
-        h1_ref[: 2 * per_row, :] = edge
-
-    @pl.when(group == groups - 1)
-    def _():
-        h1_ref[(rows + 2) * per_row :, :] = edge
+    lax.fori_loop(0, window // 8, interleave, 0, unroll=unrolled(window // 8, 18))
 
     both = 2 * out_chan
     bias = jnp.broadcast_to(bm_ref[...], (128, out_chan)).T
     bias = jnp.concatenate([bias] * 2, 0)
     bias = jnp.concatenate([bias] * (half // 128), 1)
 
-    def mid(p, carry):
-        source = pl.multiple_of(2 * p * per_row, 2 * per_row)
+    def first(q):
+        source = pl.multiple_of((4 * q + RIM - 3) * SLOT, SLOT)
+        taps = slab_ref[pl.ds(source, 6 * SLOT), :]
+        made = jnp.dot(wide_ref[...], taps, preferred_element_type=F32)
+        target = pl.multiple_of((4 * q + 2) * per_row, 2 * per_row)
+        h1_ref[pl.ds(target, 4 * per_row), :] = jnp.maximum(made, 0.0).astype(BF16)
+
+    def mid(p):
+        source = pl.multiple_of((2 * p + 2) * per_row, 2 * per_row)
         taps = h1_ref[pl.ds(source, 4 * per_row), :]
         made = jnp.dot(wm_ref[...], taps, preferred_element_type=F32)
         total = (
@@ -446,23 +434,47 @@
             + shifted(made[2 * both :], -1)
             + bias
         )
-        target = pl.multiple_of(p * both, both)
+        target = pl.multiple_of((p + 1) * both, both)
         h2_ref[pl.ds(target, both), :] = jnp.maximum(total, 0.0).astype(BF16)
-        return carry
-
-    lax.fori_loop(0, (rows + 2) // 2, mid, 0, unroll=unrolled((rows + 2) // 2, 13))
-    edge2 = jnp.zeros((out_chan, half), BF16)
+
+    quads = (rows + 4) // 4
+    some = unrolled(quads, 3)
+    edge = jnp.zeros((2 * per_row, half), BF16)
+    h1_ref[: 2 * per_row, :] = edge
+    for q in range(some):
+        first(q)
 
     @pl.when(group == 0)
     def _():
-        h2_ref[:out_chan, :] = edge2
+        h1_ref[2 * per_row : 4 * per_row, :] = edge
+
+    def beside(g):
+        for k in range(2 * some):
+            mid(2 * some * (g - 1) - 1 + k)
+        for k in range(some):
+            first(some * g + k)
+
+    for g in range(1, quads // some):
+        beside(g)
 
     @pl.when(group == groups - 1)
     def _():
-        h2_ref[(rows + 1) * out_chan :, :] = edge2
+        h1_ref[(rows + 4) * per_row :, :] = edge
+
+    for k in range(2 * some):
+        mid(2 * (quads - some) - 1 + k)
+    edge2 = jnp.zeros((out_chan, half), BF16)
+
+    @pl.when(group == 0)
+    def _():
+        h2_ref[2 * out_chan : 3 * out_chan, :] = edge2
+
+    @pl.when(group == groups - 1)
+    def _():
+        h2_ref[(rows + 3) * out_chan :, :] = edge2
 
     def last(q, carry):
-        source = pl.multiple_of(8 * q * out_chan, 8 * out_chan)
+        source = pl.multiple_of((8 * q + 2) * out_chan, 2 * out_chan)
         taps = h2_ref[pl.ds(source, 10 * out_chan), :]
         made = jnp.dot(wl_ref[...], taps, preferred_element_type=F32)
         total = made[48:96] + shifted(made[:48], 1) + shifted(made[96:], -1)
@@ -478,7 +490,7 @@
             )
         return carry
 
-    lax.fori_loop(0, rows // 8, last, 0, unroll=unrolled(rows // 8, 8))
+    lax.fori_loop(0, rows // 8, last, 0, unroll=unrolled(rows // 8, 16))
 
 
 def swaps(count, size, odd):
@@ -523,8 +535,8 @@
             pltpu.VMEM((12 * out_chan, 6 * SLOT), BF16),
             pltpu.VMEM((6 * out_chan, 12 * out_chan), BF16),
             pltpu.VMEM((144, 10 * out_chan), BF16),
-            pltpu.VMEM(((rows + 4) * 3 * out_chan, half), BF16),
-            pltpu.VMEM(((rows + 2) * out_chan, half), BF16),
+            pltpu.VMEM(((rows + 6) * 3 * out_chan, half), BF16),
+            pltpu.VMEM(((rows + 4) * out_chan, half), BF16),
         ],
         cost_estimate=pl.CostEstimate(
             flops=2 * (rows + 2) * half * 192 * 1152,

time: 74.1 us -> 72.1 us (0.973)
  Pallas kernels: 40.4 us -> 38.4 us
    pallas_call x1, Pallas kernels: 19.3 us -> 17.3 us  [denoise(): pl.pallas_call(functools.partial(denoise_kernel, groups, frames), in_spec...]
where the time goes in v4:
time: 72.1 us; the launch traced here: 71.9 us
  Pallas kernels  38.4 us (53%)
  waiting for transfers between devices  15.6 us (22%)
  starting transfers between devices  14.3 us (20%)
  other arithmetic  2.71 us (4%)
  local copies, waits for them, and re-layouts  0.74 us (1%)
    pallas_call x1, Pallas kernels, data_step(): pl.pallas_call(functools.partial(data_kernel, coils_at_once, 32), grid=(c...  21.1 us
    pallas_call x1, Pallas kernels, denoise(): pl.pallas_call(functools.partial(denoise_kernel, groups, frames), in_spec...  17.3 us
    ppermute x1, waiting for transfers between devices, denoise(): outer = lax.ppermute(outer, 'frame', across).astype(F32)  5.75 us
    ppermute x1, waiting for transfers between devices, data_step(): lax.ppermute(low, 'coil', shift(hop))  4.16 us
    ppermute x1, waiting for transfers between devices, data_step(): own = own + lax.ppermute(send[hop - 1], 'coil', shift(hop)).astype(F32)  3.97 us
    ppermute x1, starting transfers between devices, denoise(): other_handed = lax.ppermute(other_pair, 'frame', within)  3.84 us
    ppermute x1, starting transfers between devices, denoise(): partner = lax.ppermute(hidden, 'frame', within)  3.04 us
    ppermute x1, starting transfers between devices, denoise(): other_pair = lax.ppermute(hidden, 'frame', swaps(frames, 2, 1))  3 us
  transfers between devices with their start and end apart: 9, of which 5 were waited for; matrix products, arithmetic and copies ran while one was open for 0% of the time, Pallas kernels for 0%

profile of v4, /device:TPU:29, one launch (start us, length us, event | category | flops | bytes accessed | tf_op | source)
XLA Modules:
  0.0 71.9 jit_solution(12367038018928652732)
XLA Ops:
  0.0 1.0 %bitcast_convert_fusion = bf16[128,512]{1,0:T(8,128)(2,1)S(1)} fusion(f32[1,128,512]{2,1,0:T(8,128)} %param.17), kind=kLoop, calls=%fused_computation.2 | loop fusion | flops 65536 | bytes 393216 | tf_op jit(solution)/shard_map/convert_element_type | solution.py:207
  1.0 0.3 collective-permute-start
  1.3 4.2 %collective-permute-done = bf16[128,512]{1,0:T(8,128)(2,1)S(1)} collective-permute-done((bf16[128,512]{1,0:T(8,128)(2,1)S(1)}, bf16[128,512]{1,0:T(8,128)(2,1)S(1)}, u32[]{:S(2)}, u32[]{:S(2)}) %collective-permute-start) | collective-permute-done | bytes 131104 | tf_op jit(solution)/shard_map/ppermute | solution.py:208
  5.4 0.0 copy-start.8
  5.4 0.6 copy-done.8
  6.1 0.0 copy-start.6
  6.1 0.0 copy-start.7
  6.1 0.0 copy-start
  6.1 0.0 copy-start.1
  6.1 0.0 copy-start.2
  6.1 0.0 copy-start.3
  6.1 0.0 copy-start.4
  6.1 0.0 copy-start.5
  6.1 21.1 %data_step.1 = (f32[144,512]{1,0:T(8,128)}, bf16[1,144,512]{2,1,0:T(8,128)(2,1)}) custom-call(s32[1]{0:T(128)} %bitcast.where_ref.group_ref, f32[128,512]{1,0:T(8,128)} %bitcast.17, bf16[1,128,512]{2,1,0:T(8,128)(2,1)} %bitcast.21, bf16[32,256,512]{2,1,0:T(8,128)(2,1)} %bitcast.19, bf16[32,256,512]{2,1,0:T(8,128)(2,1)} %sens_ref.1, s32[32,256]{1,0:T(8,128)} %bitcast.22, ...), custom_call_target="tpu_custom_call" | custom-call | flops 17179869184 | bytes 16777216 | tf_op jit(solution)/shard_map/data_step/pallas_call | solution.py:216
  27.2 0.2 collective-permute-start.1
  27.5 4.0 %collective-permute-done.1 = bf16[144,512]{1,0:T(8,128)(2,1)S(1)} collective-permute-done((bf16[144,512]{1,0:T(8,128)(2,1)}, bf16[144,512]{1,0:T(8,128)(2,1)S(1)}, u32[]{:S(2)}, u32[]{:S(2)}) %collective-permute-start.1) | collective-permute-done | bytes 147488 | tf_op jit(solution)/shard_map/ppermute | solution.py:259
  31.4 1.0 %fusion = (bf16[144,512]{1,0:T(8,128)(2,1)S(1)}, f32[144,512]{1,0:T(8,128)S(1)}) fusion(f32[144,512]{1,0:T(8,128)} %get-tuple-element.10, bf16[144,512]{1,0:T(8,128)(2,1)S(1)} %collective-permute-done.1), kind=kLoop, calls=%fused_computation.3 | loop fusion | flops 221184 | bytes 884736 | tf_op jit(solution)/shard_map/convert_element_type | solution.py:505
  32.4 3.0 %collective-permute-start.4 = (bf16[144,512]{1,0:T(8,128)(2,1)S(1)}, bf16[144,512]{1,0:T(8,128)(2,1)S(1)}, u32[]{:S(2)}, u32[]{:S(2)}) collective-permute-start(bf16[144,512]{1,0:T(8,128)(2,1)S(1)} %get-tuple-element.15.hidden_ref), channel_id=1, source_target_pairs={{4,8},{6,10},{12,16},{14,18},{20,24},{22,26},{8,4},{10,6},{16,12},... | collective-permute-start | bytes 442376 | tf_op jit(solution)/shard_map/ppermute | solution.py:509
  35.5 0.1 collective-permute-start.3
  35.5 3.0 %collective-permute-start.2 = (bf16[144,512]{1,0:T(8,128)(2,1)S(1)}, bf16[144,512]{1,0:T(8,128)(2,1)S(1)}, u32[]{:S(2)}, u32[]{:S(2)}) collective-permute-start(bf16[144,512]{1,0:T(8,128)(2,1)S(1)} %get-tuple-element.15.hidden_ref), channel_id=1, source_target_pairs={{0,2},{4,6},{8,10},{12,14},{16,18},{20,22},{24,26},{28,30},{2,0},{... | collective-permute-start | bytes 442376 | tf_op jit(solution)/shard_map/ppermute | solution.py:507
  38.6 0.8 %collective-permute-done.4.other_pair_ref = bf16[144,512]{1,0:T(8,128)(2,1)S(1)} collective-permute-done((bf16[144,512]{1,0:T(8,128)(2,1)S(1)}, bf16[144,512]{1,0:T(8,128)(2,1)S(1)}, u32[]{:S(2)}, u32[]{:S(2)}) %collective-permute-start.4) | collective-permute-done | bytes 147488 | tf_op jit(solution)/shard_map/ppermute | solution.py:509
  39.3 3.8 %collective-permute-start.6 = (bf16[144,512]{1,0:T(8,128)(2,1)S(1)}, bf16[144,512]{1,0:T(8,128)(2,1)S(1)}, u32[]{:S(2)}, u32[]{:S(2)}) collective-permute-start(bf16[144,512]{1,0:T(8,128)(2,1)S(1)} %collective-permute-done.4.other_pair_ref), channel_id=1, source_target_pairs={{0,2},{4,6},{8,10},{12,14},{16,18},{20,22},{24,26},{28,30},{2,0},{... | collective-permute-start | bytes 442376 | tf_op jit(solution)/shard_map/ppermute | solution.py:511
  43.2 0.0 collective-permute-done.3.first_pair_ref
  43.2 1.5 %collective-permute-start.5 = (bf16[144,512]{1,0:T(8,128)(2,1)S(1)}, bf16[144,512]{1,0:T(8,128)(2,1)S(1)}, u32[]{:S(2)}, u32[]{:S(2)}) collective-permute-start(bf16[144,512]{1,0:T(8,128)(2,1)S(1)} %collective-permute-done.3.first_pair_ref), channel_id=1, source_target_pairs={{0,2},{4,6},{8,10},{12,14},{16,18},{20,22},{24,26},{28,30},{2,0},{... | collective-permute-start | bytes 442376 | tf_op jit(solution)/shard_map/ppermute | solution.py:510
  44.7 0.0 copy-done.6
  44.7 0.0 copy-done.7
  44.7 0.0 collective-permute-done.2.partner_ref
  44.8 0.0 collective-permute-done.6.other_handed_ref
  44.8 0.9 %collective-permute-done.5.first_handed_ref = bf16[144,512]{1,0:T(8,128)(2,1)S(1)} collective-permute-done((bf16[144,512]{1,0:T(8,128)(2,1)S(1)}, bf16[144,512]{1,0:T(8,128)(2,1)S(1)}, u32[]{:S(2)}, u32[]{:S(2)}) %collective-permute-start.5) | collective-permute-done | bytes 147488 | tf_op jit(solution)/shard_map/ppermute | solution.py:510
  45.7 0.0 copy-done
  45.7 0.0 copy-done.1
  45.7 0.0 copy-done.2
  45.7 0.0 copy-done.3
  45.7 0.0 copy-done.4
  45.7 0.0 copy-done.5
  45.7 17.3 %denoise.1 = (bf16[128,512]{1,0:T(8,128)(2,1)S(1)}, f32[128,512]{1,0:T(8,128)S(1)}, bf16[128,512]{1,0:T(8,128)(2,1)S(1)}) custom-call(s32[1]{0:T(128)} %bitcast.where_ref.group_ref, s32[1]{0:T(128)} %bitcast.1.frame_ref, f32[144,512]{1,0:T(8,128)S(1)} %get-tuple-element.16.x_ref, bf16[144,512]{1,0:T(8,128)(2,1)S(1)} %get-tuple-element.15.hidden_ref, ...), custom_call_target="tpu_custom_call" | custom-call | flops 14722007040 | bytes 1474560 | tf_op jit(solution)/shard_map/denoise/pallas_call | solution.py:526
  63.0 0.4 collective-permute-start.7
  63.5 1.9 %collective-permute-start.8 = (bf16[128,512]{1,0:T(8,128)(2,1)S(1)}, bf16[128,512]{1,0:T(8,128)(2,1)S(1)}, u32[]{:S(2)}, u32[]{:S(2)}) collective-permute-start(bf16[128,512]{1,0:T(8,128)(2,1)S(1)} %get-tuple-element.14), channel_id=1, source_target_pairs={{2,4},{6,8},{10,12},{14,16},{18,20},{22,24},{26,28},{4,2},{8,6},{1... | collective-permute-start | bytes 393224 | tf_op jit(solution)/shard_map/ppermute | solution.py:555
  65.4 0.0 collective-permute-done.7
  65.4 5.8 %collective-permute-done.8 = bf16[128,512]{1,0:T(8,128)(2,1)S(1)} collective-permute-done((bf16[128,512]{1,0:T(8,128)(2,1)S(1)}, bf16[128,512]{1,0:T(8,128)(2,1)S(1)}, u32[]{:S(2)}, u32[]{:S(2)}) %collective-permute-start.8) | collective-permute-done | bytes 131104 | tf_op jit(solution)/shard_map/ppermute | solution.py:555
  71.1 0.7 %add_bitcast_fusion = f32[1,128,512]{2,1,0:T(8,128)} fusion(bf16[128,512]{1,0:T(8,128)(2,1)S(1)} %collective-permute-done.8, f32[128,512]{1,0:T(8,128)S(1)} %get-tuple-element.12, bf16[128,512]{1,0:T(8,128)(2,1)S(1)} %collective-permute-done.7), kind=kLoop, calls=%fused_computation.1 | loop fusion | flops 262144 | bytes 786432 | tf_op jit(solution)/shard_map/broadcast_in_dim | solution.py:565
  (2 shorter events, 0.1 us)
Async XLA Ops:
  1.0 4.4 %collective-permute-start = (bf16[128,512]{1,0:T(8,128)(2,1)S(1)}, bf16[128,512]{1,0:T(8,128)(2,1)S(1)}, u32[]{:S(2)}, u32[]{:S(2)}) collective-permute-start(bf16[128,512]{1,0:T(8,128)(2,1)S(1)} %bitcast_convert_fusion), channel_id=1, source_target_pairs={{0,1},{1,0},{2,3},{3,2},{4,5},{5,4},{6,7},{7,6},{8,9},{9,8},{10,11... | collective-permute-start | bytes 393224 | tf_op jit(solution)/shard_map/ppermute | solution.py:208
  5.4 0.6 copy-start.8
  6.1 38.6 %copy-start.6 = (bf16[3,3,3,64,2]{3,4,2,1,0:T(2,128)(2,1)S(1)}, bf16[3,3,3,64,2]{3,4,2,1,0:T(2,128)(2,1)}, u32[]{:S(2)}) copy-start(bf16[3,3,3,64,2]{3,4,2,1,0:T(2,128)(2,1)} %param.18) | copy-start | bytes 20740
  6.1 38.6 %copy-start.7 = (bf16[3,3,3,2,64]{4,3,2,1,0:T(2,128)(2,1)S(1)}, bf16[3,3,3,2,64]{4,3,2,1,0:T(2,128)(2,1)}, u32[]{:S(2)}) copy-start(bf16[3,3,3,2,64]{4,3,2,1,0:T(2,128)(2,1)} %param.22) | copy-start | bytes 20740
  6.1 39.6 %copy-start = (bf16[3,3,3,64,64]{4,3,2,1,0:T(8,128)(2,1)S(1)}, bf16[3,3,3,64,64]{4,3,2,1,0:T(8,128)(2,1)}, u32[]{:S(2)}) copy-start(bf16[3,3,3,64,64]{4,3,2,1,0:T(8,128)(2,1)} %param.20) | copy-start | bytes 663556
  6.1 39.6 %copy-start.1 = (f32[64]{0:T(128)S(1)}, f32[64]{0:T(128)}, u32[]{:S(2)}) copy-start(f32[64]{0:T(128)} %param.19) | copy-start | bytes 772
  6.1 39.6 %copy-start.2 = (f32[64]{0:T(128)S(1)}, f32[64]{0:T(128)}, u32[]{:S(2)}) copy-start(f32[64]{0:T(128)} %param.21) | copy-start | bytes 772
  6.1 39.6 %copy-start.3 = (bf16[12,64,192]{2,1,0:T(8,128)(2,1)S(1)}, bf16[12,64,192]{2,1,0:T(8,128)(2,1)}, u32[]{:S(2)}) copy-start(bf16[12,64,192]{2,1,0:T(8,128)(2,1)} %constant.20.clone.select_ref) | copy-start | bytes 884740
  6.1 39.6 %copy-start.4 = (bf16[256,256]{1,0:T(8,128)(2,1)S(1)}, bf16[256,256]{1,0:T(8,128)(2,1)}, u32[]{:S(2)}) copy-start(bf16[256,256]{1,0:T(8,128)(2,1)} %constant.21.clone.order_ref) | copy-start | bytes 393220
  6.1 39.6 %copy-start.5 = (bf16[432,54]{1,0:T(8,128)(2,1)S(1)}, bf16[432,54]{1,0:T(8,128)(2,1)}, u32[]{:S(2)}) copy-start(bf16[432,54]{1,0:T(8,128)(2,1)} %constant.22.clone.place_ref) | copy-start | bytes 139972
  27.2 4.2 %collective-permute-start.1 = (bf16[144,512]{1,0:T(8,128)(2,1)}, bf16[144,512]{1,0:T(8,128)(2,1)S(1)}, u32[]{:S(2)}, u32[]{:S(2)}) collective-permute-start(bf16[144,512]{1,0:T(8,128)(2,1)} %bitcast.20), channel_id=1, source_target_pairs={{0,1},{1,0},{2,3},{3,2},{4,5},{5,4},{6,7},{7,6},{8,9},{9,8},{10,11... | collective-permute-start | bytes 442376 | tf_op jit(solution)/shard_map/ppermute | solution.py:259
  32.4 6.9 %collective-permute-start.4 = (bf16[144,512]{1,0:T(8,128)(2,1)S(1)}, bf16[144,512]{1,0:T(8,128)(2,1)S(1)}, u32[]{:S(2)}, u32[]{:S(2)}) collective-permute-start(bf16[144,512]{1,0:T(8,128)(2,1)S(1)} %get-tuple-element.15.hidden_ref), channel_id=1, source_target_pairs={{4,8},{6,10},{12,16},{14,18},{20,24},{22,26},{8,4},{10,6},{16,12},... | collective-permute-start | bytes 442376 | tf_op jit(solution)/shard_map/ppermute | solution.py:509
  35.5 7.7 %collective-permute-start.3 = (bf16[144,512]{1,0:T(8,128)(2,1)S(1)}, bf16[144,512]{1,0:T(8,128)(2,1)S(1)}, u32[]{:S(2)}, u32[]{:S(2)}) collective-permute-start(bf16[144,512]{1,0:T(8,128)(2,1)S(1)} %get-tuple-element.15.hidden_ref), channel_id=1, source_target_pairs={{0,4},{2,6},{8,12},{10,14},{16,20},{18,22},{24,28},{26,30},{4,0},{... | collective-permute-start | bytes 442376 | tf_op jit(solution)/shard_map/ppermute | solution.py:508
  35.5 9.2 %collective-permute-start.2 = (bf16[144,512]{1,0:T(8,128)(2,1)S(1)}, bf16[144,512]{1,0:T(8,128)(2,1)S(1)}, u32[]{:S(2)}, u32[]{:S(2)}) collective-permute-start(bf16[144,512]{1,0:T(8,128)(2,1)S(1)} %get-tuple-element.15.hidden_ref), channel_id=1, source_target_pairs={{0,2},{4,6},{8,10},{12,14},{16,18},{20,22},{24,26},{28,30},{2,0},{... | collective-permute-start | bytes 442376 | tf_op jit(solution)/shard_map/ppermute | solution.py:507
  39.3 5.4 %collective-permute-start.6 = (bf16[144,512]{1,0:T(8,128)(2,1)S(1)}, bf16[144,512]{1,0:T(8,128)(2,1)S(1)}, u32[]{:S(2)}, u32[]{:S(2)}) collective-permute-start(bf16[144,512]{1,0:T(8,128)(2,1)S(1)} %collective-permute-done.4.other_pair_ref), channel_id=1, source_target_pairs={{0,2},{4,6},{8,10},{12,14},{16,18},{20,22},{24,26},{28,30},{2,0},{... | collective-permute-start | bytes 442376 | tf_op jit(solution)/shard_map/ppermute | solution.py:511
  43.2 2.5 %collective-permute-start.5 = (bf16[144,512]{1,0:T(8,128)(2,1)S(1)}, bf16[144,512]{1,0:T(8,128)(2,1)S(1)}, u32[]{:S(2)}, u32[]{:S(2)}) collective-permute-start(bf16[144,512]{1,0:T(8,128)(2,1)S(1)} %collective-permute-done.3.first_pair_ref), channel_id=1, source_target_pairs={{0,2},{4,6},{8,10},{12,14},{16,18},{20,22},{24,26},{28,30},{2,0},{... | collective-permute-start | bytes 442376 | tf_op jit(solution)/shard_map/ppermute | solution.py:510
  63.0 2.4 %collective-permute-start.7 = (bf16[128,512]{1,0:T(8,128)(2,1)S(1)}, bf16[128,512]{1,0:T(8,128)(2,1)S(1)}, u32[]{:S(2)}, u32[]{:S(2)}) collective-permute-start(bf16[128,512]{1,0:T(8,128)(2,1)S(1)} %get-tuple-element.13), channel_id=1, source_target_pairs={{0,2},{4,6},{8,10},{12,14},{16,18},{20,22},{24,26},{28,30},{2,0},{... | collective-permute-start | bytes 393224 | tf_op jit(solution)/shard_map/ppermute | solution.py:556
  63.5 7.7 %collective-permute-start.8 = (bf16[128,512]{1,0:T(8,128)(2,1)S(1)}, bf16[128,512]{1,0:T(8,128)(2,1)S(1)}, u32[]{:S(2)}, u32[]{:S(2)}) collective-permute-start(bf16[128,512]{1,0:T(8,128)(2,1)S(1)} %get-tuple-element.14), channel_id=1, source_target_pairs={{2,4},{6,8},{10,12},{14,16},{18,20},{22,24},{26,28},{4,2},{8,6},{1... | collective-permute-start | bytes 393224 | tf_op jit(solution)/shard_map/ppermute | solution.py:555

commit v5 on v4

--- a/solution.py
+++ b/solution.py
@@ -57,7 +57,8 @@
     kspace_ref,
     sens_ref,
     mask_ref,
-    cols_ref,
+    col_ahead_ref,
+    col_behind_ref,
     rows_ref,
     own_ref,
     send_ref,
@@ -71,8 +72,6 @@
     miss_ref,
     fold_ref,
     bimg_ref,
-    col_ahead_ref,
-    col_behind_ref,
 ):
     groups = others_ref.shape[0] + 1
     own_rows = image_ref.shape[0]
@@ -84,9 +83,6 @@
 
     @pl.when(step == 0)
     def _():
-        real, imag = cols_ref[0], cols_ref[1]
-        put_table(col_ahead_ref, real, imag, -imag, real)
-        put_table(col_behind_ref, real, -imag, imag, real)
         acc_ref[...] = jnp.zeros_like(acc_ref)
         natural_ref[...] = jnp.zeros_like(natural_ref)
         for j in range(lanes):
@@ -198,6 +194,25 @@
                 send_ref[hop - 1, :, part] = natural_ref[j, pl.ds(theirs, window), :].astype(BF16)
 
 
+def prepare_kernel(
+    image_ref, mask_ref, cols_ref, image_out, mask_out, ahead_ref, behind_ref, parts_ref, sems
+):
+    copies = [
+        pltpu.make_async_copy(source, target, sems.at[k])
+        for k, (source, target) in enumerate(
+            ((cols_ref, parts_ref), (image_ref, image_out), (mask_ref, mask_out))
+        )
+    ]
+    for copy in copies:
+        copy.start()
+    copies[0].wait()
+    real, imag = parts_ref[0], parts_ref[1]
+    put_table(ahead_ref, real, imag, -imag, real)
+    put_table(behind_ref, real, -imag, imag, real)
+    copies[1].wait()
+    copies[2].wait()
+
+
 def data_step(image, kspace, sens, mask, here, groups):
     own_rows, double = image.shape
     coils, n_rows, _ = sens.shape
@@ -208,8 +223,19 @@
     others = jnp.stack([lax.ppermute(low, "coil", shift(hop)) for hop in range(1, groups)])
     cols = jnp.asarray(dft_parts(half), BF16)
     lines = jnp.asarray(halved(dft_parts(n_rows)), BF16)
+    table = jax.ShapeDtypeStruct((double, double), BF16)
+    vmem = pl.BlockSpec(memory_space=pltpu.VMEM)
+    image, mask, ahead, behind = pl.pallas_call(
+        prepare_kernel,
+        in_specs=[pl.BlockSpec(memory_space=pl.ANY)] * 3,
+        out_specs=[vmem] * 4,
+        out_shape=[jax.ShapeDtypeStruct(a.shape, a.dtype) for a in (image, mask)] + [table] * 2,
+        scratch_shapes=[pltpu.VMEM(cols.shape, BF16), pltpu.SemaphoreType.DMA((3,))],
+        compiler_params=pltpu.CompilerParams(vmem_limit_bytes=8 << 20),
+        cost_estimate=pl.CostEstimate(flops=0, bytes_accessed=6 << 20, transcendentals=0),
+        name="prepare",
+    )(image, mask, cols)
     window = own_rows + 2 * RIM
-    vmem = pl.BlockSpec(memory_space=pltpu.VMEM)
     per_coil = lambda a: pl.BlockSpec(
         (coils_at_once,) + a.shape[1:], lambda i: (i,) + (0,) * (a.ndim - 1)
     )
@@ -222,6 +248,7 @@
             vmem,
             per_coil(kspace),
             per_coil(sens),
+            vmem,
             vmem,
             vmem,
             vmem,
@@ -245,16 +272,15 @@
             pltpu.VMEM((coils_at_once * n_rows, double), BF16),
             pltpu.VMEM((coils_at_once, 2, n_rows, half), BF16),
             pltpu.VMEM((coils_at_once, 2, n_rows, half), F32),
-        ]
-        + [pltpu.VMEM((double, double), BF16)] * 2,
-        compiler_params=pltpu.CompilerParams(vmem_limit_bytes=57 << 20),
+        ],
+        compiler_params=pltpu.CompilerParams(vmem_limit_bytes=52 << 20),
         cost_estimate=pl.CostEstimate(
             flops=32 * coils * n_rows * n_rows * half,
             bytes_accessed=4 * coils * n_rows * double,
             transcendentals=0,
         ),
         name="data_step",
-    )(here, image, others, kspace, sens, mask, cols, lines)
+    )(here, image, others, kspace, sens, mask, ahead, behind, lines)
     for hop in range(1, groups):
         own = own + lax.ppermute(send[hop - 1], "coil", shift(hop)).astype(F32)
     return own

time: 72.1 us -> 69.5 us (0.964)
  waiting for transfers between devices: 15.6 us -> 11.8 us
  local copies, waits for them, and re-layouts: 0.74 us -> 2.76 us
  other arithmetic: 2.71 us -> 1.75 us
    ppermute x1, waiting for transfers between devices: 4.16 us -> 1.32 us  [data_step(): lax.ppermute(low, 'coil', shift(hop))]
    unnamed x18 -> x22, local copies, waits for them, and re-layouts: 0.69 us -> 2.7 us
    ppermute x1, starting transfers between devices: 1.49 us -> 2.84 us  [denoise(): first_handed = lax.ppermute(first_pair, 'frame', within)]
    ppermute x1, starting transfers between devices: 0.07 us -> 1.27 us  [denoise(): first_pair = lax.ppermute(hidden, 'frame', swaps(frames, 2, 0))]
    ppermute x1, starting transfers between devices: 3.84 us -> 2.69 us  [denoise(): other_handed = lax.ppermute(other_pair, 'frame', within)]
    ppermute x1, starting transfers between devices: 3 us -> 2.03 us  [denoise(): other_pair = lax.ppermute(hidden, 'frame', swaps(frames, 2, 1))]
    convert_element_type x1, other arithmetic: 1 us -> 0.04 us  [denoise(): hidden = x.astype(BF16)]
    ppermute x1, waiting for transfers between devices: 0.91 us -> 0.01 us  [denoise(): first_handed = lax.ppermute(first_pair, 'frame', within)]
  transfers between devices with their start and end apart: 9 -> 9, of which waited for: 5 -> 4; matrix products, arithmetic and copies ran while one was open for 0% -> 0% of each run, Pallas kernels for 0% -> 0%
where the time goes in v5:
time: 69.5 us; the launch traced here: 69.2 us
  Pallas kernels  37.7 us (54%)
  starting transfers between devices  15 us (22%)
  waiting for transfers between devices  11.8 us (17%)
  local copies, waits for them, and re-layouts  2.76 us (4%)
  other arithmetic  1.75 us (3%)
    pallas_call x1, Pallas kernels, data_step(): pl.pallas_call(functools.partial(data_kernel, coils_at_once, 32), grid=(c...  20.3 us
    pallas_call x1, Pallas kernels, denoise(): pl.pallas_call(functools.partial(denoise_kernel, groups, frames), in_spec...  17.3 us
    ppermute x1, waiting for transfers between devices, denoise(): outer = lax.ppermute(outer, 'frame', across).astype(F32)  5.75 us
    ppermute x1, waiting for transfers between devices, data_step(): own = own + lax.ppermute(send[hop - 1], 'coil', shift(hop)).astype(F32)  3.79 us
    ppermute x1, starting transfers between devices, denoise(): partner = lax.ppermute(hidden, 'frame', within)  3.31 us
    ppermute x1, starting transfers between devices, denoise(): first_handed = lax.ppermute(first_pair, 'frame', within)  2.84 us
    unnamed x22, local copies, waits for them, and re-layouts  2.7 us
    ppermute x1, starting transfers between devices, denoise(): other_handed = lax.ppermute(other_pair, 'frame', within)  2.69 us
  transfers between devices with their start and end apart: 9, of which 4 were waited for; matrix products, arithmetic and copies ran while one was open for 0% of the time, Pallas kernels for 0%

profile of v5, /device:TPU:29, one launch (start us, length us, event | category | flops | bytes accessed | tf_op | source)
XLA Modules:
  0.0 69.2 jit_solution(17226738825548448096)
XLA Ops:
  0.0 1.0 %bitcast_convert_fusion = bf16[128,512]{1,0:T(8,128)(2,1)S(1)} fusion(f32[1,128,512]{2,1,0:T(8,128)} %param.17), kind=kLoop, calls=%fused_computation.2 | loop fusion | flops 65536 | bytes 393216 | tf_op jit(solution)/shard_map/convert_element_type | solution.py:222
  1.0 0.3 collective-permute-start
  1.3 0.0 copy-start
  1.3 0.9 %copy-done = f32[1,128,512]{2,1,0:T(8,128)S(1)} copy-done((f32[1,128,512]{2,1,0:T(8,128)S(1)}, f32[1,128,512]{2,1,0:T(8,128)}, u32[]{:S(2)}) %copy-start) | copy-done | bytes 262168
  2.2 0.0 copy-start.1
  2.2 0.9 %copy-done.1 = bf16[2,256,256]{2,1,0:T(8,128)(2,1)S(1)} copy-done((bf16[2,256,256]{2,1,0:T(8,128)(2,1)S(1)}, bf16[2,256,256]{2,1,0:T(8,128)(2,1)}, u32[]{:S(2)}) %copy-start.1) | copy-done | bytes 262168
  3.2 0.0 copy-start.2
  3.2 0.8 %copy-done.2 = s32[1,32,256]{2,1,0:T(8,128)S(1)} copy-done((s32[1,32,256]{2,1,0:T(8,128)S(1)}, s32[1,32,256]{2,1,0:T(8,128)}, u32[]{:S(2)}) %copy-start.2) | copy-done | bytes 32792
  3.9 0.2 prepare.1
  4.1 1.3 %collective-permute-done = bf16[128,512]{1,0:T(8,128)(2,1)S(1)} collective-permute-done((bf16[128,512]{1,0:T(8,128)(2,1)S(1)}, bf16[128,512]{1,0:T(8,128)(2,1)S(1)}, u32[]{:S(2)}, u32[]{:S(2)}) %collective-permute-start) | collective-permute-done | bytes 131104 | tf_op jit(solution)/shard_map/ppermute | solution.py:223
  5.4 0.0 copy-start.9
  5.4 0.0 copy-start.10
  5.4 0.0 copy-start.3
  5.4 0.0 copy-start.4
  5.4 0.0 copy-start.5
  5.4 0.0 copy-start.6
  5.5 0.0 copy-start.7
  5.5 0.0 copy-start.8
  5.5 20.3 %data_step.1 = (f32[144,512]{1,0:T(8,128)S(1)}, bf16[1,144,512]{2,1,0:T(8,128)(2,1)S(1)}) custom-call(s32[1]{0:T(128)} %bitcast.where_ref.group_ref, f32[128,512]{1,0:T(8,128)S(1)} %get-tuple-element.14.image_ref, bf16[1,128,512]{2,1,0:T(8,128)(2,1)S(1)} %bitcast.18, bf16[32,256,512]{2,1,0:T(8,128)(2,1)} %bitcast.22, bf16[32,256,512]{2,1,0:T(8,128)(2,1)} %sens_ref.1, ...), custom_call_target="tpu_custom_call" | custom-call | flops 17179869184 | bytes 16777216 | tf_op jit(solution)/shard_map/data_step/pallas_call | solution.py:242
  25.8 0.3 collective-permute-start.1
  26.0 3.8 %collective-permute-done.1 = bf16[144,512]{1,0:T(8,128)(2,1)S(1)} collective-permute-done((bf16[144,512]{1,0:T(8,128)(2,1)S(1)}, bf16[144,512]{1,0:T(8,128)(2,1)S(1)}, u32[]{:S(2)}, u32[]{:S(2)}) %collective-permute-start.1) | collective-permute-done | bytes 147488 | tf_op jit(solution)/shard_map/ppermute | solution.py:285
  29.9 1.3 %collective-permute-start.3 = (bf16[144,512]{1,0:T(8,128)(2,1)S(1)}, bf16[144,512]{1,0:T(8,128)(2,1)S(1)}, u32[]{:S(2)}, u32[]{:S(2)}) collective-permute-start(bf16[144,512]{1,0:T(8,128)(2,1)S(1)} %get-tuple-element.23.hidden_ref), channel_id=1, source_target_pairs={{0,4},{2,6},{8,12},{10,14},{16,20},{18,22},{24,28},{26,30},{4,0},{... | collective-permute-start | bytes 442376 | tf_op jit(solution)/shard_map/ppermute | solution.py:534
  31.1 2.0 %collective-permute-start.4 = (bf16[144,512]{1,0:T(8,128)(2,1)S(1)}, bf16[144,512]{1,0:T(8,128)(2,1)S(1)}, u32[]{:S(2)}, u32[]{:S(2)}) collective-permute-start(bf16[144,512]{1,0:T(8,128)(2,1)S(1)} %get-tuple-element.23.hidden_ref), channel_id=1, source_target_pairs={{4,8},{6,10},{12,16},{14,18},{20,24},{22,26},{8,4},{10,6},{16,12},... | collective-permute-start | bytes 442376 | tf_op jit(solution)/shard_map/ppermute | solution.py:535
  33.2 3.3 %collective-permute-start.2 = (bf16[144,512]{1,0:T(8,128)(2,1)S(1)}, bf16[144,512]{1,0:T(8,128)(2,1)S(1)}, u32[]{:S(2)}, u32[]{:S(2)}) collective-permute-start(bf16[144,512]{1,0:T(8,128)(2,1)S(1)} %get-tuple-element.23.hidden_ref), channel_id=1, source_target_pairs={{0,2},{4,6},{8,10},{12,14},{16,18},{20,22},{24,26},{28,30},{2,0},{... | collective-permute-start | bytes 442376 | tf_op jit(solution)/shard_map/ppermute | solution.py:533
  36.5 0.0 collective-permute-done.3.first_pair_ref
  36.5 2.8 %collective-permute-start.5 = (bf16[144,512]{1,0:T(8,128)(2,1)S(1)}, bf16[144,512]{1,0:T(8,128)(2,1)S(1)}, u32[]{:S(2)}, u32[]{:S(2)}) collective-permute-start(bf16[144,512]{1,0:T(8,128)(2,1)S(1)} %collective-permute-done.3.first_pair_ref), channel_id=1, source_target_pairs={{0,2},{4,6},{8,10},{12,14},{16,18},{20,22},{24,26},{28,30},{2,0},{... | collective-permute-start | bytes 442376 | tf_op jit(solution)/shard_map/ppermute | solution.py:536
  39.3 0.0 collective-permute-done.4.other_pair_ref
  39.3 2.7 %collective-permute-start.6 = (bf16[144,512]{1,0:T(8,128)(2,1)S(1)}, bf16[144,512]{1,0:T(8,128)(2,1)S(1)}, u32[]{:S(2)}, u32[]{:S(2)}) collective-permute-start(bf16[144,512]{1,0:T(8,128)(2,1)S(1)} %collective-permute-done.4.other_pair_ref), channel_id=1, source_target_pairs={{0,2},{4,6},{8,10},{12,14},{16,18},{20,22},{24,26},{28,30},{2,0},{... | collective-permute-start | bytes 442376 | tf_op jit(solution)/shard_map/ppermute | solution.py:537
  42.0 0.0 copy-done.9
  42.0 0.0 copy-done.10
  42.1 0.0 collective-permute-done.2.partner_ref
  42.1 0.0 collective-permute-done.5.first_handed_ref
  42.1 0.9 %collective-permute-done.6.other_handed_ref = bf16[144,512]{1,0:T(8,128)(2,1)S(1)} collective-permute-done((bf16[144,512]{1,0:T(8,128)(2,1)S(1)}, bf16[144,512]{1,0:T(8,128)(2,1)S(1)}, u32[]{:S(2)}, u32[]{:S(2)}) %collective-permute-start.6) | collective-permute-done | bytes 147488 | tf_op jit(solution)/shard_map/ppermute | solution.py:537
  43.0 0.0 copy-done.3
  43.0 0.0 copy-done.4
  43.0 0.0 copy-done.5
  43.0 0.0 copy-done.6
  43.0 0.0 copy-done.7
  43.0 0.0 copy-done.8
  43.1 17.3 %denoise.1 = (bf16[128,512]{1,0:T(8,128)(2,1)S(1)}, f32[128,512]{1,0:T(8,128)S(1)}, bf16[128,512]{1,0:T(8,128)(2,1)S(1)}) custom-call(s32[1]{0:T(128)} %bitcast.where_ref.group_ref, s32[1]{0:T(128)} %bitcast.1.frame_ref, f32[144,512]{1,0:T(8,128)S(1)} %get-tuple-element.24.x_ref, bf16[144,512]{1,0:T(8,128)(2,1)S(1)} %get-tuple-element.23.hidden_ref, ...), custom_call_target="tpu_custom_call" | custom-call | flops 14722007040 | bytes 1474560 | tf_op jit(solution)/shard_map/denoise/pallas_call | solution.py:552
  60.4 0.4 collective-permute-start.7
  60.8 1.9 %collective-permute-start.8 = (bf16[128,512]{1,0:T(8,128)(2,1)S(1)}, bf16[128,512]{1,0:T(8,128)(2,1)S(1)}, u32[]{:S(2)}, u32[]{:S(2)}) collective-permute-start(bf16[128,512]{1,0:T(8,128)(2,1)S(1)} %get-tuple-element.22), channel_id=1, source_target_pairs={{2,4},{6,8},{10,12},{14,16},{18,20},{22,24},{26,28},{4,2},{8,6},{1... | collective-permute-start | bytes 393224 | tf_op jit(solution)/shard_map/ppermute | solution.py:581
  62.7 0.0 collective-permute-done.7
  62.7 5.8 %collective-permute-done.8 = bf16[128,512]{1,0:T(8,128)(2,1)S(1)} collective-permute-done((bf16[128,512]{1,0:T(8,128)(2,1)S(1)}, bf16[128,512]{1,0:T(8,128)(2,1)S(1)}, u32[]{:S(2)}, u32[]{:S(2)}) %collective-permute-start.8) | collective-permute-done | bytes 131104 | tf_op jit(solution)/shard_map/ppermute | solution.py:581
  68.5 0.7 %add_bitcast_fusion = f32[1,128,512]{2,1,0:T(8,128)} fusion(bf16[128,512]{1,0:T(8,128)(2,1)S(1)} %collective-permute-done.8, f32[128,512]{1,0:T(8,128)S(1)} %get-tuple-element.20, bf16[128,512]{1,0:T(8,128)(2,1)S(1)} %collective-permute-done.7), kind=kLoop, calls=%fused_computation.1 | loop fusion | flops 262144 | bytes 786432 | tf_op jit(solution)/shard_map/broadcast_in_dim | solution.py:591
  (3 shorter events, 0.1 us)
Async XLA Ops:
  1.0 4.4 %collective-permute-start = (bf16[128,512]{1,0:T(8,128)(2,1)S(1)}, bf16[128,512]{1,0:T(8,128)(2,1)S(1)}, u32[]{:S(2)}, u32[]{:S(2)}) collective-permute-start(bf16[128,512]{1,0:T(8,128)(2,1)S(1)} %bitcast_convert_fusion), channel_id=1, source_target_pairs={{0,1},{1,0},{2,3},{3,2},{4,5},{5,4},{6,7},{7,6},{8,9},{9,8},{10,11... | collective-permute-start | bytes 393224 | tf_op jit(solution)/shard_map/ppermute | solution.py:223
  1.3 0.9 %copy-start = (f32[1,128,512]{2,1,0:T(8,128)S(1)}, f32[1,128,512]{2,1,0:T(8,128)}, u32[]{:S(2)}) copy-start(f32[1,128,512]{2,1,0:T(8,128)} %param.17) | copy-start | bytes 786436
  2.2 0.9 %copy-start.1 = (bf16[2,256,256]{2,1,0:T(8,128)(2,1)S(1)}, bf16[2,256,256]{2,1,0:T(8,128)(2,1)}, u32[]{:S(2)}) copy-start(bf16[2,256,256]{2,1,0:T(8,128)(2,1)} %constant.18.clone.cols_ref) | copy-start | bytes 786436
  3.2 0.8 %copy-start.2 = (s32[1,32,256]{2,1,0:T(8,128)S(1)}, s32[1,32,256]{2,1,0:T(8,128)}, u32[]{:S(2)}) copy-start(s32[1,32,256]{2,1,0:T(8,128)} %param.16) | copy-start | bytes 98308
  5.4 36.6 %copy-start.9 = (bf16[3,3,3,2,64]{4,3,2,1,0:T(2,128)(2,1)S(1)}, bf16[3,3,3,2,64]{4,3,2,1,0:T(2,128)(2,1)}, u32[]{:S(2)}) copy-start(bf16[3,3,3,2,64]{4,3,2,1,0:T(2,128)(2,1)} %param.22) | copy-start | bytes 20740
  5.4 36.6 %copy-start.10 = (bf16[3,3,3,64,2]{3,4,2,1,0:T(2,128)(2,1)S(1)}, bf16[3,3,3,64,2]{3,4,2,1,0:T(2,128)(2,1)}, u32[]{:S(2)}) copy-start(bf16[3,3,3,64,2]{3,4,2,1,0:T(2,128)(2,1)} %param.18) | copy-start | bytes 20740
  5.4 37.6 %copy-start.3 = (bf16[3,3,3,64,64]{4,3,2,1,0:T(8,128)(2,1)S(1)}, bf16[3,3,3,64,64]{4,3,2,1,0:T(8,128)(2,1)}, u32[]{:S(2)}) copy-start(bf16[3,3,3,64,64]{4,3,2,1,0:T(8,128)(2,1)} %param.20) | copy-start | bytes 663556
  5.4 37.6 %copy-start.4 = (f32[64]{0:T(128)S(1)}, f32[64]{0:T(128)}, u32[]{:S(2)}) copy-start(f32[64]{0:T(128)} %param.19) | copy-start | bytes 772
  5.4 37.6 %copy-start.5 = (f32[64]{0:T(128)S(1)}, f32[64]{0:T(128)}, u32[]{:S(2)}) copy-start(f32[64]{0:T(128)} %param.21) | copy-start | bytes 772
  5.4 37.6 %copy-start.6 = (bf16[12,64,192]{2,1,0:T(8,128)(2,1)S(1)}, bf16[12,64,192]{2,1,0:T(8,128)(2,1)}, u32[]{:S(2)}) copy-start(bf16[12,64,192]{2,1,0:T(8,128)(2,1)} %constant.20.clone.select_ref) | copy-start | bytes 884740
  5.5 37.6 %copy-start.7 = (bf16[256,256]{1,0:T(8,128)(2,1)S(1)}, bf16[256,256]{1,0:T(8,128)(2,1)}, u32[]{:S(2)}) copy-start(bf16[256,256]{1,0:T(8,128)(2,1)} %constant.21.clone.order_ref) | copy-start | bytes 393220
  5.5 37.6 %copy-start.8 = (bf16[432,54]{1,0:T(8,128)(2,1)S(1)}, bf16[432,54]{1,0:T(8,128)(2,1)}, u32[]{:S(2)}) copy-start(bf16[432,54]{1,0:T(8,128)(2,1)} %constant.22.clone.place_ref) | copy-start | bytes 139972
  25.8 4.1 %collective-permute-start.1 = (bf16[144,512]{1,0:T(8,128)(2,1)S(1)}, bf16[144,512]{1,0:T(8,128)(2,1)S(1)}, u32[]{:S(2)}, u32[]{:S(2)}) collective-permute-start(bf16[144,512]{1,0:T(8,128)(2,1)S(1)} %bitcast.17), channel_id=1, source_target_pairs={{0,1},{1,0},{2,3},{3,2},{4,5},{5,4},{6,7},{7,6},{8,9},{9,8},{10,11... | collective-permute-start | bytes 442376 | tf_op jit(solution)/shard_map/ppermute | solution.py:285
  29.9 6.6 %collective-permute-start.3 = (bf16[144,512]{1,0:T(8,128)(2,1)S(1)}, bf16[144,512]{1,0:T(8,128)(2,1)S(1)}, u32[]{:S(2)}, u32[]{:S(2)}) collective-permute-start(bf16[144,512]{1,0:T(8,128)(2,1)S(1)} %get-tuple-element.23.hidden_ref), channel_id=1, source_target_pairs={{0,4},{2,6},{8,12},{10,14},{16,20},{18,22},{24,28},{26,30},{4,0},{... | collective-permute-start | bytes 442376 | tf_op jit(solution)/shard_map/ppermute | solution.py:534
  31.1 8.2 %collective-permute-start.4 = (bf16[144,512]{1,0:T(8,128)(2,1)S(1)}, bf16[144,512]{1,0:T(8,128)(2,1)S(1)}, u32[]{:S(2)}, u32[]{:S(2)}) collective-permute-start(bf16[144,512]{1,0:T(8,128)(2,1)S(1)} %get-tuple-element.23.hidden_ref), channel_id=1, source_target_pairs={{4,8},{6,10},{12,16},{14,18},{20,24},{22,26},{8,4},{10,6},{16,12},... | collective-permute-start | bytes 442376 | tf_op jit(solution)/shard_map/ppermute | solution.py:535
  33.2 8.9 %collective-permute-start.2 = (bf16[144,512]{1,0:T(8,128)(2,1)S(1)}, bf16[144,512]{1,0:T(8,128)(2,1)S(1)}, u32[]{:S(2)}, u32[]{:S(2)}) collective-permute-start(bf16[144,512]{1,0:T(8,128)(2,1)S(1)} %get-tuple-element.23.hidden_ref), channel_id=1, source_target_pairs={{0,2},{4,6},{8,10},{12,14},{16,18},{20,22},{24,26},{28,30},{2,0},{... | collective-permute-start | bytes 442376 | tf_op jit(solution)/shard_map/ppermute | solution.py:533
  36.5 5.6 %collective-permute-start.5 = (bf16[144,512]{1,0:T(8,128)(2,1)S(1)}, bf16[144,512]{1,0:T(8,128)(2,1)S(1)}, u32[]{:S(2)}, u32[]{:S(2)}) collective-permute-start(bf16[144,512]{1,0:T(8,128)(2,1)S(1)} %collective-permute-done.3.first_pair_ref), channel_id=1, source_target_pairs={{0,2},{4,6},{8,10},{12,14},{16,18},{20,22},{24,26},{28,30},{2,0},{... | collective-permute-start | bytes 442376 | tf_op jit(solution)/shard_map/ppermute | solution.py:536
  39.3 3.7 %collective-permute-start.6 = (bf16[144,512]{1,0:T(8,128)(2,1)S(1)}, bf16[144,512]{1,0:T(8,128)(2,1)S(1)}, u32[]{:S(2)}, u32[]{:S(2)}) collective-permute-start(bf16[144,512]{1,0:T(8,128)(2,1)S(1)} %collective-permute-done.4.other_pair_ref), channel_id=1, source_target_pairs={{0,2},{4,6},{8,10},{12,14},{16,18},{20,22},{24,26},{28,30},{2,0},{... | collective-permute-start | bytes 442376 | tf_op jit(solution)/shard_map/ppermute | solution.py:537
  60.4 2.4 %collective-permute-start.7 = (bf16[128,512]{1,0:T(8,128)(2,1)S(1)}, bf16[128,512]{1,0:T(8,128)(2,1)S(1)}, u32[]{:S(2)}, u32[]{:S(2)}) collective-permute-start(bf16[128,512]{1,0:T(8,128)(2,1)S(1)} %get-tuple-element.21), channel_id=1, source_target_pairs={{0,2},{4,6},{8,10},{12,14},{16,18},{20,22},{24,26},{28,30},{2,0},{... | collective-permute-start | bytes 393224 | tf_op jit(solution)/shard_map/ppermute | solution.py:582
  60.8 7.7 %collective-permute-start.8 = (bf16[128,512]{1,0:T(8,128)(2,1)S(1)}, bf16[128,512]{1,0:T(8,128)(2,1)S(1)}, u32[]{:S(2)}, u32[]{:S(2)}) collective-permute-start(bf16[128,512]{1,0:T(8,128)(2,1)S(1)} %get-tuple-element.22), channel_id=1, source_target_pairs={{2,4},{6,8},{10,12},{14,16},{18,20},{22,24},{26,28},{4,2},{8,6},{1... | collective-permute-start | bytes 393224 | tf_op jit(solution)/shard_map/ppermute | solution.py:581

commit v6 on v5

--- a/solution.py
+++ b/solution.py
@@ -354,9 +354,9 @@
     bm_ref,
     wlast_ref,
     place_ref,
+    outer_ref,
+    base_ref,
     inner_ref,
-    base_ref,
-    outer_ref,
     plane_ref,
     slab_ref,
     wide_ref,
@@ -549,7 +549,7 @@
     vmem = pl.BlockSpec(memory_space=pltpu.VMEM)
     smem = pl.BlockSpec(memory_space=pltpu.SMEM)
     out = lambda dtype: jax.ShapeDtypeStruct((rows, double), dtype)
-    inner, base, outer = pl.pallas_call(
+    outer, base, inner = pl.pallas_call(
         functools.partial(denoise_kernel, groups, frames),
         in_specs=[smem] * 2 + [vmem] * 15,
         out_specs=[vmem] * 3,
@@ -578,9 +578,10 @@
         *weights,
     )
     across = swaps(frames, 1, 1)
-    outer = lax.ppermute(outer, "frame", across).astype(F32)
+    outer = lax.ppermute(outer, "frame", across)
     inner = lax.ppermute(inner, "frame", within).astype(F32)
-    return base + inner + outer
+    outer = outer.astype(F32)
+    return base + outer + inner
 
 
 def shards(kspace, sens, mask, image, w_first, b_first, w_mid, b_mid, w_last):

time: 69.5 us -> 69.1 us (level)
  no operation moved by 1% of the time
where the time goes in v6:
time: 69.1 us; the launch traced here: 68.8 us
  Pallas kernels  37.7 us (55%)
  starting transfers between devices  15.2 us (22%)
  waiting for transfers between devices  11.2 us (16%)
  local copies, waits for them, and re-layouts  2.76 us (4%)
  other arithmetic  1.75 us (3%)
    pallas_call x1, Pallas kernels, data_step(): pl.pallas_call(functools.partial(data_kernel, coils_at_once, 32), grid=(c...  20.3 us
    pallas_call x1, Pallas kernels, denoise(): pl.pallas_call(functools.partial(denoise_kernel, groups, frames), in_spec...  17.3 us
    ppermute x1, waiting for transfers between devices, denoise(): outer = lax.ppermute(outer, 'frame', across)  5.17 us
    ppermute x1, waiting for transfers between devices, data_step(): own = own + lax.ppermute(send[hop - 1], 'coil', shift(hop)).astype(F32)  3.79 us
    ppermute x1, starting transfers between devices, denoise(): partner = lax.ppermute(hidden, 'frame', within)  3.31 us
    ppermute x1, starting transfers between devices, denoise(): first_handed = lax.ppermute(first_pair, 'frame', within)  2.84 us
    unnamed x22, local copies, waits for them, and re-layouts  2.7 us
    ppermute x1, starting transfers between devices, denoise(): other_handed = lax.ppermute(other_pair, 'frame', within)  2.69 us
  transfers between devices with their start and end apart: 9, of which 4 were waited for; matrix products, arithmetic and copies ran while one was open for 0% of the time, Pallas kernels for 0%

profile of v6, /device:TPU:29, one launch (start us, length us, event | category | flops | bytes accessed | tf_op | source)
XLA Modules:
  0.0 68.8 jit_solution(2130913477747708831)
XLA Ops:
  0.0 1.0 %bitcast_convert_fusion = bf16[128,512]{1,0:T(8,128)(2,1)S(1)} fusion(f32[1,128,512]{2,1,0:T(8,128)} %param.17), kind=kLoop, calls=%fused_computation.2 | loop fusion | flops 65536 | bytes 393216 | tf_op jit(solution)/shard_map/convert_element_type | solution.py:222
  1.0 0.3 collective-permute-start
  1.3 0.0 copy-start
  1.3 0.9 %copy-done = f32[1,128,512]{2,1,0:T(8,128)S(1)} copy-done((f32[1,128,512]{2,1,0:T(8,128)S(1)}, f32[1,128,512]{2,1,0:T(8,128)}, u32[]{:S(2)}) %copy-start) | copy-done | bytes 262168
  2.2 0.0 copy-start.1
  2.2 0.9 %copy-done.1 = bf16[2,256,256]{2,1,0:T(8,128)(2,1)S(1)} copy-done((bf16[2,256,256]{2,1,0:T(8,128)(2,1)S(1)}, bf16[2,256,256]{2,1,0:T(8,128)(2,1)}, u32[]{:S(2)}) %copy-start.1) | copy-done | bytes 262168
  3.2 0.0 copy-start.2
  3.2 0.8 %copy-done.2 = s32[1,32,256]{2,1,0:T(8,128)S(1)} copy-done((s32[1,32,256]{2,1,0:T(8,128)S(1)}, s32[1,32,256]{2,1,0:T(8,128)}, u32[]{:S(2)}) %copy-start.2) | copy-done | bytes 32792
  3.9 0.2 prepare.1
  4.1 1.3 %collective-permute-done = bf16[128,512]{1,0:T(8,128)(2,1)S(1)} collective-permute-done((bf16[128,512]{1,0:T(8,128)(2,1)S(1)}, bf16[128,512]{1,0:T(8,128)(2,1)S(1)}, u32[]{:S(2)}, u32[]{:S(2)}) %collective-permute-start) | collective-permute-done | bytes 131104 | tf_op jit(solution)/shard_map/ppermute | solution.py:223
  5.4 0.0 copy-start.9
  5.4 0.0 copy-start.10
  5.4 0.0 copy-start.3
  5.4 0.0 copy-start.4
  5.4 0.0 copy-start.5
  5.4 0.0 copy-start.6
  5.5 0.0 copy-start.7
  5.5 0.0 copy-start.8
  5.5 20.3 %data_step.1 = (f32[144,512]{1,0:T(8,128)S(1)}, bf16[1,144,512]{2,1,0:T(8,128)(2,1)S(1)}) custom-call(s32[1]{0:T(128)} %bitcast.where_ref.group_ref, f32[128,512]{1,0:T(8,128)S(1)} %get-tuple-element.14.image_ref, bf16[1,128,512]{2,1,0:T(8,128)(2,1)S(1)} %bitcast.18, bf16[32,256,512]{2,1,0:T(8,128)(2,1)} %bitcast.22, bf16[32,256,512]{2,1,0:T(8,128)(2,1)} %sens_ref.1, ...), custom_call_target="tpu_custom_call" | custom-call | flops 17179869184 | bytes 16777216 | tf_op jit(solution)/shard_map/data_step/pallas_call | solution.py:242
  25.8 0.3 collective-permute-start.1
  26.0 3.8 %collective-permute-done.1 = bf16[144,512]{1,0:T(8,128)(2,1)S(1)} collective-permute-done((bf16[144,512]{1,0:T(8,128)(2,1)S(1)}, bf16[144,512]{1,0:T(8,128)(2,1)S(1)}, u32[]{:S(2)}, u32[]{:S(2)}) %collective-permute-start.1) | collective-permute-done | bytes 147488 | tf_op jit(solution)/shard_map/ppermute | solution.py:285
  29.9 1.3 %collective-permute-start.3 = (bf16[144,512]{1,0:T(8,128)(2,1)S(1)}, bf16[144,512]{1,0:T(8,128)(2,1)S(1)}, u32[]{:S(2)}, u32[]{:S(2)}) collective-permute-start(bf16[144,512]{1,0:T(8,128)(2,1)S(1)} %get-tuple-element.23.hidden_ref), channel_id=1, source_target_pairs={{0,4},{2,6},{8,12},{10,14},{16,20},{18,22},{24,28},{26,30},{4,0},{... | collective-permute-start | bytes 442376 | tf_op jit(solution)/shard_map/ppermute | solution.py:534
  31.1 2.0 %collective-permute-start.4 = (bf16[144,512]{1,0:T(8,128)(2,1)S(1)}, bf16[144,512]{1,0:T(8,128)(2,1)S(1)}, u32[]{:S(2)}, u32[]{:S(2)}) collective-permute-start(bf16[144,512]{1,0:T(8,128)(2,1)S(1)} %get-tuple-element.23.hidden_ref), channel_id=1, source_target_pairs={{4,8},{6,10},{12,16},{14,18},{20,24},{22,26},{8,4},{10,6},{16,12},... | collective-permute-start | bytes 442376 | tf_op jit(solution)/shard_map/ppermute | solution.py:535
  33.2 3.3 %collective-permute-start.2 = (bf16[144,512]{1,0:T(8,128)(2,1)S(1)}, bf16[144,512]{1,0:T(8,128)(2,1)S(1)}, u32[]{:S(2)}, u32[]{:S(2)}) collective-permute-start(bf16[144,512]{1,0:T(8,128)(2,1)S(1)} %get-tuple-element.23.hidden_ref), channel_id=1, source_target_pairs={{0,2},{4,6},{8,10},{12,14},{16,18},{20,22},{24,26},{28,30},{2,0},{... | collective-permute-start | bytes 442376 | tf_op jit(solution)/shard_map/ppermute | solution.py:533
  36.5 0.0 collective-permute-done.3.first_pair_ref
  36.5 2.8 %collective-permute-start.5 = (bf16[144,512]{1,0:T(8,128)(2,1)S(1)}, bf16[144,512]{1,0:T(8,128)(2,1)S(1)}, u32[]{:S(2)}, u32[]{:S(2)}) collective-permute-start(bf16[144,512]{1,0:T(8,128)(2,1)S(1)} %collective-permute-done.3.first_pair_ref), channel_id=1, source_target_pairs={{0,2},{4,6},{8,10},{12,14},{16,18},{20,22},{24,26},{28,30},{2,0},{... | collective-permute-start | bytes 442376 | tf_op jit(solution)/shard_map/ppermute | solution.py:536
  39.3 0.0 collective-permute-done.4.other_pair_ref
  39.3 2.7 %collective-permute-start.6 = (bf16[144,512]{1,0:T(8,128)(2,1)S(1)}, bf16[144,512]{1,0:T(8,128)(2,1)S(1)}, u32[]{:S(2)}, u32[]{:S(2)}) collective-permute-start(bf16[144,512]{1,0:T(8,128)(2,1)S(1)} %collective-permute-done.4.other_pair_ref), channel_id=1, source_target_pairs={{0,2},{4,6},{8,10},{12,14},{16,18},{20,22},{24,26},{28,30},{2,0},{... | collective-permute-start | bytes 442376 | tf_op jit(solution)/shard_map/ppermute | solution.py:537
  42.0 0.0 copy-done.9
  42.0 0.0 copy-done.10
  42.1 0.0 collective-permute-done.2.partner_ref
  42.1 0.0 collective-permute-done.5.first_handed_ref
  42.1 0.9 %collective-permute-done.6.other_handed_ref = bf16[144,512]{1,0:T(8,128)(2,1)S(1)} collective-permute-done((bf16[144,512]{1,0:T(8,128)(2,1)S(1)}, bf16[144,512]{1,0:T(8,128)(2,1)S(1)}, u32[]{:S(2)}, u32[]{:S(2)}) %collective-permute-start.6) | collective-permute-done | bytes 147488 | tf_op jit(solution)/shard_map/ppermute | solution.py:537
  43.0 0.0 copy-done.3
  43.0 0.0 copy-done.4
  43.0 0.0 copy-done.5
  43.0 0.0 copy-done.6
  43.0 0.0 copy-done.7
  43.0 0.0 copy-done.8
  43.1 17.3 %denoise.1 = (bf16[128,512]{1,0:T(8,128)(2,1)S(1)}, f32[128,512]{1,0:T(8,128)S(1)}, bf16[128,512]{1,0:T(8,128)(2,1)S(1)}) custom-call(s32[1]{0:T(128)} %bitcast.where_ref.group_ref, s32[1]{0:T(128)} %bitcast.1.frame_ref, f32[144,512]{1,0:T(8,128)S(1)} %get-tuple-element.24.x_ref, bf16[144,512]{1,0:T(8,128)(2,1)S(1)} %get-tuple-element.23.hidden_ref, ...), custom_call_target="tpu_custom_call" | custom-call | flops 14722007040 | bytes 1474560 | tf_op jit(solution)/shard_map/denoise/pallas_call | solution.py:552
  60.4 1.9 %collective-permute-start.7 = (bf16[128,512]{1,0:T(8,128)(2,1)S(1)}, bf16[128,512]{1,0:T(8,128)(2,1)S(1)}, u32[]{:S(2)}, u32[]{:S(2)}) collective-permute-start(bf16[128,512]{1,0:T(8,128)(2,1)S(1)} %get-tuple-element.21), channel_id=1, source_target_pairs={{2,4},{6,8},{10,12},{14,16},{18,20},{22,24},{26,28},{4,2},{8,6},{1... | collective-permute-start | bytes 393224 | tf_op jit(solution)/shard_map/ppermute | solution.py:581
  62.3 0.6 collective-permute-start.8
  62.9 5.2 %collective-permute-done.7 = bf16[128,512]{1,0:T(8,128)(2,1)S(1)} collective-permute-done((bf16[128,512]{1,0:T(8,128)(2,1)S(1)}, bf16[128,512]{1,0:T(8,128)(2,1)S(1)}, u32[]{:S(2)}, u32[]{:S(2)}) %collective-permute-start.7) | collective-permute-done | bytes 131104 | tf_op jit(solution)/shard_map/ppermute | solution.py:581
  68.1 0.0 collective-permute-done.8
  68.1 0.7 %add_bitcast_fusion = f32[1,128,512]{2,1,0:T(8,128)} fusion(bf16[128,512]{1,0:T(8,128)(2,1)S(1)} %collective-permute-done.8, f32[128,512]{1,0:T(8,128)S(1)} %get-tuple-element.20, bf16[128,512]{1,0:T(8,128)(2,1)S(1)} %collective-permute-done.7), kind=kLoop, calls=%fused_computation.1 | loop fusion | flops 262144 | bytes 786432 | tf_op jit(solution)/shard_map/broadcast_in_dim | solution.py:592
  (3 shorter events, 0.1 us)
Async XLA Ops:
  1.0 4.4 %collective-permute-start = (bf16[128,512]{1,0:T(8,128)(2,1)S(1)}, bf16[128,512]{1,0:T(8,128)(2,1)S(1)}, u32[]{:S(2)}, u32[]{:S(2)}) collective-permute-start(bf16[128,512]{1,0:T(8,128)(2,1)S(1)} %bitcast_convert_fusion), channel_id=1, source_target_pairs={{0,1},{1,0},{2,3},{3,2},{4,5},{5,4},{6,7},{7,6},{8,9},{9,8},{10,11... | collective-permute-start | bytes 393224 | tf_op jit(solution)/shard_map/ppermute | solution.py:223
  1.3 0.9 %copy-start = (f32[1,128,512]{2,1,0:T(8,128)S(1)}, f32[1,128,512]{2,1,0:T(8,128)}, u32[]{:S(2)}) copy-start(f32[1,128,512]{2,1,0:T(8,128)} %param.17) | copy-start | bytes 786436
  2.2 0.9 %copy-start.1 = (bf16[2,256,256]{2,1,0:T(8,128)(2,1)S(1)}, bf16[2,256,256]{2,1,0:T(8,128)(2,1)}, u32[]{:S(2)}) copy-start(bf16[2,256,256]{2,1,0:T(8,128)(2,1)} %constant.18.clone.cols_ref) | copy-start | bytes 786436
  3.2 0.8 %copy-start.2 = (s32[1,32,256]{2,1,0:T(8,128)S(1)}, s32[1,32,256]{2,1,0:T(8,128)}, u32[]{:S(2)}) copy-start(s32[1,32,256]{2,1,0:T(8,128)} %param.16) | copy-start | bytes 98308
  5.4 36.6 %copy-start.9 = (bf16[3,3,3,2,64]{4,3,2,1,0:T(2,128)(2,1)S(1)}, bf16[3,3,3,2,64]{4,3,2,1,0:T(2,128)(2,1)}, u32[]{:S(2)}) copy-start(bf16[3,3,3,2,64]{4,3,2,1,0:T(2,128)(2,1)} %param.22) | copy-start | bytes 20740
  5.4 36.6 %copy-start.10 = (bf16[3,3,3,64,2]{3,4,2,1,0:T(2,128)(2,1)S(1)}, bf16[3,3,3,64,2]{3,4,2,1,0:T(2,128)(2,1)}, u32[]{:S(2)}) copy-start(bf16[3,3,3,64,2]{3,4,2,1,0:T(2,128)(2,1)} %param.18) | copy-start | bytes 20740
  5.4 37.6 %copy-start.3 = (bf16[3,3,3,64,64]{4,3,2,1,0:T(8,128)(2,1)S(1)}, bf16[3,3,3,64,64]{4,3,2,1,0:T(8,128)(2,1)}, u32[]{:S(2)}) copy-start(bf16[3,3,3,64,64]{4,3,2,1,0:T(8,128)(2,1)} %param.20) | copy-start | bytes 663556
  5.4 37.6 %copy-start.4 = (f32[64]{0:T(128)S(1)}, f32[64]{0:T(128)}, u32[]{:S(2)}) copy-start(f32[64]{0:T(128)} %param.19) | copy-start | bytes 772
  5.4 37.6 %copy-start.5 = (f32[64]{0:T(128)S(1)}, f32[64]{0:T(128)}, u32[]{:S(2)}) copy-start(f32[64]{0:T(128)} %param.21) | copy-start | bytes 772
  5.4 37.6 %copy-start.6 = (bf16[12,64,192]{2,1,0:T(8,128)(2,1)S(1)}, bf16[12,64,192]{2,1,0:T(8,128)(2,1)}, u32[]{:S(2)}) copy-start(bf16[12,64,192]{2,1,0:T(8,128)(2,1)} %constant.20.clone.select_ref) | copy-start | bytes 884740
  5.5 37.6 %copy-start.7 = (bf16[256,256]{1,0:T(8,128)(2,1)S(1)}, bf16[256,256]{1,0:T(8,128)(2,1)}, u32[]{:S(2)}) copy-start(bf16[256,256]{1,0:T(8,128)(2,1)} %constant.21.clone.order_ref) | copy-start | bytes 393220
  5.5 37.6 %copy-start.8 = (bf16[432,54]{1,0:T(8,128)(2,1)S(1)}, bf16[432,54]{1,0:T(8,128)(2,1)}, u32[]{:S(2)}) copy-start(bf16[432,54]{1,0:T(8,128)(2,1)} %constant.22.clone.place_ref) | copy-start | bytes 139972
  25.8 4.1 %collective-permute-start.1 = (bf16[144,512]{1,0:T(8,128)(2,1)S(1)}, bf16[144,512]{1,0:T(8,128)(2,1)S(1)}, u32[]{:S(2)}, u32[]{:S(2)}) collective-permute-start(bf16[144,512]{1,0:T(8,128)(2,1)S(1)} %bitcast.17), channel_id=1, source_target_pairs={{0,1},{1,0},{2,3},{3,2},{4,5},{5,4},{6,7},{7,6},{8,9},{9,8},{10,11... | collective-permute-start | bytes 442376 | tf_op jit(solution)/shard_map/ppermute | solution.py:285
  29.9 6.6 %collective-permute-start.3 = (bf16[144,512]{1,0:T(8,128)(2,1)S(1)}, bf16[144,512]{1,0:T(8,128)(2,1)S(1)}, u32[]{:S(2)}, u32[]{:S(2)}) collective-permute-start(bf16[144,512]{1,0:T(8,128)(2,1)S(1)} %get-tuple-element.23.hidden_ref), channel_id=1, source_target_pairs={{0,4},{2,6},{8,12},{10,14},{16,20},{18,22},{24,28},{26,30},{4,0},{... | collective-permute-start | bytes 442376 | tf_op jit(solution)/shard_map/ppermute | solution.py:534
  31.1 8.2 %collective-permute-start.4 = (bf16[144,512]{1,0:T(8,128)(2,1)S(1)}, bf16[144,512]{1,0:T(8,128)(2,1)S(1)}, u32[]{:S(2)}, u32[]{:S(2)}) collective-permute-start(bf16[144,512]{1,0:T(8,128)(2,1)S(1)} %get-tuple-element.23.hidden_ref), channel_id=1, source_target_pairs={{4,8},{6,10},{12,16},{14,18},{20,24},{22,26},{8,4},{10,6},{16,12},... | collective-permute-start | bytes 442376 | tf_op jit(solution)/shard_map/ppermute | solution.py:535
  33.2 8.9 %collective-permute-start.2 = (bf16[144,512]{1,0:T(8,128)(2,1)S(1)}, bf16[144,512]{1,0:T(8,128)(2,1)S(1)}, u32[]{:S(2)}, u32[]{:S(2)}) collective-permute-start(bf16[144,512]{1,0:T(8,128)(2,1)S(1)} %get-tuple-element.23.hidden_ref), channel_id=1, source_target_pairs={{0,2},{4,6},{8,10},{12,14},{16,18},{20,22},{24,26},{28,30},{2,0},{... | collective-permute-start | bytes 442376 | tf_op jit(solution)/shard_map/ppermute | solution.py:533
  36.5 5.6 %collective-permute-start.5 = (bf16[144,512]{1,0:T(8,128)(2,1)S(1)}, bf16[144,512]{1,0:T(8,128)(2,1)S(1)}, u32[]{:S(2)}, u32[]{:S(2)}) collective-permute-start(bf16[144,512]{1,0:T(8,128)(2,1)S(1)} %collective-permute-done.3.first_pair_ref), channel_id=1, source_target_pairs={{0,2},{4,6},{8,10},{12,14},{16,18},{20,22},{24,26},{28,30},{2,0},{... | collective-permute-start | bytes 442376 | tf_op jit(solution)/shard_map/ppermute | solution.py:536
  39.3 3.7 %collective-permute-start.6 = (bf16[144,512]{1,0:T(8,128)(2,1)S(1)}, bf16[144,512]{1,0:T(8,128)(2,1)S(1)}, u32[]{:S(2)}, u32[]{:S(2)}) collective-permute-start(bf16[144,512]{1,0:T(8,128)(2,1)S(1)} %collective-permute-done.4.other_pair_ref), channel_id=1, source_target_pairs={{0,2},{4,6},{8,10},{12,14},{16,18},{20,22},{24,26},{28,30},{2,0},{... | collective-permute-start | bytes 442376 | tf_op jit(solution)/shard_map/ppermute | solution.py:537
  60.4 7.7 %collective-permute-start.7 = (bf16[128,512]{1,0:T(8,128)(2,1)S(1)}, bf16[128,512]{1,0:T(8,128)(2,1)S(1)}, u32[]{:S(2)}, u32[]{:S(2)}) collective-permute-start(bf16[128,512]{1,0:T(8,128)(2,1)S(1)} %get-tuple-element.21), channel_id=1, source_target_pairs={{2,4},{6,8},{10,12},{14,16},{18,20},{22,24},{26,28},{4,2},{8,6},{1... | collective-permute-start | bytes 393224 | tf_op jit(solution)/shard_map/ppermute | solution.py:581
  62.3 5.8 %collective-permute-start.8 = (bf16[128,512]{1,0:T(8,128)(2,1)S(1)}, bf16[128,512]{1,0:T(8,128)(2,1)S(1)}, u32[]{:S(2)}, u32[]{:S(2)}) collective-permute-start(bf16[128,512]{1,0:T(8,128)(2,1)S(1)} %get-tuple-element.22), channel_id=1, source_target_pairs={{0,2},{4,6},{8,10},{12,14},{16,18},{20,22},{24,26},{28,30},{2,0},{... | collective-permute-start | bytes 393224 | tf_op jit(solution)/shard_map/ppermute | solution.py:582
